TPU v7x, 32 devices: a whole 2x2x4 slice. The times are simulated.
32 devices in a mesh: segment: 4 (over z), dp: 8 (over y, x, core).
Axes of the slice: x: 2, y: 2, z: 4, core: 2. Of those that a mesh axis runs over, the one named last changes fastest.
Arguments:
- acts: bfloat16 [4, 1024, 8192], P('segment', 'dp'), may hold values from -6 to 6
- weights: bfloat16 [4, 2, 64, 128, 128], P('segment'), may hold values from -0.5 to 0.5
- gains: float32 [4, 8192], P('segment'), may hold values from 0.5 to 1.5
- cotangent: bfloat16 [1024, 8192], P('dp'), may hold values from -6 to 6
- block_order: int32 [64], replicated, may hold values from 0 to 63, each once
- owner_table: int32 [128], replicated, may hold values from 0 to 127, each once
Outputs:
- input_grads: bfloat16 [4, 1024, 8192], P('segment', 'dp')
- block_grads: float32 [4, 128, 128, 128], P('segment', 'dp')
- gain_grads: float32 [4, 8192], P('segment', 'dp')
Inputs may be any that keep to these rules, and one draw needn't show every extreme that they name: `block_order`: a permutation. `owner_table`: a permutation.
All inputs are finite; a program needn't handle non-finite values.
Results may differ from a plain program's by a relative error of at most 0.012.
Values may be sent and summed in bfloat16 or wider, within the bound.
No kernel may reach another device: no remote copies, remote signals or barrier semaphores. Data moves between devices by JAX's collectives and lax.ppermute only.
A program may use at most 128 MiB of HBM per device.

v0:
```python
import functools
import math

import jax
import jax.numpy as jnp
from jax import lax
from jax.experimental import pallas as pl
from jax.experimental.pallas import tpu as pltpu
from jax.sharding import PartitionSpec as P

F = 64
B = 128
EPS = 1e-05
CHUNKS = 8
LAG = 2
ANY = pl.BlockSpec(memory_space=pl.ANY)
VMEM = pl.BlockSpec(memory_space=pltpu.VMEM)
SMEM = pl.BlockSpec(memory_space=pltpu.SMEM)
NT = (((1,), (1,)), ((), ()))


def dot(a, b):
    return jnp.dot(a, b, preferred_element_type=jnp.float32)


def dot_nt(a, b):
    return lax.dot_general(a, b, NT, preferred_element_type=jnp.float32)


def col(j):
    if isinstance(j, int):
        return pl.ds(j * B, B)
    return pl.ds(pl.multiple_of(j * B, B), B)


def exchange(parts, lane_bit):
    lane = lax.broadcasted_iota(jnp.int32, parts[0].shape, 1)
    parts = list(parts)
    for i in range(3):
        shift = 1 << (lane_bit + i)
        upper = (lane & shift) != 0
        for low in range(8):
            if low & (1 << i):
                continue
            high = low | (1 << i)
            a, b = parts[low], parts[high]
            parts[low] = jnp.where(upper, pltpu.roll(b, shift, 1), a)
            parts[high] = jnp.where(upper, b, pltpu.roll(a, B - shift, 1))
    return parts


def gelu_pair(v):
    cdf = 0.5 * (1.0 + lax.erf(v * 0.7071067811865476))
    density = jnp.exp(-0.5 * v * v) * 0.3989422804014327
    return v * cdf, cdf + v * density


def inverse_rms(x_ref, rows):
    def add(j, total):
        v = x_ref[rows, col(j)].astype(jnp.float32)
        return total + v * v

    size = x_ref.shape[0] if rows == slice(None) else rows.size
    total = lax.fori_loop(0, F, add, jnp.zeros((size, B), jnp.float32), unroll=8)
    mean = jnp.sum(total, axis=1, keepdims=True) * (1.0 / (F * B))
    return lax.rsqrt(mean + EPS)


def prologue_kernel(order_ref, x_ref, gain_ref, w0_ref, eye_ref, take_ref, slope_ref, left_ref, inv_ref, half_ref, mix_ref):
    step = pl.program_id(0)
    n = x_ref.shape[0]
    sub = 32

    @pl.when(step == 0)
    def _():
        inv_ref[...] = jnp.broadcast_to(inverse_rms(x_ref, slice(None)), (n, B))

    eye = eye_ref[...]
    base = step * 8
    for i in range(8):
        at = col(base + i)
        h = (x_ref[:, at].astype(jnp.float32) * inv_ref[...] * gain_ref[:, at]).astype(jnp.bfloat16)
        left_ref[base + i] = dot_nt(eye, h).astype(jnp.bfloat16)
        z, slope = gelu_pair(dot(h, w0_ref[i]))
        slope_ref[:, col(i)] = slope.astype(slope_ref.dtype)
        half_ref[base + i] = z
    for t in range(0, n, sub):
        rows = pl.ds(t, sub)
        parts = exchange([half_ref[base + i, rows, :] for i in range(8)], 1)
        for i in range(8):
            half_ref[base + i, rows, :] = parts[i]

    @pl.when(step == pl.num_programs(0) - 1)
    def _():
        for low in range(8):
            for t in range(0, n, sub):
                rows = pl.ds(t, sub)
                parts = exchange([half_ref[8 * g + low, rows, :] for g in range(8)], 4)
                for g in range(8):
                    mix_ref[8 * g + low, rows, :] = parts[g].astype(jnp.bfloat16)
        take = take_ref[...]

        @pl.loop(0, F)
        def _(j):
            left_ref[F + j] = dot_nt(take, mix_ref[order_ref[j]]).astype(jnp.bfloat16)


def prologue(order, x, gain, w0, eye, take):
    n = x.shape[0]
    whole = lambda *shape: pl.BlockSpec(shape, lambda s: (0,) * len(shape))
    return pl.pallas_call(
        prologue_kernel,
        grid=(F // 8,),
        out_shape=(
            jax.ShapeDtypeStruct((n, F * B), jnp.bfloat16),
            jax.ShapeDtypeStruct((2 * F, B, n), jnp.bfloat16),
        ),
        in_specs=[
            SMEM,
            whole(n, F * B),
            whole(1, F * B),
            pl.BlockSpec((8, B, B), lambda s: (s, 0, 0)),
            whole(B, B),
            whole(B, B),
        ],
        out_specs=(pl.BlockSpec((n, 8 * B), lambda s: (0, s)), whole(2 * F, B, n)),
        scratch_shapes=[
            pltpu.VMEM((n, B), jnp.float32),
            pltpu.VMEM((F, n, B), jnp.float32),
            pltpu.VMEM((F, n, B), jnp.bfloat16),
        ],
        compiler_params=pltpu.CompilerParams(vmem_limit_bytes=40 << 20),
        name="prologue",
    )(order, x, gain, w0, eye, take)


def stage_kernel(step, segments, first, *refs):
    (order_ref, cot_ref, inc_ref, x_ref, slope_ref, gain_ref, w1_ref, w0_ref) = refs[:8]
    refs = refs[8:] if first else refs[11:]
    (send_ref, right_ref, out_ref, part_ref) = refs[:4]
    (g_buf, x_buf, s_buf, w1_buf, w0_buf, low_buf, mid_buf, cg_buf, gp_buf, o_buf, p_buf, sem, sem1, sem0) = refs[4:]
    rows = g_buf.shape[0]
    position = lax.axis_index("segment")
    chunk = step - LAG * (segments - 1 - position)
    top = position == segments - 1
    valid = jnp.logical_and(chunk >= 0, chunk < CHUNKS)

    @pl.when(valid)
    def _():
        at_rows = pl.ds(pl.multiple_of(chunk * rows, rows), rows)

        @pl.when(top)
        def _():
            pltpu.make_async_copy(cot_ref.at[at_rows, :], g_buf, sem.at[0]).start()

        @pl.when(jnp.logical_not(top))
        def _():
            pltpu.make_async_copy(inc_ref, g_buf, sem.at[0]).start()

        w1_copies = [pltpu.make_async_copy(w1_ref.at[pl.ds(8 * k, 8)], w1_buf.at[pl.ds(8 * k, 8)], sem1.at[k]) for k in range(8)]
        w0_copies = [pltpu.make_async_copy(w0_ref.at[pl.ds(8 * k, 8)], w0_buf.at[pl.ds(8 * k, 8)], sem0.at[k]) for k in range(8)]
        x_copy = pltpu.make_async_copy(x_ref.at[at_rows, :], x_buf, sem.at[1])
        s_copy = pltpu.make_async_copy(slope_ref.at[at_rows, :], s_buf, sem.at[2])
        for k in range(8):
            w1_copies[k].start()
        x_copy.start()
        s_copy.start()
        for k in range(8):
            w0_copies[k].start()
        pltpu.make_async_copy(inc_ref, g_buf, sem.at[0]).wait()
        g_copy = pltpu.make_async_copy(g_buf, right_ref.at[at_rows, pl.ds(F * B, F * B)], sem.at[3])
        g_copy.start()

        @pl.loop(0, 8)
        def _(k):
            pltpu.make_async_copy(w1_ref.at[pl.ds(0, 8)], w1_buf.at[pl.ds(0, 8)], sem1.at[k]).wait()
            for i in range(8):
                j = 8 * k + i
                low_buf[order_ref[j]] = dot_nt(g_buf[:, col(j)], w1_buf[j])

        x_copy.wait()
        inv = inverse_rms(x_buf, slice(None))

        @pl.loop(0, 8)
        def _(k):
            parts = exchange([low_buf[8 * k + i] for i in range(8)], 1)
            for i in range(8):
                mid_buf[8 * i + k] = parts[i]

        s_copy.wait()
        for k in range(8):
            w0_copies[k].wait()

        def second(low, inner):
            parts = exchange([mid_buf[8 * low + g] for g in range(8)], 4)
            for g in range(8):
                j = 8 * g + low
                at = col(j)
                gp = (parts[g] * s_buf[:, at].astype(jnp.float32)).astype(jnp.bfloat16)
                gp_buf[:, at] = gp
                gh = dot_nt(gp, w0_buf[j])
                xh = x_buf[:, at].astype(jnp.float32) * inv
                term = gh * xh
                part = term[:8]
                for t in range(8, rows, 8):
                    part = part + term[t : t + 8]
                p_buf[:, at] = part
                gain = gain_ref[:, at]
                cg_buf[:, at] = gh * gain
                inner = inner + term * gain
            return inner

        inner = lax.fori_loop(0, 8, second, jnp.zeros((rows, B), jnp.float32))
        gp_copy = pltpu.make_async_copy(gp_buf, right_ref.at[at_rows, pl.ds(0, F * B)], sem.at[4])
        gp_copy.start()
        p_copy = pltpu.make_async_copy(p_buf, part_ref.at[chunk], sem.at[5])
        p_copy.start()
        inner = jnp.sum(inner, axis=1, keepdims=True) * (1.0 / (F * B))

        @pl.loop(0, F, unroll=8)
        def _(j):
            at = col(j)
            xh = x_buf[:, at].astype(jnp.float32) * inv
            o_buf[:, at] = (g_buf[:, at].astype(jnp.float32) + inv * (cg_buf[:, at] - xh * inner)).astype(jnp.bfloat16)

        o_copy = pltpu.make_async_copy(o_buf, send_ref, sem.at[6])
        o_copy.start()
        i_copy = pltpu.make_async_copy(o_buf, out_ref.at[at_rows, :], sem.at[7])
        i_copy.start()
        for copy in (g_copy, gp_copy, p_copy, o_copy, i_copy):
            copy.wait()


def stage(step, segments, order, cot, inc, x, slope, gain, w1, w0, carried):
    n = x.shape[0]
    rows = n // CHUNKS
    wide = F * B
    bf, f32 = jnp.bfloat16, jnp.float32
    first = carried is None
    args = [order, cot, inc, x, slope, gain, w1, w0] + ([] if first else list(carried))
    return pl.pallas_call(
        functools.partial(stage_kernel, step, segments, first),
        out_shape=(
            jax.ShapeDtypeStruct((rows, wide), bf),
            jax.ShapeDtypeStruct((n, 2 * wide), bf),
            jax.ShapeDtypeStruct((n, wide), bf),
            jax.ShapeDtypeStruct((CHUNKS, 8, wide), f32),
        ),
        in_specs=[SMEM] + [ANY] * 4 + [VMEM] + [ANY] * (2 if first else 5),
        out_specs=(ANY,) * 4,
        scratch_shapes=[
            pltpu.VMEM((rows, wide), bf),
            pltpu.VMEM((rows, wide), bf),
            pltpu.VMEM((rows, wide), bf),
            pltpu.VMEM((F, B, B), bf),
            pltpu.VMEM((F, B, B), bf),
            pltpu.VMEM((F, rows, B), f32),
            pltpu.VMEM((F, rows, B), f32),
            pltpu.VMEM((rows, wide), f32),
            pltpu.VMEM((rows, wide), bf),
            pltpu.VMEM((rows, wide), bf),
            pltpu.VMEM((8, wide), f32),
            pltpu.SemaphoreType.DMA((8,)),
            pltpu.SemaphoreType.DMA((8,)),
            pltpu.SemaphoreType.DMA((8,)),
        ],
        input_output_aliases={} if first else {8: 1, 9: 2, 10: 3},
        compiler_params=pltpu.CompilerParams(vmem_limit_bytes=24 << 20),
        cost_estimate=pl.CostEstimate(flops=4 * rows * wide * B, bytes_accessed=6 << 20, transcendentals=0),
        name="stage",
    )(*args)


def grads_kernel(scale, blocks, table_ref, perm_ref, left_ref, right_ref, part_ref, send_ref, keep_ref, s_buf, k_buf, sem):
    me = lax.axis_index("dp")
    half = F
    chunk_rows = 8 * B

    def rows_of(k, size=chunk_rows):
        return pl.ds(pl.multiple_of(k * chunk_rows, chunk_rows), size)

    for j in range(F):
        total = jnp.sum(jnp.sum(part_ref[:, :, j * B : (j + 1) * B], axis=0), axis=0, keepdims=True) * scale
        k_buf[half * B + j : half * B + j + 1, :] = total
    s_buf[half * B :, :] = k_buf[half * B :, :].astype(jnp.bfloat16)

    @pl.loop(0, 8)
    def _(k):
        for i in range(8):
            p = 8 * k + i
            which = table_ref[perm_ref[p] ^ (me * blocks)]
            value = dot(left_ref[which], right_ref[:, col(which)]) * scale
            s_buf[pl.ds(pl.multiple_of(p * B, B), B), :] = value.astype(jnp.bfloat16)
        pltpu.make_async_copy(s_buf.at[rows_of(k)], send_ref.at[rows_of(k)], sem.at[0]).start()

    @pl.loop(0, 8)
    def _(k):
        for i in range(8):
            p = 8 * k + i
            which = table_ref[perm_ref[half + p] ^ (me * blocks)]
            k_buf[pl.ds(pl.multiple_of(p * B, B), B), :] = dot(left_ref[which], right_ref[:, col(which)]) * scale
        pltpu.make_async_copy(k_buf.at[rows_of(k)], keep_ref.at[rows_of(k)], sem.at[1]).start()

    tail = pl.ds(half * B, F)
    pltpu.make_async_copy(s_buf.at[tail], send_ref.at[tail], sem.at[0]).start()
    pltpu.make_async_copy(k_buf.at[tail], keep_ref.at[tail], sem.at[1]).start()
    pltpu.make_async_copy(s_buf, send_ref, sem.at[0]).wait()
    pltpu.make_async_copy(k_buf, keep_ref, sem.at[1]).wait()


def grads(scale, blocks, table, perm, left, right, part):
    rows = F * B + F
    return pl.pallas_call(
        functools.partial(grads_kernel, scale, blocks),
        out_shape=(jax.ShapeDtypeStruct((rows, B), jnp.bfloat16), jax.ShapeDtypeStruct((rows, B), jnp.float32)),
        in_specs=[SMEM, SMEM, VMEM, VMEM, VMEM],
        out_specs=(ANY, ANY),
        scratch_shapes=[
            pltpu.VMEM((rows, B), jnp.bfloat16),
            pltpu.VMEM((rows, B), jnp.float32),
            pltpu.SemaphoreType.DMA((2,)),
        ],
        compiler_params=pltpu.CompilerParams(vmem_limit_bytes=40 << 20),
        name="grads",
    )(table, perm, left, right, part)


def order_of(bits, low_first):
    def place(q):
        digits = [(q >> k) & 1 for k in range(bits)]
        if not low_first:
            digits = digits[::-1]
        return [1 - d for d in digits]

    return sorted(range(1 << bits), key=place)


def swap(array, axis, bit):
    size = lax.axis_size(axis)
    return lax.ppermute(array, axis, [(i, i ^ (1 << bit)) for i in range(size)])


def reduce_owners(send, keep, dp, blocks):
    bits = dp.bit_length() - 2
    got = swap(send, "dp", 0)
    total = keep + got.astype(jnp.float32)
    first = max(blocks // 2, 1)
    cut = (dp // 2) * first * B
    sides = [(total[:cut], list(range(1, bits + 1))), (total[cut : F * B], list(range(bits, 0, -1)))]
    gain = total[F * B :]
    ends = []
    for index in range(bits):
        sent = []
        for side, bits_of in sides:
            half = side.shape[0] // 2
            if side.shape[0]:
                sent.append(swap(side[:half].astype(jnp.bfloat16), "dp", bits_of[index]))
            else:
                sent.append(None)
        got_gain = swap(gain, "dp", index + 1)
        gain = gain + got_gain
        sides = [
            (side[side.shape[0] // 2 :] + (0 if other is None else other.astype(jnp.float32)), bits_of)
            for (side, bits_of), other in zip(sides, sent)
        ]
    return jnp.concatenate([side for side, _ in sides], axis=0), gain


def local(acts, weights, gains, cotangent, block_order, owner_table):
    x = acts[0]
    n = x.shape[0]
    segments = lax.axis_size("segment")
    dp = lax.axis_size("dp")
    blocks = 2 * F // dp
    scale = 1.0 / math.sqrt(n * dp)
    w0 = weights[0, 0]
    w1 = weights[0, 1].reshape(F, 2, B // 2, B).swapaxes(1, 2).reshape(F, B, B)
    row = lax.broadcasted_iota(jnp.int32, (B, B), 0)
    column = lax.broadcasted_iota(jnp.int32, (B, B), 1)
    eye = (row == column).astype(jnp.bfloat16)
    take = (2 * (row % (B // 2)) + row // (B // 2) == column).astype(jnp.bfloat16)
    slope, left = prologue(block_order, x, gains, w0, eye, take)

    rows = n // CHUNKS
    steps = CHUNKS + LAG * (segments - 1)
    pairs = [(i, i - 1) for i in range(1, segments)]
    sent, carried = [], None
    for step in range(steps):
        inc = sent[step - LAG] if step >= LAG else cotangent[:rows]
        out = stage(step, segments, block_order, cotangent, inc, x, slope, gains, w1, w0, carried)
        carried = out[1:]
        if step < steps - LAG:
            sent.append(lax.ppermute(out[0], "segment", pairs))
    right, input_gradient, part = carried

    bits = dp.bit_length() - 2
    first = max(blocks // 2, 1)
    places = [(2 * q) * blocks + i for q in order_of(bits, True) for i in range(first)]
    places += [(2 * q) * blocks + i for q in order_of(bits, False) for i in range(first, blocks)]
    perm = jnp.array([p + blocks for p in places] + places, jnp.int32)
    send, keep = grads(scale, blocks, owner_table, perm, left, right, part)
    owned, gain = reduce_owners(send, keep, dp, blocks)
    width = F * B // dp
    own_gain = lax.dynamic_slice(gain.reshape(F * B), (lax.axis_index("dp") * width,), (width,))
    return input_gradient[None], owned.reshape(1, blocks, B, B), own_gain[None]


def solution(mesh):
    return jax.shard_map(
        local,
        mesh=mesh,
        in_specs=(
            P("segment", "dp", None),
            P("segment", None, None, None, None),
            P("segment", None),
            P("dp", None),
            P(),
            P(),
        ),
        out_specs=(P("segment", "dp", None), P("segment", "dp", None, None), P("segment", "dp")),
        check_vma=False,
    )
```

profile of v0, /device:TPU:0, one launch (start us, length us, event | category | flops | bytes accessed | tf_op | source)
XLA Modules:
  0.0 221.7 jit_solution(8607578388640006487)
XLA Ops:
  0.7 2.7 %fusion.3 = (bf16[1,1,64,128,128]{4,3,2,1,0:T(8,128)(2,1)S(1)}, bf16[64,128,128]{2,1,0:T(8,128)(2,1)S(1)}) fusion(bf16[1,2,64,128,128]{4,3,2,1,0:T(8,128)(2,1)} %param.8), kind=kLoop, calls=%fused_computation.23 | loop fusion | bytes 8388608 | tf_op jit(solution)/shard_map/slice | solution.py:377
  3.5 2.2 copy.49
  5.9 22.6 %prologue.1 = (bf16[128,8192]{1,0:T(8,128)(2,1)S(1)}, bf16[128,128,128]{2,1,0:T(8,128)(2,1)S(1)}) custom-call(s32[64]{0:T(128)S(1)} %copy-done.7, bf16[128,8192]{1,0:T(8,128)(2,1)S(1)} %bitcast.12, f32[1,8192]{1,0:T(1,128)S(1)} %copy-done.4, bf16[64,128,128]{2,1,0:T(8,128)(2,1)S(1)} %get-tuple-element.124.w0_ref.refs_7_, ...), custom_call_target="tpu_custom_call" | custom-call | tf_op jit(solution)/shard_map/prologue/pallas_call | solution.py:111
  33.9 8.7 %collective-permute-done.1.refs_2_ = bf16[16,8192]{1,0:T(8,128)(2,1)S(1)} collective-permute-done((bf16[16,8192]{1,0:T(8,128)(2,1)S(1)}, bf16[16,8192]{1,0:T(8,128)(2,1)S(1)}, u32[]{:S(2)}, u32[]{:S(2)}) %collective-permute-start.1) | collective-permute-done | bytes 262176 | tf_op jit(solution)/shard_map/ppermute | solution.py:393
  44.7 3.5 %collective-permute-done.refs_2_ = bf16[16,8192]{1,0:T(8,128)(2,1)S(1)} collective-permute-done((bf16[16,8192]{1,0:T(8,128)(2,1)S(1)}, bf16[16,8192]{1,0:T(8,128)(2,1)S(1)}, u32[]{:S(2)}, u32[]{:S(2)}) %collective-permute-start) | collective-permute-done | bytes 262176 | tf_op jit(solution)/shard_map/ppermute | solution.py:393
  50.3 3.7 %collective-permute-done.3.refs_2_ = bf16[16,8192]{1,0:T(8,128)(2,1)S(1)} collective-permute-done((bf16[16,8192]{1,0:T(8,128)(2,1)S(1)}, bf16[16,8192]{1,0:T(8,128)(2,1)S(1)}, u32[]{:S(2)}, u32[]{:S(2)}) %collective-permute-start.3) | collective-permute-done | bytes 262176 | tf_op jit(solution)/shard_map/ppermute | solution.py:393
  56.1 2.5 %collective-permute-done.2.refs_2_ = bf16[16,8192]{1,0:T(8,128)(2,1)S(1)} collective-permute-done((bf16[16,8192]{1,0:T(8,128)(2,1)S(1)}, bf16[16,8192]{1,0:T(8,128)(2,1)S(1)}, u32[]{:S(2)}, u32[]{:S(2)}) %collective-permute-start.2) | collective-permute-done | bytes 262176 | tf_op jit(solution)/shard_map/ppermute | solution.py:393
  60.9 25.6 %collective-permute-done.5.refs_2_ = bf16[16,8192]{1,0:T(8,128)(2,1)S(1)} collective-permute-done((bf16[16,8192]{1,0:T(8,128)(2,1)S(1)}, bf16[16,8192]{1,0:T(8,128)(2,1)S(1)}, u32[]{:S(2)}, u32[]{:S(2)}) %collective-permute-start.5) | collective-permute-done | bytes 262176 | tf_op jit(solution)/shard_map/ppermute | solution.py:393
  86.5 9.8 %stage.20 = (bf16[16,8192]{1,0:T(8,128)(2,1)S(1)}, bf16[128,16384]{1,0:T(8,128)(2,1)S(1)}, bf16[128,8192]{1,0:T(8,128)(2,1)}, f32[8,8,8192]{2,1,0:T(8,128)S(1)}) custom-call(s32[64]{0:T(128)S(1)} %copy-done.7, bf16[128,8192]{1,0:T(8,128)(2,1)S(1)} %copy-done.1, ...), custom_call_target="tpu_custom_call", output_to_operand_aliasing={{1}: (8, {}), {2}: (9, {}), {3}: (10, {})} | custom-call | flops 67108864 | bytes 6291456 | tf_op jit(solution)/shard_map/stage/pallas_call | solution.py:241
  98.2 9.8 %stage.21 = (bf16[16,8192]{1,0:T(8,128)(2,1)S(1)}, bf16[128,16384]{1,0:T(8,128)(2,1)S(1)}, bf16[128,8192]{1,0:T(8,128)(2,1)}, f32[8,8,8192]{2,1,0:T(8,128)S(1)}) custom-call(s32[64]{0:T(128)S(1)} %copy-done.7, bf16[128,8192]{1,0:T(8,128)(2,1)S(1)} %copy-done.1, ...), custom_call_target="tpu_custom_call", output_to_operand_aliasing={{1}: (8, {}), {2}: (9, {}), {3}: (10, {})} | custom-call | flops 67108864 | bytes 6291456 | tf_op jit(solution)/shard_map/stage/pallas_call | solution.py:241
  110.0 9.8 %stage.22 = (bf16[16,8192]{1,0:T(8,128)(2,1)S(1)}, bf16[128,16384]{1,0:T(8,128)(2,1)S(1)}, bf16[128,8192]{1,0:T(8,128)(2,1)}, f32[8,8,8192]{2,1,0:T(8,128)S(1)}) custom-call(s32[64]{0:T(128)S(1)} %copy-done.7, bf16[128,8192]{1,0:T(8,128)(2,1)S(1)} %copy-done.1, ...), custom_call_target="tpu_custom_call", output_to_operand_aliasing={{1}: (8, {}), {2}: (9, {}), {3}: (10, {})} | custom-call | flops 67108864 | bytes 6291456 | tf_op jit(solution)/shard_map/stage/pallas_call | solution.py:241
  121.8 9.8 %stage.23 = (bf16[16,8192]{1,0:T(8,128)(2,1)S(1)}, bf16[128,16384]{1,0:T(8,128)(2,1)S(1)}, bf16[128,8192]{1,0:T(8,128)(2,1)}, f32[8,8,8192]{2,1,0:T(8,128)S(1)}) custom-call(s32[64]{0:T(128)S(1)} %copy-done.7, bf16[128,8192]{1,0:T(8,128)(2,1)S(1)} %copy-done.1, ...), custom_call_target="tpu_custom_call", output_to_operand_aliasing={{1}: (8, {}), {2}: (9, {}), {3}: (10, {})} | custom-call | flops 67108864 | bytes 6291456 | tf_op jit(solution)/shard_map/stage/pallas_call | solution.py:241
  133.5 9.8 %stage.24 = (bf16[16,8192]{1,0:T(8,128)(2,1)S(1)}, bf16[128,16384]{1,0:T(8,128)(2,1)S(1)}, bf16[128,8192]{1,0:T(8,128)(2,1)}, f32[8,8,8192]{2,1,0:T(8,128)S(1)}) custom-call(s32[64]{0:T(128)S(1)} %copy-done.7, bf16[128,8192]{1,0:T(8,128)(2,1)S(1)} %copy-done.1, ...), custom_call_target="tpu_custom_call", output_to_operand_aliasing={{1}: (8, {}), {2}: (9, {}), {3}: (10, {})} | custom-call | flops 67108864 | bytes 6291456 | tf_op jit(solution)/shard_map/stage/pallas_call | solution.py:241
  145.3 9.8 %stage.25 = (bf16[16,8192]{1,0:T(8,128)(2,1)S(1)}, bf16[128,16384]{1,0:T(8,128)(2,1)S(1)}, bf16[128,8192]{1,0:T(8,128)(2,1)}, f32[8,8,8192]{2,1,0:T(8,128)S(1)}) custom-call(s32[64]{0:T(128)S(1)} %copy-done.7, bf16[128,8192]{1,0:T(8,128)(2,1)S(1)} %copy-done.1, ...), custom_call_target="tpu_custom_call", output_to_operand_aliasing={{1}: (8, {}), {2}: (9, {}), {3}: (10, {})} | custom-call | flops 67108864 | bytes 6291456 | tf_op jit(solution)/shard_map/stage/pallas_call | solution.py:241
  157.1 9.9 %stage.26 = (bf16[16,8192]{1,0:T(8,128)(2,1)}, bf16[128,16384]{1,0:T(8,128)(2,1)S(1)}, bf16[128,8192]{1,0:T(8,128)(2,1)}, f32[8,8,8192]{2,1,0:T(8,128)S(1)}) custom-call(s32[64]{0:T(128)S(1)} %copy-done.7, bf16[128,8192]{1,0:T(8,128)(2,1)S(1)} %copy-done.1, ...), custom_call_target="tpu_custom_call", output_to_operand_aliasing={{1}: (8, {}), {2}: (9, {}), {3}: (10, {})} | custom-call | flops 67108864 | bytes 6291456 | tf_op jit(solution)/shard_map/stage/pallas_call | solution.py:241
  166.9 1.9 collective-permute-done.10.refs_2_
  168.8 9.9 %stage.27 = (bf16[16,8192]{1,0:T(8,128)(2,1)}, bf16[128,16384]{1,0:T(8,128)(2,1)S(1)}, bf16[128,8192]{1,0:T(8,128)(2,1)}, f32[8,8,8192]{2,1,0:T(8,128)S(1)}) custom-call(s32[64]{0:T(128)S(1)} %copy-done.7, bf16[128,8192]{1,0:T(8,128)(2,1)S(1)} %copy-done.1, ...), custom_call_target="tpu_custom_call", output_to_operand_aliasing={{1}: (8, {}), {2}: (9, {}), {3}: (10, {})} | custom-call | flops 67108864 | bytes 6291456 | tf_op jit(solution)/shard_map/stage/pallas_call | solution.py:241
  180.1 1.6 copy-done.3
  181.7 2.2 copy-done.6
  183.9 5.5 %grads.1 = (bf16[8256,128]{1,0:T(8,128)(2,1)S(1)}, f32[8256,128]{1,0:T(8,128)}) custom-call(s32[128]{0:T(128)S(1)} %copy-done.8, s32[128]{0:T(128)S(1)} %copy-done.9, bf16[128,128,128]{2,1,0:T(8,128)(2,1)S(1)} %copy-done.6, bf16[128,16384]{1,0:T(8,128)(2,1)S(1)} %get-tuple-element.115.right_ref, f32[8,8,8192]{2,1,0:T(8,128)S(1)} %copy-done.3), custom_call_target="tpu_custom_call" | custom-call | tf_op jit(solution)/shard_map/grads/pallas_call | solution.py:313
  189.4 4.2 %collective-permute-done.12 = bf16[8256,128]{1,0:T(8,128)(2,1)S(1)} collective-permute-done((bf16[8256,128]{1,0:T(8,128)(2,1)S(1)}, bf16[8256,128]{1,0:T(8,128)(2,1)S(1)}, u32[]{:S(2)}, u32[]{:S(2)}) %collective-permute-start.12) | collective-permute-done | bytes 2113568 | tf_op jit(solution)/shard_map/ppermute | solution.py:340
  193.6 2.5 %fusion.2 = (bf16[8256,128]{1,0:T(8,128)(2,1)S(1)}, f32[8256,128]{1,0:T(8,128)S(1)}) fusion(f32[8256,128]{1,0:T(8,128)} %get-tuple-element.117, bf16[8256,128]{1,0:T(8,128)(2,1)S(1)} %collective-permute-done.12), kind=kLoop, calls=%fused_computation.22 | loop fusion | flops 3170304 | bytes 12681216 | tf_op jit(solution)/shard_map/convert.3
  199.9 10.7 %collective-permute-done.13 = bf16[2048,128]{1,0:T(8,128)(2,1)S(1)} collective-permute-done((bf16[2048,128]{1,0:T(8,128)(2,1)S(1)}, bf16[2048,128]{1,0:T(8,128)(2,1)S(1)}, u32[]{:S(2)}, u32[]{:S(2)}) %collective-permute-start.13) | collective-permute-done | bytes 524320 | tf_op jit(solution)/shard_map/ppermute | solution.py:340
  214.6 5.1 %collective-permute-done.18 = f32[64,128]{1,0:T(8,128)S(1)} collective-permute-done((f32[64,128]{1,0:T(8,128)S(1)}, f32[64,128]{1,0:T(8,128)S(1)}, u32[]{:S(2)}, u32[]{:S(2)}) %collective-permute-start.18) | collective-permute-done | bytes 32800 | tf_op jit(solution)/shard_map/ppermute | solution.py:340
  (70 shorter events, 36.8 us)
Async XLA Ops:
  3.5 2.5 %copy-start = (bf16[1,128,8192]{2,1,0:T(8,128)(2,1)S(1)}, bf16[1,128,8192]{2,1,0:T(8,128)(2,1)}, u32[]{:S(2)}) copy-start(bf16[1,128,8192]{2,1,0:T(8,128)(2,1)} %param.7) | copy-start | bytes 6291460
  3.5 2.5 %copy-start.4 = (f32[1,8192]{1,0:T(1,128)S(1)}, f32[1,8192]{1,0:T(1,128)}, u32[]{:S(2)}) copy-start(f32[1,8192]{1,0:T(1,128)} %refs_5_.27) | copy-start | bytes 98308
  3.5 2.5 %copy-start.7 = (s32[64]{0:T(128)S(1)}, s32[64]{0:T(128)}, u32[]{:S(2)}) copy-start(s32[64]{0:T(128)} %refs_0_.27) | copy-start | bytes 772
  30.6 12.0 %collective-permute-start.1 = (bf16[16,8192]{1,0:T(8,128)(2,1)S(1)}, bf16[16,8192]{1,0:T(8,128)(2,1)S(1)}, u32[]{:S(2)}, u32[]{:S(2)}) collective-permute-start(bf16[16,8192]{1,0:T(8,128)(2,1)S(1)} %get-tuple-element.66), channel_id=1, source_target_pairs={{8,0},{16,8},{24,16},{9,1},{17,9},{25,17},{10,2},{18,10},{26,18},{... | collective-permute-start | bytes 786440 | tf_op jit(solution)/shard_map/ppermute | solution.py:393
  32.6 15.6 %collective-permute-start = (bf16[16,8192]{1,0:T(8,128)(2,1)S(1)}, bf16[16,8192]{1,0:T(8,128)(2,1)S(1)}, u32[]{:S(2)}, u32[]{:S(2)}) collective-permute-start(bf16[16,8192]{1,0:T(8,128)(2,1)S(1)} %get-tuple-element.65), channel_id=1, source_target_pairs={{8,0},{16,8},{24,16},{9,1},{17,9},{25,17},{10,2},{18,10},{26,18},{... | collective-permute-start | bytes 786440 | tf_op jit(solution)/shard_map/ppermute | solution.py:393
  43.4 10.6 %collective-permute-start.3 = (bf16[16,8192]{1,0:T(8,128)(2,1)S(1)}, bf16[16,8192]{1,0:T(8,128)(2,1)S(1)}, u32[]{:S(2)}, u32[]{:S(2)}) collective-permute-start(bf16[16,8192]{1,0:T(8,128)(2,1)S(1)} %get-tuple-element.74), channel_id=1, source_target_pairs={{8,0},{16,8},{24,16},{9,1},{17,9},{25,17},{10,2},{18,10},{26,18},{... | collective-permute-start | bytes 786440 | tf_op jit(solution)/shard_map/ppermute | solution.py:393
  49.0 9.6 %collective-permute-start.2 = (bf16[16,8192]{1,0:T(8,128)(2,1)S(1)}, bf16[16,8192]{1,0:T(8,128)(2,1)S(1)}, u32[]{:S(2)}, u32[]{:S(2)}) collective-permute-start(bf16[16,8192]{1,0:T(8,128)(2,1)S(1)} %get-tuple-element.73), channel_id=1, source_target_pairs={{8,0},{16,8},{24,16},{9,1},{17,9},{25,17},{10,2},{18,10},{26,18},{... | collective-permute-start | bytes 786440 | tf_op jit(solution)/shard_map/ppermute | solution.py:393
  54.8 31.7 %collective-permute-start.5 = (bf16[16,8192]{1,0:T(8,128)(2,1)S(1)}, bf16[16,8192]{1,0:T(8,128)(2,1)S(1)}, u32[]{:S(2)}, u32[]{:S(2)}) collective-permute-start(bf16[16,8192]{1,0:T(8,128)(2,1)S(1)} %get-tuple-element.82), channel_id=1, source_target_pairs={{8,0},{16,8},{24,16},{9,1},{17,9},{25,17},{10,2},{18,10},{26,18},{... | collective-permute-start | bytes 786440 | tf_op jit(solution)/shard_map/ppermute | solution.py:393
  59.6 38.6 %collective-permute-start.4 = (bf16[16,8192]{1,0:T(8,128)(2,1)S(1)}, bf16[16,8192]{1,0:T(8,128)(2,1)S(1)}, u32[]{:S(2)}, u32[]{:S(2)}) collective-permute-start(bf16[16,8192]{1,0:T(8,128)(2,1)S(1)} %get-tuple-element.81), channel_id=1, source_target_pairs={{8,0},{16,8},{24,16},{9,1},{17,9},{25,17},{10,2},{18,10},{26,18},{... | collective-permute-start | bytes 786440 | tf_op jit(solution)/shard_map/ppermute | solution.py:393
  96.3 13.7 %collective-permute-start.7 = (bf16[16,8192]{1,0:T(8,128)(2,1)S(1)}, bf16[16,8192]{1,0:T(8,128)(2,1)S(1)}, u32[]{:S(2)}, u32[]{:S(2)}) collective-permute-start(bf16[16,8192]{1,0:T(8,128)(2,1)S(1)} %get-tuple-element.90), channel_id=1, source_target_pairs={{8,0},{16,8},{24,16},{9,1},{17,9},{25,17},{10,2},{18,10},{26,18},{... | collective-permute-start | bytes 786440 | tf_op jit(solution)/shard_map/ppermute | solution.py:393
  108.1 13.7 %collective-permute-start.6 = (bf16[16,8192]{1,0:T(8,128)(2,1)S(1)}, bf16[16,8192]{1,0:T(8,128)(2,1)S(1)}, u32[]{:S(2)}, u32[]{:S(2)}) collective-permute-start(bf16[16,8192]{1,0:T(8,128)(2,1)S(1)} %get-tuple-element.89), channel_id=1, source_target_pairs={{8,0},{16,8},{24,16},{9,1},{17,9},{25,17},{10,2},{18,10},{26,18},{... | collective-permute-start | bytes 786440 | tf_op jit(solution)/shard_map/ppermute | solution.py:393
  119.8 13.7 %collective-permute-start.9 = (bf16[16,8192]{1,0:T(8,128)(2,1)S(1)}, bf16[16,8192]{1,0:T(8,128)(2,1)S(1)}, u32[]{:S(2)}, u32[]{:S(2)}) collective-permute-start(bf16[16,8192]{1,0:T(8,128)(2,1)S(1)} %get-tuple-element.98), channel_id=1, source_target_pairs={{8,0},{16,8},{24,16},{9,1},{17,9},{25,17},{10,2},{18,10},{26,18},{... | collective-permute-start | bytes 786440 | tf_op jit(solution)/shard_map/ppermute | solution.py:393
  131.6 13.7 %collective-permute-start.8 = (bf16[16,8192]{1,0:T(8,128)(2,1)S(1)}, bf16[16,8192]{1,0:T(8,128)(2,1)S(1)}, u32[]{:S(2)}, u32[]{:S(2)}) collective-permute-start(bf16[16,8192]{1,0:T(8,128)(2,1)S(1)} %get-tuple-element.97), channel_id=1, source_target_pairs={{8,0},{16,8},{24,16},{9,1},{17,9},{25,17},{10,2},{18,10},{26,18},{... | collective-permute-start | bytes 786440 | tf_op jit(solution)/shard_map/ppermute | solution.py:393
  143.4 13.7 %collective-permute-start.11 = (bf16[16,8192]{1,0:T(8,128)(2,1)S(1)}, bf16[16,8192]{1,0:T(8,128)(2,1)S(1)}, u32[]{:S(2)}, u32[]{:S(2)}) collective-permute-start(bf16[16,8192]{1,0:T(8,128)(2,1)S(1)} %get-tuple-element.106), channel_id=1, source_target_pairs={{8,0},{16,8},{24,16},{9,1},{17,9},{25,17},{10,2},{18,10},{26,18},{... | collective-permute-start | bytes 786440 | tf_op jit(solution)/shard_map/ppermute | solution.py:393
  155.1 13.7 %collective-permute-start.10 = (bf16[16,8192]{1,0:T(8,128)(2,1)S(1)}, bf16[16,8192]{1,0:T(8,128)(2,1)S(1)}, u32[]{:S(2)}, u32[]{:S(2)}) collective-permute-start(bf16[16,8192]{1,0:T(8,128)(2,1)S(1)} %get-tuple-element.105), channel_id=1, source_target_pairs={{8,0},{16,8},{24,16},{9,1},{17,9},{25,17},{10,2},{18,10},{26,18},{... | collective-permute-start | bytes 786440 | tf_op jit(solution)/shard_map/ppermute | solution.py:393
  168.8 11.3 %copy-start.8 = (s32[128]{0:T(128)S(1)}, s32[128]{0:T(128)}, u32[]{:S(2)}) copy-start(s32[128]{0:T(128)} %table_ref.1) | copy-start | bytes 1540
  168.8 11.3 %copy-start.9 = (s32[128]{0:T(128)S(1)}, s32[128]{0:T(128)}, u32[]{:S(2)}) copy-start(s32[128]{0:T(128)} %constant.44.clone.perm_ref) | copy-start | bytes 1540
  189.4 4.2 %collective-permute-start.12 = (bf16[8256,128]{1,0:T(8,128)(2,1)S(1)}, bf16[8256,128]{1,0:T(8,128)(2,1)S(1)}, u32[]{:S(2)}, u32[]{:S(2)}) collective-permute-start(bf16[8256,128]{1,0:T(8,128)(2,1)S(1)} %get-tuple-element.118), channel_id=1, source_target_pairs={{0,1},{1,0},{2,3},{3,2},{4,5},{5,4},{6,7},{7,6},{8,9},{9,8},{10,11... | collective-permute-start | bytes 6340616 | tf_op jit(solution)/shard_map/ppermute | solution.py:340
  196.2 14.4 %collective-permute-start.13 = (bf16[2048,128]{1,0:T(8,128)(2,1)S(1)}, bf16[2048,128]{1,0:T(8,128)(2,1)S(1)}, u32[]{:S(2)}, u32[]{:S(2)}) collective-permute-start(bf16[2048,128]{1,0:T(8,128)(2,1)S(1)} %get-tuple-element.125), channel_id=1, source_target_pairs={{0,2},{1,3},{2,0},{3,1},{4,6},{5,7},{6,4},{7,5},{8,10},{9,11},{10,... | collective-permute-start | bytes 1572872 | tf_op jit(solution)/shard_map/ppermute | solution.py:340
  197.8 13.7 %collective-permute-start.15 = (bf16[2048,128]{1,0:T(8,128)(2,1)S(1)}, bf16[2048,128]{1,0:T(8,128)(2,1)S(1)}, u32[]{:S(2)}, u32[]{:S(2)}) collective-permute-start(bf16[2048,128]{1,0:T(8,128)(2,1)S(1)} %get-tuple-element.126), channel_id=1, source_target_pairs={{0,4},{1,5},{2,6},{3,7},{4,0},{5,1},{6,2},{7,3},{8,12},{9,13},{10,... | collective-permute-start | bytes 1572872 | tf_op jit(solution)/shard_map/ppermute | solution.py:340
  199.3 14.0 %collective-permute-start.17 = (f32[64,128]{1,0:T(8,128)S(1)}, f32[64,128]{1,0:T(8,128)S(1)}, u32[]{:S(2)}, u32[]{:S(2)}) collective-permute-start(f32[64,128]{1,0:T(8,128)S(1)} %slice.67), channel_id=1, source_target_pairs={{0,2},{1,3},{2,0},{3,1},{4,6},{5,7},{6,4},{7,5},{8,10},{9,11},{10,... | collective-permute-start | bytes 98312 | tf_op jit(solution)/shard_map/ppermute | solution.py:340
  211.7 8.6 %collective-permute-start.14 = (bf16[1024,128]{1,0:T(8,128)(2,1)S(1)}, bf16[1024,128]{1,0:T(8,128)(2,1)S(1)}, u32[]{:S(2)}, u32[]{:S(2)}) collective-permute-start(bf16[1024,128]{1,0:T(8,128)(2,1)S(1)} %slice.77), channel_id=1, source_target_pairs={{0,4},{1,5},{2,6},{3,7},{4,0},{5,1},{6,2},{7,3},{8,12},{9,13},{10,... | collective-permute-start | bytes 786440 | tf_op jit(solution)/shard_map/ppermute | solution.py:340
  213.3 6.4 %collective-permute-start.18 = (f32[64,128]{1,0:T(8,128)S(1)}, f32[64,128]{1,0:T(8,128)S(1)}, u32[]{:S(2)}, u32[]{:S(2)}) collective-permute-start(f32[64,128]{1,0:T(8,128)S(1)} %slice_add_fusion.4), channel_id=1, source_target_pairs={{0,4},{1,5},{2,6},{3,7},{4,0},{5,1},{6,2},{7,3},{8,12},{9,13},{10,... | collective-permute-start | bytes 98312 | tf_op jit(solution)/shard_map/ppermute | solution.py:340
  213.9 6.7 %collective-permute-start.16 = (bf16[1024,128]{1,0:T(8,128)(2,1)S(1)}, bf16[1024,128]{1,0:T(8,128)(2,1)S(1)}, u32[]{:S(2)}, u32[]{:S(2)}) collective-permute-start(bf16[1024,128]{1,0:T(8,128)(2,1)S(1)} %slice.76), channel_id=1, source_target_pairs={{0,2},{1,3},{2,0},{3,1},{4,6},{5,7},{6,4},{7,5},{8,10},{9,11},{10,... | collective-permute-start | bytes 786440 | tf_op jit(solution)/shard_map/ppermute | solution.py:340
  (5 other events, 9.4 us)
where the time goes:
time: 222 us
  Pallas kernels  112 us (50%)
  waiting for transfers between devices  70.9 us (32%)
  starting transfers between devices  22.1 us (10%)
  local copies, waits for them, and re-layouts  12 us (5%)
  other arithmetic  4.04 us (2%)
    pallas_call x14, Pallas kernels, stage(): pl.pallas_call(functools.partial(stage_kernel, step, segments, first), ou...  83.4 us
    ppermute x12, waiting for transfers between devices, local(): sent.append(lax.ppermute(out[0], 'segment', pairs))  49.8 us
    pallas_call x1, Pallas kernels, prologue(): pl.pallas_call(prologue_kernel, grid=(F // 8,), out_shape=(jax.ShapeDtype...  22.6 us
    ppermute x7, waiting for transfers between devices, swap(): return lax.ppermute(array, axis, [(i, i ^ 1 << bit) for i in range(size)])  21.1 us
    ppermute x12, starting transfers between devices, local(): sent.append(lax.ppermute(out[0], 'segment', pairs))  15.5 us
    ppermute x7, starting transfers between devices, swap(): return lax.ppermute(array, axis, [(i, i ^ 1 << bit) for i in range(size)])  6.57 us
    unnamed x20, local copies, waits for them, and re-layouts  6.35 us
    pallas_call x1, Pallas kernels, grads(): pl.pallas_call(functools.partial(grads_kernel, scale, blocks), out_shape=...  5.48 us
  transfers between devices with their start and end apart: 19, of which 17 were waited for; matrix products, arithmetic and copies ran while one was open for 0% of the time, Pallas kernels for 33%

commit v1 on v0

v1 whole, which is shorter than its diff:
```python
import functools
import math

import jax
import jax.numpy as jnp
from jax import lax
from jax.experimental import pallas as pl
from jax.experimental.pallas import tpu as pltpu
from jax.sharding import PartitionSpec as P

F = 64
B = 128
EPS = 1e-05
CHUNKS = 8
LAG = 2
ANY = pl.BlockSpec(memory_space=pl.ANY)
VMEM = pl.BlockSpec(memory_space=pltpu.VMEM)
SMEM = pl.BlockSpec(memory_space=pltpu.SMEM)
TN = (((0,), (0,)), ((), ()))
LIMIT = 16 << 20


def dot(a, b):
    return jnp.dot(a, b, preferred_element_type=jnp.float32)


def dot_tn(a, b):
    return lax.dot_general(a, b, TN, preferred_element_type=jnp.float32)


def col(j):
    if isinstance(j, int):
        return pl.ds(j * B, B)
    return pl.ds(pl.multiple_of(j * B, B), B)


def exchange(parts, lane_bit):
    lane = lax.broadcasted_iota(jnp.int32, parts[0].shape, 1)
    parts = list(parts)
    for i in range(3):
        shift = 1 << (lane_bit + i)
        upper = (lane & shift) != 0
        for low in range(8):
            if low & (1 << i):
                continue
            high = low | (1 << i)
            a, b = parts[low], parts[high]
            parts[low] = jnp.where(upper, pltpu.roll(b, shift, 1), a)
            parts[high] = jnp.where(upper, b, pltpu.roll(a, B - shift, 1))
    return parts


def gelu_pair(v):
    cdf = 0.5 * (1.0 + lax.erf(v * 0.7071067811865476))
    density = jnp.exp(-0.5 * v * v) * 0.3989422804014327
    return v * cdf, cdf + v * density


def matrix(rule):
    row = lax.broadcasted_iota(jnp.int32, (B, B), 0)
    column = lax.broadcasted_iota(jnp.int32, (B, B), 1)
    return rule(row, column).astype(jnp.float32).astype(jnp.bfloat16)


def prepare_kernel(w_ref, w1_ref, w0_ref):
    half = B // 2
    mixed = matrix(lambda r, c: c == 2 * (r % half) + r // half)
    eye = matrix(lambda r, c: c == r)
    for j in range(F):
        w1_ref[j] = dot_tn(w_ref[1, j], mixed).astype(jnp.bfloat16)
    for j in range(F):
        w0_ref[j] = dot_tn(w_ref[0, j], eye).astype(jnp.bfloat16)


def prepare(weights):
    shape = jax.ShapeDtypeStruct((F, B, B), jnp.bfloat16)
    return pl.pallas_call(
        prepare_kernel,
        out_shape=(shape, shape),
        in_specs=[VMEM],
        out_specs=(VMEM, VMEM),
        compiler_params=pltpu.CompilerParams(vmem_limit_bytes=LIMIT),
        name="prepare",
    )(weights)


def span(plan, step, segments):
    position = lax.axis_index("segment")
    first = last = 0
    for p in range(segments):
        done, now = sum(plan[p][:step]), sum(plan[p][: step + 1])
        first = jnp.where(position == p, done, first)
        last = jnp.where(position == p, now, last)
    return first, last


def spread(pieces, slots, ready):
    plan = [0] * (max(slots) + 1)
    left = pieces
    for index, step in enumerate(slots):
        share = -(-left // (len(slots) - index))
        share = min(share, ready(step) - (pieces - left))
        plan[step] = share
        left -= share
    assert left == 0
    return plan


def plans(segments):
    steps = CHUNKS + LAG * (segments - 1)
    forward_plan, mix_plan = [], []
    for p in range(segments):
        begin = LAG * (segments - 1 - p)
        end = begin + CHUNKS
        if begin == 0:
            ahead = spread(CHUNKS, range(CHUNKS), lambda step: CHUNKS)
        else:
            ahead = spread(CHUNKS, range(min(begin, 4)), lambda step: CHUNKS)
        ahead += [0] * (steps - len(ahead))
        idle = [step for step in range(steps) if step < begin or step >= end]
        if begin == 0 or begin < steps - end:
            idle = [step for step in idle if step >= end][:4]
        blend = spread(CHUNKS // 2, idle[-4:], lambda step: sum(ahead[: step + 1]) // 2)
        blend += [0] * (steps - len(blend))
        forward_plan.append(ahead)
        mix_plan.append(blend)
    return forward_plan, mix_plan


def forward_kernel(step, plan, first, *refs):
    x_ref, gain_ref, w_ref = refs[:3]
    inv_ref, left_ref, z_ref, slope_ref, pre_buf = refs[3:] if first else refs[7:]
    rows = pre_buf.shape[0]

    @pl.loop(*span(plan, step, len(plan)))
    def _(chunk):
        at_rows = pl.ds(pl.multiple_of(chunk * rows, rows), rows)

        def square(j, total):
            v = x_ref[at_rows, col(j)].astype(jnp.float32)
            return total + v * v

        total = lax.fori_loop(0, F, square, jnp.zeros((rows, B), jnp.float32), unroll=16)
        mean = jnp.sum(total, axis=1, keepdims=True) * (1.0 / (F * B))
        inv = jnp.broadcast_to(lax.rsqrt(mean + EPS), (rows, B))
        inv_ref[at_rows, :] = inv

        @pl.loop(0, F, unroll=32)
        def _(j):
            h = (x_ref[at_rows, col(j)].astype(jnp.float32) * inv * gain_ref[:, col(j)]).astype(jnp.bfloat16)
            left_ref[at_rows, col(j)] = h
            pre_buf[:, col(j)] = dot(h, w_ref[0, j])

        @pl.loop(0, F, unroll=8)
        def _(j):
            z, slope = gelu_pair(pre_buf[:, col(j)])
            slope_ref[at_rows, col(j)] = slope
            z_ref[at_rows, col(j)] = z.astype(jnp.bfloat16)


def forward(step, plan, x, gain, weights, carried):
    n = x.shape[0]
    wide = F * B
    first = carried is None
    return pl.pallas_call(
        functools.partial(forward_kernel, step, plan, first),
        out_shape=(
            jax.ShapeDtypeStruct((n, B), jnp.float32),
            jax.ShapeDtypeStruct((n, 2 * wide), jnp.bfloat16),
            jax.ShapeDtypeStruct((n, wide), jnp.bfloat16),
            jax.ShapeDtypeStruct((n, wide), jnp.float32),
        ),
        in_specs=[VMEM] * (3 if first else 7),
        out_specs=(VMEM,) * 4,
        scratch_shapes=[pltpu.VMEM((n // CHUNKS, wide), jnp.float32)],
        input_output_aliases={} if first else {3: 0, 4: 1, 5: 2, 6: 3},
        compiler_params=pltpu.CompilerParams(vmem_limit_bytes=LIMIT),
        cost_estimate=pl.CostEstimate(flops=1 << 20, bytes_accessed=4 << 20, transcendentals=0),
        name="forward",
    )(x, gain, weights, *(() if first else carried))


def mix_kernel(step, plan, z_ref, old_ref, left_ref, low_buf, mid_buf):
    rows = low_buf.shape[1]
    half = B // 2
    apart = matrix(lambda r, c: c == r // 2 + half * (r % 2))

    @pl.loop(*span(plan, step, len(plan)))
    def _(pair):
        at_rows = pl.ds(pl.multiple_of(pair * rows, rows), rows)

        @pl.loop(0, F, unroll=8)
        def _(j):
            low_buf[j] = dot(z_ref[at_rows, col(j)], apart).astype(jnp.bfloat16)

        @pl.loop(0, 8, unroll=2)
        def _(k):
            parts = exchange([low_buf[8 * k + i] for i in range(8)], 0)
            for i in range(8):
                mid_buf[8 * i + k] = parts[i]

        @pl.loop(0, 8, unroll=2)
        def _(low):
            parts = exchange([mid_buf[8 * low + g] for g in range(8)], 3)
            for g in range(8):
                left_ref[at_rows, col(F + 8 * g + low)] = parts[g]


def mix(step, plan, z, left):
    n = z.shape[0]
    return pl.pallas_call(
        functools.partial(mix_kernel, step, plan),
        out_shape=jax.ShapeDtypeStruct((n, 2 * F * B), jnp.bfloat16),
        in_specs=[VMEM] * 2,
        out_specs=VMEM,
        scratch_shapes=[pltpu.VMEM((F, 2 * n // CHUNKS, B), jnp.bfloat16)] * 2,
        input_output_aliases={1: 0},
        compiler_params=pltpu.CompilerParams(vmem_limit_bytes=LIMIT),
        cost_estimate=pl.CostEstimate(flops=1 << 20, bytes_accessed=4 << 20, transcendentals=0),
        name="mix",
    )(z, left)


def stage_kernel(step, segments, first, *refs):
    (order_ref, cot_ref, inc_ref, x_ref, inv_ref, slope_ref, gain_ref, w1_ref, w0_ref) = refs[:9]
    refs = refs[9:] if first else refs[11:]
    (send_ref, right_ref, part_ref, g_buf, low_buf, mid_buf, gh_buf) = refs
    rows = g_buf.shape[0]
    wide = F * B
    position = lax.axis_index("segment")
    chunk = step - LAG * (segments - 1 - position)
    top = position == segments - 1

    @pl.when(jnp.logical_and(chunk >= 0, chunk < CHUNKS))
    def _():
        at_rows = pl.ds(pl.multiple_of(chunk * rows, rows), rows)

        @pl.when(top)
        def _():
            g_buf[...] = cot_ref[at_rows, :]

        @pl.when(jnp.logical_not(top))
        def _():
            g_buf[...] = inc_ref[...]

        for j in range(F):
            g = g_buf[:, col(j)]
            right_ref[at_rows, col(F + j)] = g
            low_buf[order_ref[j]] = dot(g, w1_ref[j]).astype(jnp.bfloat16)

        @pl.loop(0, 8, unroll=4)
        def _(k):
            parts = exchange([low_buf[8 * k + i] for i in range(8)], 1)
            for i in range(8):
                mid_buf[8 * i + k] = parts[i]

        @pl.loop(0, 8, unroll=4)
        def _(low):
            parts = exchange([mid_buf[8 * low + g] for g in range(8)], 4)
            for g in range(8):
                at = col(8 * g + low)
                right_ref[at_rows, at] = (parts[g].astype(jnp.float32) * slope_ref[at_rows, at]).astype(jnp.bfloat16)

        inv = inv_ref[at_rows, :]
        inner = jnp.zeros((rows, B), jnp.float32)
        for j in range(F):
            gh_buf[:, col(j)] = dot(right_ref[at_rows, col(j)], w0_ref[j])

        def weigh(j, inner):
            at = col(j)
            term = gh_buf[:, at] * (x_ref[at_rows, at].astype(jnp.float32) * inv)
            part = term[:8]
            for t in range(8, rows, 8):
                part = part + term[t : t + 8]
            part_ref[:, at] = jnp.where(chunk == 0, 0.0, part_ref[:, at]) + part
            return inner + term * gain_ref[:, at]

        inner = lax.fori_loop(0, F, weigh, inner, unroll=8)
        inner = jnp.sum(inner, axis=1, keepdims=True) * (1.0 / (F * B))

        @pl.loop(0, F, unroll=8)
        def _(j):
            at = col(j)
            xh = x_ref[at_rows, at].astype(jnp.float32) * inv
            value = g_buf[:, at].astype(jnp.float32) + inv * (gh_buf[:, at] * gain_ref[:, at] - xh * inner)
            value = value.astype(jnp.bfloat16)
            send_ref[:, at] = value
            right_ref[at_rows, col(2 * F + j)] = value


def stage(step, segments, order, cot, inc, x, inv, slope, gain, w1, w0, carried):
    n = x.shape[0]
    rows = n // CHUNKS
    wide = F * B
    bf, f32 = jnp.bfloat16, jnp.float32
    first = carried is None
    args = [order, cot, inc, x, inv, slope, gain, w1, w0] + ([] if first else list(carried))
    return pl.pallas_call(
        functools.partial(stage_kernel, step, segments, first),
        out_shape=(
            jax.ShapeDtypeStruct((rows, wide), bf),
            jax.ShapeDtypeStruct((n, 3 * wide), bf),
            jax.ShapeDtypeStruct((8, wide), f32),
        ),
        in_specs=[SMEM] + [VMEM] * (8 if first else 10),
        out_specs=(VMEM,) * 3,
        scratch_shapes=[
            pltpu.VMEM((rows, wide), bf),
            pltpu.VMEM((F, rows, B), bf),
            pltpu.VMEM((F, rows, B), bf),
            pltpu.VMEM((rows, wide), f32),
        ],
        input_output_aliases={} if first else {9: 1, 10: 2},
        compiler_params=pltpu.CompilerParams(vmem_limit_bytes=LIMIT),
        cost_estimate=pl.CostEstimate(flops=4 * rows * wide * B, bytes_accessed=6 << 20, transcendentals=0),
        name="stage",
    )(*args)


def grads_kernel(scale, blocks, table_ref, perm_ref, left_col_ref, left_ref, right_ref, part_ref, send_ref, keep_ref, grad_ref, s_buf, k_buf, sem):
    me = lax.axis_index("dp")
    half = F
    chunk_rows = 8 * B
    out = pltpu.make_async_copy(right_ref.at[:, pl.ds(2 * F * B, F * B)], grad_ref, sem.at[2])
    out.start()

    def rows_of(k, size=chunk_rows):
        return pl.ds(pl.multiple_of(k * chunk_rows, chunk_rows), size)

    for j in range(F):
        total = jnp.sum(part_ref[:, j * B : (j + 1) * B], axis=0, keepdims=True) * scale
        k_buf[half * B + j : half * B + j + 1, :] = total
    s_buf[half * B :, :] = k_buf[half * B :, :].astype(jnp.bfloat16)

    def product(p, buf, at):
        which = table_ref[perm_ref[p] ^ (me * blocks)]
        value = dot_tn(left_ref[:, col(left_col_ref[which])], right_ref[:, col(which)]) * scale
        buf[at, :] = value.astype(buf.dtype)

    for buf, ref, base, index in ((s_buf, send_ref, 0, 0), (k_buf, keep_ref, half, 1)):

        @pl.loop(0, 8)
        def _(k):
            for i in range(8):
                p = 8 * k + i
                product(base + p, buf, pl.ds(pl.multiple_of(p * B, B), B))
            pltpu.make_async_copy(buf.at[rows_of(k)], ref.at[rows_of(k)], sem.at[index]).start()

    tail = pl.ds(half * B, F)
    pltpu.make_async_copy(s_buf.at[tail], send_ref.at[tail], sem.at[0]).start()
    pltpu.make_async_copy(k_buf.at[tail], keep_ref.at[tail], sem.at[1]).start()
    pltpu.make_async_copy(s_buf, send_ref, sem.at[0]).wait()
    pltpu.make_async_copy(k_buf, keep_ref, sem.at[1]).wait()
    out.wait()


def grads(scale, blocks, table, perm, left_col, left, right, part):
    rows = F * B + F
    n = left.shape[0]
    return pl.pallas_call(
        functools.partial(grads_kernel, scale, blocks),
        out_shape=(
            jax.ShapeDtypeStruct((rows, B), jnp.bfloat16),
            jax.ShapeDtypeStruct((rows, B), jnp.float32),
            jax.ShapeDtypeStruct((n, F * B), jnp.bfloat16),
        ),
        in_specs=[SMEM, SMEM, SMEM, VMEM, VMEM, VMEM],
        out_specs=(ANY, ANY, ANY),
        scratch_shapes=[
            pltpu.VMEM((rows, B), jnp.bfloat16),
            pltpu.VMEM((rows, B), jnp.float32),
            pltpu.SemaphoreType.DMA((3,)),
        ],
        compiler_params=pltpu.CompilerParams(vmem_limit_bytes=LIMIT),
        name="grads",
    )(table, perm, left_col, left, right, part)


def order_of(bits, low_first):
    def place(q):
        digits = [(q >> k) & 1 for k in range(bits)]
        if not low_first:
            digits = digits[::-1]
        return [1 - d for d in digits]

    return sorted(range(1 << bits), key=place)


def swap(array, axis, bit):
    size = lax.axis_size(axis)
    return lax.ppermute(array, axis, [(i, i ^ (1 << bit)) for i in range(size)])


def reduce_owners(send, keep, dp, blocks):
    bits = dp.bit_length() - 2
    got = swap(send, "dp", 0)
    total = keep + got.astype(jnp.float32)
    first = max(blocks // 2, 1)
    cut = (dp // 2) * first * B
    sides = [(total[:cut], list(range(1, bits + 1))), (total[cut : F * B], list(range(bits, 0, -1)))]
    gain = total[F * B :]
    ends = []
    for index in range(bits):
        sent = []
        for side, bits_of in sides:
            half = side.shape[0] // 2
            if side.shape[0]:
                sent.append(swap(side[:half].astype(jnp.bfloat16), "dp", bits_of[index]))
            else:
                sent.append(None)
        got_gain = swap(gain, "dp", index + 1)
        gain = gain + got_gain
        sides = [
            (side[side.shape[0] // 2 :] + (0 if other is None else other.astype(jnp.float32)), bits_of)
            for (side, bits_of), other in zip(sides, sent)
        ]
    return jnp.concatenate([side for side, _ in sides], axis=0), gain


def local(acts, weights, gains, cotangent, block_order, owner_table):
    x = acts[0]
    n = x.shape[0]
    segments = lax.axis_size("segment")
    dp = lax.axis_size("dp")
    blocks = 2 * F // dp
    scale = 1.0 / math.sqrt(n * dp)
    rows = n // CHUNKS
    steps = CHUNKS + LAG * (segments - 1)
    pairs = [(i, i - 1) for i in range(1, segments)]
    w1, w0 = prepare(weights[0])
    forward_plan, mix_plan = plans(segments)
    sent, carried, ahead = [], None, None
    for step in range(steps):
        if any(plan[step] for plan in forward_plan):
            ahead = forward(step, forward_plan, x, gains, weights[0], ahead)
        inv, left, z, slope = ahead
        inc = sent[step - LAG] if step >= LAG else cotangent[:rows]
        out = stage(step, segments, block_order, cotangent, inc, x, inv, slope, gains, w1, w0, carried)
        carried = out[1:]
        if step < steps - LAG:
            sent.append(lax.ppermute(out[0], "segment", pairs))
        if any(plan[step] for plan in mix_plan):
            ahead = (inv, mix(step, mix_plan, z, left), z, slope)
    inv, left, z, slope = ahead
    right, part = carried

    bits = dp.bit_length() - 2
    first = max(blocks // 2, 1)
    places = [(2 * q) * blocks + i for q in order_of(bits, True) for i in range(first)]
    places += [(2 * q) * blocks + i for q in order_of(bits, False) for i in range(first, blocks)]
    perm = jnp.array([p + blocks for p in places] + places, jnp.int32)
    send, keep, input_gradient = grads(
        scale, blocks, owner_table, perm, jnp.concatenate([jnp.arange(F, dtype=jnp.int32), F + block_order]), left, right, part
    )
    owned, gain = reduce_owners(send, keep, dp, blocks)
    width = F * B // dp
    own_gain = lax.dynamic_slice(gain.reshape(F * B), (lax.axis_index("dp") * width,), (width,))
    return input_gradient[None], owned.reshape(1, blocks, B, B), own_gain[None]


def solution(mesh):
    return jax.shard_map(
        local,
        mesh=mesh,
        in_specs=(
            P("segment", "dp", None),
            P("segment", None, None, None, None),
            P("segment", None),
            P("dp", None),
            P(),
            P(),
        ),
        out_specs=(P("segment", "dp", None), P("segment", "dp", None, None), P("segment", "dp")),
        check_vma=False,
    )
```

time: 222 us -> 142 us (0.64)
  the two profiles are of different devices: /device:TPU:0 before, /device:TPU:16 now
where the time goes in v1:
time: 142 us
  Pallas kernels  67.8 us (48%)
  starting transfers between devices  37.9 us (27%)
  waiting for transfers between devices  27.8 us (20%)
  local copies, waits for them, and re-layouts  5.29 us (4%)
  other arithmetic  1.97 us (1%)
    pallas_call x14, Pallas kernels, stage(): pl.pallas_call(functools.partial(stage_kernel, step, segments, first), ou...  35 us
    ppermute x12, starting transfers between devices, local(): sent.append(lax.ppermute(out[0], 'segment', pairs))  31.3 us
    ppermute x7, waiting for transfers between devices, swap(): return lax.ppermute(array, axis, [(i, i ^ 1 << bit) for i in range(size)])  21.1 us
    pallas_call x10, Pallas kernels, mix(): pl.pallas_call(functools.partial(mix_kernel, step, plan), out_shape=jax.S...  15 us
    pallas_call x8, Pallas kernels, forward(): pl.pallas_call(functools.partial(forward_kernel, step, plan, first), out_...  10.4 us
    ppermute x12, waiting for transfers between devices, local(): sent.append(lax.ppermute(out[0], 'segment', pairs))  6.67 us
    ppermute x7, starting transfers between devices, swap(): return lax.ppermute(array, axis, [(i, i ^ 1 << bit) for i in range(size)])  6.54 us
    pallas_call x1, Pallas kernels, grads(): pl.pallas_call(functools.partial(grads_kernel, scale, blocks), out_shape=...  6.06 us
  transfers between devices with their start and end apart: 19, of which 11 were waited for; matrix products, arithmetic and copies ran while one was open for 1% of the time, Pallas kernels for 38%

profile of v1, /device:TPU:16, one launch (start us, length us, event | category | flops | bytes accessed | tf_op | source)
XLA Modules:
  0.0 141.9 jit_solution(8384969576589144928)
XLA Ops:
  0.7 2.3 %copy-done.2 = bf16[1,2,64,128,128]{4,3,2,1,0:T(8,128)(2,1)S(1)} copy-done((bf16[1,2,64,128,128]{4,3,2,1,0:T(8,128)(2,1)S(1)}, bf16[1,2,64,128,128]{4,3,2,1,0:T(8,128)(2,1)}, u32[]{:S(2)}) %copy-start.2) | copy-done | bytes 4194328
  6.6 5.1 %forward.8 = (f32[128,128]{1,0:T(8,128)S(1)}, bf16[128,16384]{1,0:T(8,128)(2,1)S(1)}, bf16[128,8192]{1,0:T(8,128)(2,1)S(1)}, f32[128,8192]{1,0:T(8,128)S(1)}) custom-call(bf16[128,8192]{1,0:T(8,128)(2,1)S(1)} %bitcast.7, f32[1,8192]{1,0:T(1,128)S(1)} %copy-done.5, bf16[2,64,128,128]{3,2,1,0:T(8,128)(2,1)S(1)} %bitcast.30), custom_call_target="tpu_custom_call" | custom-call | flops 1048576 | bytes 4194304 | tf_op jit(solution)/shard_map/forward/pallas_call | solution.py:165
  14.3 5.2 %forward.9 = (f32[128,128]{1,0:T(8,128)S(1)}, bf16[128,16384]{1,0:T(8,128)(2,1)S(1)}, bf16[128,8192]{1,0:T(8,128)(2,1)S(1)}, f32[128,8192]{1,0:T(8,128)S(1)}) custom-call(bf16[128,8192]{1,0:T(8,128)(2,1)S(1)} %bitcast.9, f32[1,8192]{1,0:T(1,128)S(1)} %copy-done.5, ...), custom_call_target="tpu_custom_call", output_to_operand_aliasing={{0}: (3, {}), {1}: (4, {}), {2}: (5, {}), {3}: (6, {})} | custom-call | flops 1048576 | bytes 4194304 | tf_op jit(solution)/shard_map/forward/pallas_call | solution.py:165
  22.3 3.7 %stage.16 = (bf16[16,8192]{1,0:T(8,128)(2,1)S(1)}, bf16[128,24576]{1,0:T(8,128)(2,1)S(1)}, f32[8,8192]{1,0:T(8,128)S(1)}) custom-call(s32[64]{0:T(128)S(1)} %copy-done.6, bf16[128,8192]{1,0:T(8,128)(2,1)S(1)} %copy-done.1, bf16[16,8192]{1,0:T(8,128)(2,1)S(1)} %collective-permute-done.1.refs_2_, ...), custom_call_target="tpu_custom_call", output_to_operand_aliasing={{1}: (9, {}), {2}: (10, {})} | custom-call | flops 67108864 | bytes 6291456 | tf_op jit(solution)/shard_map/stage/pallas_call | solution.py:298
  30.0 3.7 %stage.17 = (bf16[16,8192]{1,0:T(8,128)(2,1)S(1)}, bf16[128,24576]{1,0:T(8,128)(2,1)S(1)}, f32[8,8192]{1,0:T(8,128)S(1)}) custom-call(s32[64]{0:T(128)S(1)} %copy-done.6, bf16[128,8192]{1,0:T(8,128)(2,1)S(1)} %copy-done.1, bf16[16,8192]{1,0:T(8,128)(2,1)S(1)} %collective-permute-done.refs_2_, ...), custom_call_target="tpu_custom_call", output_to_operand_aliasing={{1}: (9, {}), {2}: (10, {})} | custom-call | flops 67108864 | bytes 6291456 | tf_op jit(solution)/shard_map/stage/pallas_call | solution.py:298
  36.4 3.9 %stage.18 = (bf16[16,8192]{1,0:T(8,128)(2,1)S(1)}, bf16[128,24576]{1,0:T(8,128)(2,1)S(1)}, f32[8,8192]{1,0:T(8,128)S(1)}) custom-call(s32[64]{0:T(128)S(1)} %copy-done.6, bf16[128,8192]{1,0:T(8,128)(2,1)S(1)} %copy-done.1, bf16[16,8192]{1,0:T(8,128)(2,1)S(1)} %collective-permute-done.3.refs_2_, ...), custom_call_target="tpu_custom_call", output_to_operand_aliasing={{1}: (9, {}), {2}: (10, {})} | custom-call | flops 67108864 | bytes 6291456 | tf_op jit(solution)/shard_map/stage/pallas_call | solution.py:298
  40.3 3.2 %collective-permute-start.5 = (bf16[16,8192]{1,0:T(8,128)(2,1)S(1)}, bf16[16,8192]{1,0:T(8,128)(2,1)S(1)}, u32[]{:S(2)}, u32[]{:S(2)}) collective-permute-start(bf16[16,8192]{1,0:T(8,128)(2,1)S(1)} %get-tuple-element.129), channel_id=1, source_target_pairs={{8,0},{16,8},{24,16},{9,1},{17,9},{25,17},{10,2},{18,10},{26,18},{... | collective-permute-start | bytes 786440 | tf_op jit(solution)/shard_map/ppermute | solution.py:441
  43.6 3.7 %stage.19 = (bf16[16,8192]{1,0:T(8,128)(2,1)S(1)}, bf16[128,24576]{1,0:T(8,128)(2,1)S(1)}, f32[8,8192]{1,0:T(8,128)S(1)}) custom-call(s32[64]{0:T(128)S(1)} %copy-done.6, bf16[128,8192]{1,0:T(8,128)(2,1)S(1)} %copy-done.1, bf16[16,8192]{1,0:T(8,128)(2,1)S(1)} %collective-permute-done.2.refs_2_, ...), custom_call_target="tpu_custom_call", output_to_operand_aliasing={{1}: (9, {}), {2}: (10, {})} | custom-call | flops 67108864 | bytes 6291456 | tf_op jit(solution)/shard_map/stage/pallas_call | solution.py:298
  49.4 3.7 %stage.20 = (bf16[16,8192]{1,0:T(8,128)(2,1)S(1)}, bf16[128,24576]{1,0:T(8,128)(2,1)S(1)}, f32[8,8192]{1,0:T(8,128)S(1)}) custom-call(s32[64]{0:T(128)S(1)} %copy-done.6, bf16[128,8192]{1,0:T(8,128)(2,1)S(1)} %copy-done.1, bf16[16,8192]{1,0:T(8,128)(2,1)S(1)} %collective-permute-done.5.refs_2_, ...), custom_call_target="tpu_custom_call", output_to_operand_aliasing={{1}: (9, {}), {2}: (10, {})} | custom-call | flops 67108864 | bytes 6291456 | tf_op jit(solution)/shard_map/stage/pallas_call | solution.py:298
  53.1 3.5 %collective-permute-start.7 = (bf16[16,8192]{1,0:T(8,128)(2,1)S(1)}, bf16[16,8192]{1,0:T(8,128)(2,1)S(1)}, u32[]{:S(2)}, u32[]{:S(2)}) collective-permute-start(bf16[16,8192]{1,0:T(8,128)(2,1)S(1)} %get-tuple-element.135), channel_id=1, source_target_pairs={{8,0},{16,8},{24,16},{9,1},{17,9},{25,17},{10,2},{18,10},{26,18},{... | collective-permute-start | bytes 786440 | tf_op jit(solution)/shard_map/ppermute | solution.py:441
  56.7 3.7 %stage.21 = (bf16[16,8192]{1,0:T(8,128)(2,1)S(1)}, bf16[128,24576]{1,0:T(8,128)(2,1)S(1)}, f32[8,8192]{1,0:T(8,128)S(1)}) custom-call(s32[64]{0:T(128)S(1)} %copy-done.6, bf16[128,8192]{1,0:T(8,128)(2,1)S(1)} %copy-done.1, bf16[16,8192]{1,0:T(8,128)(2,1)S(1)} %collective-permute-done.4.refs_2_, ...), custom_call_target="tpu_custom_call", output_to_operand_aliasing={{1}: (9, {}), {2}: (10, {})} | custom-call | flops 67108864 | bytes 6291456 | tf_op jit(solution)/shard_map/stage/pallas_call | solution.py:298
  62.9 3.7 %stage.22 = (bf16[16,8192]{1,0:T(8,128)(2,1)S(1)}, bf16[128,24576]{1,0:T(8,128)(2,1)S(1)}, f32[8,8192]{1,0:T(8,128)S(1)}) custom-call(s32[64]{0:T(128)S(1)} %copy-done.6, bf16[128,8192]{1,0:T(8,128)(2,1)S(1)} %copy-done.1, bf16[16,8192]{1,0:T(8,128)(2,1)S(1)} %collective-permute-done.7.refs_2_, ...), custom_call_target="tpu_custom_call", output_to_operand_aliasing={{1}: (9, {}), {2}: (10, {})} | custom-call | flops 67108864 | bytes 6291456 | tf_op jit(solution)/shard_map/stage/pallas_call | solution.py:298
  69.3 3.7 %stage.23 = (bf16[16,8192]{1,0:T(8,128)(2,1)S(1)}, bf16[128,24576]{1,0:T(8,128)(2,1)S(1)}, f32[8,8192]{1,0:T(8,128)S(1)}) custom-call(s32[64]{0:T(128)S(1)} %copy-done.6, bf16[128,8192]{1,0:T(8,128)(2,1)S(1)} %copy-done.1, bf16[16,8192]{1,0:T(8,128)(2,1)S(1)} %collective-permute-done.6.refs_2_, ...), custom_call_target="tpu_custom_call", output_to_operand_aliasing={{1}: (9, {}), {2}: (10, {})} | custom-call | flops 67108864 | bytes 6291456 | tf_op jit(solution)/shard_map/stage/pallas_call | solution.py:298
  75.7 5.2 %collective-permute-start.11 = (bf16[16,8192]{1,0:T(8,128)(2,1)S(1)}, bf16[16,8192]{1,0:T(8,128)(2,1)S(1)}, u32[]{:S(2)}, u32[]{:S(2)}) collective-permute-start(bf16[16,8192]{1,0:T(8,128)(2,1)S(1)} %get-tuple-element.147), channel_id=1, source_target_pairs={{8,0},{16,8},{24,16},{9,1},{17,9},{25,17},{10,2},{18,10},{26,18},{... | collective-permute-start | bytes 786440 | tf_op jit(solution)/shard_map/ppermute | solution.py:441
  80.9 3.1 %collective-permute-done.8.refs_2_ = bf16[16,8192]{1,0:T(8,128)(2,1)S(1)} collective-permute-done((bf16[16,8192]{1,0:T(8,128)(2,1)S(1)}, bf16[16,8192]{1,0:T(8,128)(2,1)S(1)}, u32[]{:S(2)}, u32[]{:S(2)}) %collective-permute-start.8) | collective-permute-done | bytes 262176 | tf_op jit(solution)/shard_map/ppermute | solution.py:441
  84.8 3.1 %collective-permute-start.10 = (bf16[16,8192]{1,0:T(8,128)(2,1)S(1)}, bf16[16,8192]{1,0:T(8,128)(2,1)S(1)}, u32[]{:S(2)}, u32[]{:S(2)}) collective-permute-start(bf16[16,8192]{1,0:T(8,128)(2,1)S(1)} %get-tuple-element.146), channel_id=1, source_target_pairs={{8,0},{16,8},{24,16},{9,1},{17,9},{25,17},{10,2},{18,10},{26,18},{... | collective-permute-start | bytes 786440 | tf_op jit(solution)/shard_map/ppermute | solution.py:441
  88.0 3.7 %mix.16.old_ref = bf16[128,16384]{1,0:T(8,128)(2,1)S(1)} custom-call(bf16[128,8192]{1,0:T(8,128)(2,1)S(1)} %get-tuple-element.108.z_ref, bf16[128,16384]{1,0:T(8,128)(2,1)S(1)} %mix.15.old_ref), custom_call_target="tpu_custom_call", output_to_operand_aliasing={{}: (1, {})} | custom-call | flops 1048576 | bytes 4194304 | tf_op jit(solution)/shard_map/mix/pallas_call | solution.py:211
  91.7 3.7 %mix.17.old_ref = bf16[128,16384]{1,0:T(8,128)(2,1)S(1)} custom-call(bf16[128,8192]{1,0:T(8,128)(2,1)S(1)} %get-tuple-element.108.z_ref, bf16[128,16384]{1,0:T(8,128)(2,1)S(1)} %mix.16.old_ref), custom_call_target="tpu_custom_call", output_to_operand_aliasing={{}: (1, {})} | custom-call | flops 1048576 | bytes 4194304 | tf_op jit(solution)/shard_map/mix/pallas_call | solution.py:211
  95.5 3.7 %mix.18.old_ref = bf16[128,16384]{1,0:T(8,128)(2,1)S(1)} custom-call(bf16[128,8192]{1,0:T(8,128)(2,1)S(1)} %get-tuple-element.108.z_ref, bf16[128,16384]{1,0:T(8,128)(2,1)S(1)} %mix.17.old_ref), custom_call_target="tpu_custom_call", output_to_operand_aliasing={{}: (1, {})} | custom-call | flops 1048576 | bytes 4194304 | tf_op jit(solution)/shard_map/mix/pallas_call | solution.py:211
  99.2 3.7 %mix.19.left_ref = bf16[128,16384]{1,0:T(8,128)(2,1)S(1)} custom-call(bf16[128,8192]{1,0:T(8,128)(2,1)S(1)} %get-tuple-element.108.z_ref, bf16[128,16384]{1,0:T(8,128)(2,1)S(1)} %mix.18.old_ref), custom_call_target="tpu_custom_call", output_to_operand_aliasing={{}: (1, {})} | custom-call | flops 1048576 | bytes 4194304 | tf_op jit(solution)/shard_map/mix/pallas_call | solution.py:211
  105.5 6.1 %grads.1 = (bf16[8256,128]{1,0:T(8,128)(2,1)S(1)}, f32[8256,128]{1,0:T(8,128)S(1)}, bf16[128,8192]{1,0:T(8,128)(2,1)}) custom-call(s32[128]{0:T(128)S(1)} %copy-done.7, s32[128]{0:T(128)S(1)} %copy-done.8, s32[128]{0:T(128)S(1)} %pad_add_fusion.left_col_ref, bf16[128,16384]{1,0:T(8,128)(2,1)S(1)} %mix.19.left_ref, ...), custom_call_target="tpu_custom_call" | custom-call | tf_op jit(solution)/shard_map/grads/pallas_call | solution.py:360
  111.6 4.2 %collective-permute-done.12 = bf16[8256,128]{1,0:T(8,128)(2,1)S(1)} collective-permute-done((bf16[8256,128]{1,0:T(8,128)(2,1)S(1)}, bf16[8256,128]{1,0:T(8,128)(2,1)S(1)}, u32[]{:S(2)}, u32[]{:S(2)}) %collective-permute-start.12) | collective-permute-done | bytes 2113568 | tf_op jit(solution)/shard_map/ppermute | solution.py:391
  120.1 10.8 %collective-permute-done.13 = bf16[2048,128]{1,0:T(8,128)(2,1)S(1)} collective-permute-done((bf16[2048,128]{1,0:T(8,128)(2,1)S(1)}, bf16[2048,128]{1,0:T(8,128)(2,1)S(1)}, u32[]{:S(2)}, u32[]{:S(2)}) %collective-permute-start.13) | collective-permute-done | bytes 524320 | tf_op jit(solution)/shard_map/ppermute | solution.py:391
  134.8 5.1 %collective-permute-done.18 = f32[64,128]{1,0:T(8,128)S(1)} collective-permute-done((f32[64,128]{1,0:T(8,128)S(1)}, f32[64,128]{1,0:T(8,128)S(1)}, u32[]{:S(2)}, u32[]{:S(2)}) %collective-permute-start.18) | collective-permute-done | bytes 32800 | tf_op jit(solution)/shard_map/ppermute | solution.py:391
  (82 shorter events, 39.1 us)
Async XLA Ops:
  0.6 3.7 %copy-start.1 = (bf16[128,8192]{1,0:T(8,128)(2,1)S(1)}, bf16[128,8192]{1,0:T(8,128)(2,1)}, u32[]{:S(2)}) copy-start(bf16[128,8192]{1,0:T(8,128)(2,1)} %refs_1_.43) | copy-start | bytes 6291460
  0.6 3.7 %copy-start = (bf16[1,128,8192]{2,1,0:T(8,128)(2,1)S(1)}, bf16[1,128,8192]{2,1,0:T(8,128)(2,1)}, u32[]{:S(2)}) copy-start(bf16[1,128,8192]{2,1,0:T(8,128)(2,1)} %param.7) | copy-start | bytes 6291460
  0.7 2.3 %copy-start.2 = (bf16[1,2,64,128,128]{4,3,2,1,0:T(8,128)(2,1)S(1)}, bf16[1,2,64,128,128]{4,3,2,1,0:T(8,128)(2,1)}, u32[]{:S(2)}) copy-start(bf16[1,2,64,128,128]{4,3,2,1,0:T(8,128)(2,1)} %param.8) | copy-start | bytes 12582916
  4.3 7.4 %copy-start.6 = (s32[64]{0:T(128)S(1)}, s32[64]{0:T(128)}, u32[]{:S(2)}) copy-start(s32[64]{0:T(128)} %refs_0_.27) | copy-start | bytes 772
  11.7 2.6 %copy-start.4 = (bf16[1,2,64,128,128]{4,3,2,1,0:T(8,128)(2,1)S(1)}, bf16[1,2,64,128,128]{4,3,2,1,0:T(8,128)(2,1)}, u32[]{:S(2)}) copy-start(bf16[1,2,64,128,128]{4,3,2,1,0:T(8,128)(2,1)} %param.8) | copy-start | bytes 12582916
  12.3 10.1 %collective-permute-start.1 = (bf16[16,8192]{1,0:T(8,128)(2,1)S(1)}, bf16[16,8192]{1,0:T(8,128)(2,1)S(1)}, u32[]{:S(2)}, u32[]{:S(2)}) collective-permute-start(bf16[16,8192]{1,0:T(8,128)(2,1)S(1)} %get-tuple-element.115), channel_id=1, source_target_pairs={{8,0},{16,8},{24,16},{9,1},{17,9},{25,17},{10,2},{18,10},{26,18},{... | collective-permute-start | bytes 786440 | tf_op jit(solution)/shard_map/ppermute | solution.py:441
  20.1 9.9 %collective-permute-start = (bf16[16,8192]{1,0:T(8,128)(2,1)S(1)}, bf16[16,8192]{1,0:T(8,128)(2,1)S(1)}, u32[]{:S(2)}, u32[]{:S(2)}) collective-permute-start(bf16[16,8192]{1,0:T(8,128)(2,1)S(1)} %get-tuple-element.114), channel_id=1, source_target_pairs={{8,0},{16,8},{24,16},{9,1},{17,9},{25,17},{10,2},{18,10},{26,18},{... | collective-permute-start | bytes 786440 | tf_op jit(solution)/shard_map/ppermute | solution.py:441
  26.1 10.3 %collective-permute-start.3 = (bf16[16,8192]{1,0:T(8,128)(2,1)S(1)}, bf16[16,8192]{1,0:T(8,128)(2,1)S(1)}, u32[]{:S(2)}, u32[]{:S(2)}) collective-permute-start(bf16[16,8192]{1,0:T(8,128)(2,1)S(1)} %get-tuple-element.121), channel_id=1, source_target_pairs={{8,0},{16,8},{24,16},{9,1},{17,9},{25,17},{10,2},{18,10},{26,18},{... | collective-permute-start | bytes 786440 | tf_op jit(solution)/shard_map/ppermute | solution.py:441
  33.7 9.9 %collective-permute-start.2 = (bf16[16,8192]{1,0:T(8,128)(2,1)S(1)}, bf16[16,8192]{1,0:T(8,128)(2,1)S(1)}, u32[]{:S(2)}, u32[]{:S(2)}) collective-permute-start(bf16[16,8192]{1,0:T(8,128)(2,1)S(1)} %get-tuple-element.120), channel_id=1, source_target_pairs={{8,0},{16,8},{24,16},{9,1},{17,9},{25,17},{10,2},{18,10},{26,18},{... | collective-permute-start | bytes 786440 | tf_op jit(solution)/shard_map/ppermute | solution.py:441
  40.3 9.1 %collective-permute-start.5 = (bf16[16,8192]{1,0:T(8,128)(2,1)S(1)}, bf16[16,8192]{1,0:T(8,128)(2,1)S(1)}, u32[]{:S(2)}, u32[]{:S(2)}) collective-permute-start(bf16[16,8192]{1,0:T(8,128)(2,1)S(1)} %get-tuple-element.129), channel_id=1, source_target_pairs={{8,0},{16,8},{24,16},{9,1},{17,9},{25,17},{10,2},{18,10},{26,18},{... | collective-permute-start | bytes 786440 | tf_op jit(solution)/shard_map/ppermute | solution.py:441
  47.4 9.3 %collective-permute-start.4 = (bf16[16,8192]{1,0:T(8,128)(2,1)S(1)}, bf16[16,8192]{1,0:T(8,128)(2,1)S(1)}, u32[]{:S(2)}, u32[]{:S(2)}) collective-permute-start(bf16[16,8192]{1,0:T(8,128)(2,1)S(1)} %get-tuple-element.126), channel_id=1, source_target_pairs={{8,0},{16,8},{24,16},{9,1},{17,9},{25,17},{10,2},{18,10},{26,18},{... | collective-permute-start | bytes 786440 | tf_op jit(solution)/shard_map/ppermute | solution.py:441
  53.1 9.7 %collective-permute-start.7 = (bf16[16,8192]{1,0:T(8,128)(2,1)S(1)}, bf16[16,8192]{1,0:T(8,128)(2,1)S(1)}, u32[]{:S(2)}, u32[]{:S(2)}) collective-permute-start(bf16[16,8192]{1,0:T(8,128)(2,1)S(1)} %get-tuple-element.135), channel_id=1, source_target_pairs={{8,0},{16,8},{24,16},{9,1},{17,9},{25,17},{10,2},{18,10},{26,18},{... | collective-permute-start | bytes 786440 | tf_op jit(solution)/shard_map/ppermute | solution.py:441
  60.5 8.8 %collective-permute-start.6 = (bf16[16,8192]{1,0:T(8,128)(2,1)S(1)}, bf16[16,8192]{1,0:T(8,128)(2,1)S(1)}, u32[]{:S(2)}, u32[]{:S(2)}) collective-permute-start(bf16[16,8192]{1,0:T(8,128)(2,1)S(1)} %get-tuple-element.134), channel_id=1, source_target_pairs={{8,0},{16,8},{24,16},{9,1},{17,9},{25,17},{10,2},{18,10},{26,18},{... | collective-permute-start | bytes 786440 | tf_op jit(solution)/shard_map/ppermute | solution.py:441
  66.6 8.5 %collective-permute-start.9 = (bf16[16,8192]{1,0:T(8,128)(2,1)S(1)}, bf16[16,8192]{1,0:T(8,128)(2,1)S(1)}, u32[]{:S(2)}, u32[]{:S(2)}) collective-permute-start(bf16[16,8192]{1,0:T(8,128)(2,1)S(1)} %get-tuple-element.141), channel_id=1, source_target_pairs={{8,0},{16,8},{24,16},{9,1},{17,9},{25,17},{10,2},{18,10},{26,18},{... | collective-permute-start | bytes 786440 | tf_op jit(solution)/shard_map/ppermute | solution.py:441
  73.0 11.0 %collective-permute-start.8 = (bf16[16,8192]{1,0:T(8,128)(2,1)S(1)}, bf16[16,8192]{1,0:T(8,128)(2,1)S(1)}, u32[]{:S(2)}, u32[]{:S(2)}) collective-permute-start(bf16[16,8192]{1,0:T(8,128)(2,1)S(1)} %get-tuple-element.140), channel_id=1, source_target_pairs={{8,0},{16,8},{24,16},{9,1},{17,9},{25,17},{10,2},{18,10},{26,18},{... | collective-permute-start | bytes 786440 | tf_op jit(solution)/shard_map/ppermute | solution.py:441
  75.7 27.2 %collective-permute-start.11 = (bf16[16,8192]{1,0:T(8,128)(2,1)S(1)}, bf16[16,8192]{1,0:T(8,128)(2,1)S(1)}, u32[]{:S(2)}, u32[]{:S(2)}) collective-permute-start(bf16[16,8192]{1,0:T(8,128)(2,1)S(1)} %get-tuple-element.147), channel_id=1, source_target_pairs={{8,0},{16,8},{24,16},{9,1},{17,9},{25,17},{10,2},{18,10},{26,18},{... | collective-permute-start | bytes 786440 | tf_op jit(solution)/shard_map/ppermute | solution.py:441
  84.8 19.4 %collective-permute-start.10 = (bf16[16,8192]{1,0:T(8,128)(2,1)S(1)}, bf16[16,8192]{1,0:T(8,128)(2,1)S(1)}, u32[]{:S(2)}, u32[]{:S(2)}) collective-permute-start(bf16[16,8192]{1,0:T(8,128)(2,1)S(1)} %get-tuple-element.146), channel_id=1, source_target_pairs={{8,0},{16,8},{24,16},{9,1},{17,9},{25,17},{10,2},{18,10},{26,18},{... | collective-permute-start | bytes 786440 | tf_op jit(solution)/shard_map/ppermute | solution.py:441
  111.5 4.2 %collective-permute-start.12 = (bf16[8256,128]{1,0:T(8,128)(2,1)S(1)}, bf16[8256,128]{1,0:T(8,128)(2,1)S(1)}, u32[]{:S(2)}, u32[]{:S(2)}) collective-permute-start(bf16[8256,128]{1,0:T(8,128)(2,1)S(1)} %get-tuple-element.156), channel_id=1, source_target_pairs={{0,1},{1,0},{2,3},{3,2},{4,5},{5,4},{6,7},{7,6},{8,9},{9,8},{10,11... | collective-permute-start | bytes 6340616 | tf_op jit(solution)/shard_map/ppermute | solution.py:391
  116.5 14.4 %collective-permute-start.13 = (bf16[2048,128]{1,0:T(8,128)(2,1)S(1)}, bf16[2048,128]{1,0:T(8,128)(2,1)S(1)}, u32[]{:S(2)}, u32[]{:S(2)}) collective-permute-start(bf16[2048,128]{1,0:T(8,128)(2,1)S(1)} %get-tuple-element.161), channel_id=1, source_target_pairs={{0,2},{1,3},{2,0},{3,1},{4,6},{5,7},{6,4},{7,5},{8,10},{9,11},{10,... | collective-permute-start | bytes 1572872 | tf_op jit(solution)/shard_map/ppermute | solution.py:391
  118.0 13.7 %collective-permute-start.15 = (bf16[2048,128]{1,0:T(8,128)(2,1)S(1)}, bf16[2048,128]{1,0:T(8,128)(2,1)S(1)}, u32[]{:S(2)}, u32[]{:S(2)}) collective-permute-start(bf16[2048,128]{1,0:T(8,128)(2,1)S(1)} %get-tuple-element.162), channel_id=1, source_target_pairs={{0,4},{1,5},{2,6},{3,7},{4,0},{5,1},{6,2},{7,3},{8,12},{9,13},{10,... | collective-permute-start | bytes 1572872 | tf_op jit(solution)/shard_map/ppermute | solution.py:391
  119.5 14.0 %collective-permute-start.17 = (f32[64,128]{1,0:T(8,128)S(1)}, f32[64,128]{1,0:T(8,128)S(1)}, u32[]{:S(2)}, u32[]{:S(2)}) collective-permute-start(f32[64,128]{1,0:T(8,128)S(1)} %slice.59), channel_id=1, source_target_pairs={{0,2},{1,3},{2,0},{3,1},{4,6},{5,7},{6,4},{7,5},{8,10},{9,11},{10,... | collective-permute-start | bytes 98312 | tf_op jit(solution)/shard_map/ppermute | solution.py:391
  131.9 8.6 %collective-permute-start.14 = (bf16[1024,128]{1,0:T(8,128)(2,1)S(1)}, bf16[1024,128]{1,0:T(8,128)(2,1)S(1)}, u32[]{:S(2)}, u32[]{:S(2)}) collective-permute-start(bf16[1024,128]{1,0:T(8,128)(2,1)S(1)} %slice.68), channel_id=1, source_target_pairs={{0,4},{1,5},{2,6},{3,7},{4,0},{5,1},{6,2},{7,3},{8,12},{9,13},{10,... | collective-permute-start | bytes 786440 | tf_op jit(solution)/shard_map/ppermute | solution.py:391
  133.5 6.4 %collective-permute-start.18 = (f32[64,128]{1,0:T(8,128)S(1)}, f32[64,128]{1,0:T(8,128)S(1)}, u32[]{:S(2)}, u32[]{:S(2)}) collective-permute-start(f32[64,128]{1,0:T(8,128)S(1)} %slice_add_fusion.4), channel_id=1, source_target_pairs={{0,4},{1,5},{2,6},{3,7},{4,0},{5,1},{6,2},{7,3},{8,12},{9,13},{10,... | collective-permute-start | bytes 98312 | tf_op jit(solution)/shard_map/ppermute | solution.py:391
  134.1 6.7 %collective-permute-start.16 = (bf16[1024,128]{1,0:T(8,128)(2,1)S(1)}, bf16[1024,128]{1,0:T(8,128)(2,1)S(1)}, u32[]{:S(2)}, u32[]{:S(2)}) collective-permute-start(bf16[1024,128]{1,0:T(8,128)(2,1)S(1)} %slice.67), channel_id=1, source_target_pairs={{0,2},{1,3},{2,0},{3,1},{4,6},{5,7},{6,4},{7,5},{8,10},{9,11},{10,... | collective-permute-start | bytes 786440 | tf_op jit(solution)/shard_map/ppermute | solution.py:391
  (4 other events, 6.1 us)

commit v2 on v1

v2 whole, which is shorter than its diff:
```python
import functools
import math

import jax
import jax.numpy as jnp
from jax import lax
from jax.experimental import pallas as pl
from jax.experimental.pallas import tpu as pltpu
from jax.sharding import PartitionSpec as P

F = 64
B = 128
EPS = 1e-05
CHUNKS = 8
LAG = 2
AHEAD = 1
PREPARE_LIMIT = 46 << 20
ANY = pl.BlockSpec(memory_space=pl.ANY)
VMEM = pl.BlockSpec(memory_space=pltpu.VMEM)
HBM = pl.BlockSpec(memory_space=pltpu.HBM)
SMEM = pl.BlockSpec(memory_space=pltpu.SMEM)
TN = (((0,), (0,)), ((), ()))
LIMIT = 16 << 20


def dot(a, b):
    return jnp.dot(a, b, preferred_element_type=jnp.float32)


def dot_tn(a, b):
    return lax.dot_general(a, b, TN, preferred_element_type=jnp.float32)


def col(j):
    if isinstance(j, int):
        return pl.ds(j * B, B)
    return pl.ds(pl.multiple_of(j * B, B), B)


def exchange(parts, lane_bit):
    lane = lax.broadcasted_iota(jnp.int32, parts[0].shape, 1)
    parts = list(parts)
    for i in range(3):
        shift = 1 << (lane_bit + i)
        upper = (lane & shift) != 0
        for low in range(8):
            if low & (1 << i):
                continue
            high = low | (1 << i)
            a, b = parts[low], parts[high]
            parts[low] = jnp.where(upper, pltpu.roll(b, shift, 1), a)
            parts[high] = jnp.where(upper, b, pltpu.roll(a, B - shift, 1))
    return parts


def gelu_pair(v):
    cdf = 0.5 * (1.0 + lax.erf(v * 0.7071067811865476))
    density = jnp.exp(-0.5 * v * v) * 0.3989422804014327
    return v * cdf, cdf + v * density


def matrix(rule):
    row = lax.broadcasted_iota(jnp.int32, (B, B), 0)
    column = lax.broadcasted_iota(jnp.int32, (B, B), 1)
    return rule(row, column).astype(jnp.float32).astype(jnp.bfloat16)


def prepare_kernel(order_ref, w_ref, raw_ref, w1_ref, w0_ref, w_buf, sem):
    half = B // 2
    part = F // 4
    spans = [pl.ds(k * part, part) for k in range(4)]
    seconds = [pltpu.make_async_copy(w_ref.at[1, at], w_buf.at[at], sem.at[k]) for k, at in enumerate(spans)]
    firsts = [pltpu.make_async_copy(w_ref.at[0, at], raw_ref.at[at], sem.at[4 + k]) for k, at in enumerate(spans)]
    for copy in seconds + firsts:
        copy.start()
    mixed = matrix(lambda r, c: c == 2 * (r % half) + r // half)
    eye = matrix(lambda r, c: c == r)
    for k in range(4):
        seconds[k].wait()
        for j in range(k * part, (k + 1) * part):
            w1_ref[order_ref[j]] = dot_tn(w_buf[j], mixed).astype(jnp.bfloat16)
    for k in range(4):
        firsts[k].wait()
        for j in range(k * part, (k + 1) * part):
            w0_ref[j] = dot_tn(raw_ref[j], eye).astype(jnp.bfloat16)


def prepare(order, weights):
    bf = jnp.bfloat16
    factor = jax.ShapeDtypeStruct((F, B, B), bf)
    return pl.pallas_call(
        prepare_kernel,
        out_shape=(factor, factor, factor),
        in_specs=[SMEM, HBM],
        out_specs=(VMEM,) * 3,
        scratch_shapes=[pltpu.VMEM((F, B, B), bf), pltpu.SemaphoreType.DMA((8,))],
        compiler_params=pltpu.CompilerParams(vmem_limit_bytes=PREPARE_LIMIT),
        name="prepare",
    )(order, weights)


def shuffle_kernel(order_ref, cot_ref, out_ref):
    @pl.loop(0, F, unroll=4)
    def _(j):
        out_ref[:, col(order_ref[j])] = cot_ref[:, col(j)]


def shuffle(order, cotangent):
    return pl.pallas_call(
        shuffle_kernel,
        out_shape=jax.ShapeDtypeStruct(cotangent.shape, cotangent.dtype),
        in_specs=[SMEM, VMEM],
        out_specs=VMEM,
        compiler_params=pltpu.CompilerParams(vmem_limit_bytes=LIMIT),
        name="shuffle",
    )(order, cotangent)


def span(plan, step, ahead=0):
    position = lax.axis_index("segment")
    first = last = 0
    for p, pieces in enumerate(plan):
        first = jnp.where(position == p, sum(pieces[:step]), first)
        last = jnp.where(position == p, sum(pieces[: step + 1]), last)
    if ahead:
        total = sum(plan[-1])
        more = jnp.where(jnp.logical_and(position == len(plan) - 1, lax.axis_index("dp") % 2 == 1), ahead, 0)
        first = jnp.minimum(first + (more if step else 0), total)
        last = jnp.minimum(last + more, total)
    return first, last


def plans(segments):
    steps = CHUNKS + LAG * (segments - 1)
    forward_plan, mix_plan = [], []
    for p in range(segments):
        begin = LAG * (segments - 1 - p)
        ahead, blend = [0] * steps, [0] * steps
        if begin == 0:
            ahead[:CHUNKS] = [1] * CHUNKS
        elif begin < 4:
            ahead[:4] = [3, 3, 1, 1]
        else:
            ahead[:3] = [3, 3, 2]
        if begin >= 6:
            blend[3:5] = [2, 2]
        else:
            blend[steps - LAG - 1] = CHUNKS // 2
        forward_plan.append(ahead)
        mix_plan.append(blend)
    return forward_plan, mix_plan


def forward_kernel(step, plan, first, *refs):
    x_ref, gain_ref, w_ref = refs[:3]
    inv_ref, left_ref, z_ref, slope_ref, xh_ref, pre_buf = refs[3:] if first else refs[8:]
    rows = pre_buf.shape[0]

    @pl.loop(*span(plan, step, AHEAD))
    def _(chunk):
        at_rows = pl.ds(pl.multiple_of(chunk * rows, rows), rows)

        def square(j, total):
            v = x_ref[at_rows, col(j)].astype(jnp.float32)
            return total + v * v

        total = lax.fori_loop(0, F, square, jnp.zeros((rows, B), jnp.float32), unroll=16)
        mean = jnp.sum(total, axis=1, keepdims=True) * (1.0 / (F * B))
        inv = jnp.broadcast_to(lax.rsqrt(mean + EPS), (rows, B))
        inv_ref[at_rows, :] = inv

        @pl.loop(0, F, unroll=32)
        def _(j):
            xh = x_ref[at_rows, col(j)].astype(jnp.float32) * inv
            xh_ref[at_rows, col(j)] = xh
            h = (xh * gain_ref[:, col(j)]).astype(jnp.bfloat16)
            left_ref[at_rows, col(j)] = h
            pre_buf[:, col(j)] = dot(h, w_ref[j])

        @pl.loop(0, F, unroll=8)
        def _(j):
            z, slope = gelu_pair(pre_buf[:, col(j)])
            slope_ref[at_rows, col(j)] = slope
            z_ref[at_rows, col(j)] = z.astype(jnp.bfloat16)


def forward(step, plan, x, gain, w0, carried):
    n = x.shape[0]
    wide = F * B
    first = carried is None
    return pl.pallas_call(
        functools.partial(forward_kernel, step, plan, first),
        out_shape=(
            jax.ShapeDtypeStruct((n, B), jnp.float32),
            jax.ShapeDtypeStruct((n, 2 * wide), jnp.bfloat16),
            jax.ShapeDtypeStruct((n, wide), jnp.bfloat16),
            jax.ShapeDtypeStruct((n, wide), jnp.float32),
            jax.ShapeDtypeStruct((n, wide), jnp.float32),
        ),
        in_specs=[VMEM] * (3 if first else 8),
        out_specs=(VMEM,) * 5,
        scratch_shapes=[pltpu.VMEM((n // CHUNKS, wide), jnp.float32)],
        input_output_aliases={} if first else {3: 0, 4: 1, 5: 2, 6: 3, 7: 4},
        compiler_params=pltpu.CompilerParams(vmem_limit_bytes=LIMIT),
        cost_estimate=pl.CostEstimate(flops=1 << 20, bytes_accessed=4 << 20, transcendentals=0),
        name="forward",
    )(x, gain, w0, *(() if first else carried))


def mix_kernel(step, plan, z_ref, old_ref, left_ref, low_buf, mid_buf):
    rows = low_buf.shape[1]
    half = B // 2
    apart = matrix(lambda r, c: c == r // 2 + half * (r % 2))

    @pl.loop(*span(plan, step))
    def _(pair):
        at_rows = pl.ds(pl.multiple_of(pair * rows, rows), rows)

        @pl.loop(0, F, unroll=32)
        def _(j):
            low_buf[j] = dot(z_ref[at_rows, col(j)], apart).astype(jnp.bfloat16)

        @pl.loop(0, 8, unroll=4)
        def _(k):
            parts = exchange([low_buf[8 * k + i] for i in range(8)], 0)
            for i in range(8):
                mid_buf[8 * i + k] = parts[i]

        @pl.loop(0, 8, unroll=4)
        def _(low):
            parts = exchange([mid_buf[8 * low + g] for g in range(8)], 3)
            for g in range(8):
                left_ref[at_rows, col(F + 8 * g + low)] = parts[g]


def mix(step, plan, z, left):
    n = z.shape[0]
    return pl.pallas_call(
        functools.partial(mix_kernel, step, plan),
        out_shape=jax.ShapeDtypeStruct((n, 2 * F * B), jnp.bfloat16),
        in_specs=[VMEM] * 2,
        out_specs=VMEM,
        scratch_shapes=[pltpu.VMEM((F, 2 * n // CHUNKS, B), jnp.bfloat16)] * 2,
        input_output_aliases={1: 0},
        compiler_params=pltpu.CompilerParams(vmem_limit_bytes=LIMIT),
        cost_estimate=pl.CostEstimate(flops=1 << 20, bytes_accessed=4 << 20, transcendentals=0),
        name="mix",
    )(z, left)


def stage_kernel(step, segments, first, *refs):
    (order_ref, cot_ref, inc_ref, xh_ref, inv_ref, slope_ref, gain_ref, w1_ref, w0_ref) = refs[:9]
    refs = refs[10:] if first else refs[12:]
    (send_ref, right_ref, part_ref, g_buf, mid_buf, gh_buf, order_buf, sem) = refs
    rows = g_buf.shape[0]
    wide = F * B
    position = lax.axis_index("segment")
    chunk = step - LAG * (segments - 1 - position)
    top = position == segments - 1
    if first:
        part_ref[...] = jnp.zeros_like(part_ref)

    @pl.when(jnp.logical_and(chunk >= 0, chunk < CHUNKS))
    def _():
        at_rows = pl.ds(pl.multiple_of(chunk * rows, rows), rows)
        order_copy = pltpu.make_async_copy(order_ref, order_buf, sem)
        order_copy.start()

        @pl.when(top)
        def _():
            g_buf[...] = cot_ref[at_rows, :]

        @pl.when(jnp.logical_not(top))
        def _():
            g_buf[...] = inc_ref[...]

        for k in range(8):
            parts = [dot(g_buf[:, col(8 * k + i)], w1_ref[8 * k + i]).astype(jnp.bfloat16) for i in range(8)]
            parts = exchange(parts, 1)
            for i in range(8):
                mid_buf[8 * i + k] = parts[i]
                right_ref[at_rows, col(F + 8 * k + i)] = g_buf[:, col(8 * k + i)]

        inner = jnp.zeros((rows, B), jnp.float32)
        for low in range(8):
            parts = exchange([mid_buf[8 * low + g] for g in range(8)], 4)
            for g in range(8):
                at = col(8 * g + low)
                gp = (parts[g].astype(jnp.float32) * slope_ref[at_rows, at]).astype(jnp.bfloat16)
                right_ref[at_rows, at] = gp
                gh = dot(gp, w0_ref[8 * g + low])
                gh_buf[:, at] = gh
                term = gh * xh_ref[at_rows, at]
                part = term[:8]
                for t in range(8, rows, 8):
                    part = part + term[t : t + 8]
                part_ref[:, at] = part_ref[:, at] + part
                inner = inner + term * gain_ref[:, at]

        inner = jnp.sum(inner, axis=1, keepdims=True) * (1.0 / (F * B))
        inv = inv_ref[at_rows, :]
        inner = inner * inv
        order_copy.wait()

        @pl.loop(0, F, unroll=8)
        def _(j):
            at = col(j)
            to = col(order_buf[j])
            value = g_buf[:, to].astype(jnp.float32) + (inv * gain_ref[:, at]) * gh_buf[:, at] - xh_ref[at_rows, at] * inner
            value = value.astype(jnp.bfloat16)
            send_ref[:, to] = value
            right_ref[at_rows, col(2 * F + j)] = value


def stage(step, segments, order, cot, inc, xh, inv, slope, gain, w1, w0, left, carried):
    n = xh.shape[0]
    rows = n // CHUNKS
    wide = F * B
    bf, f32 = jnp.bfloat16, jnp.float32
    first = carried is None
    args = [order, cot, inc, xh, inv, slope, gain, w1, w0, left] + ([] if first else list(carried))
    return pl.pallas_call(
        functools.partial(stage_kernel, step, segments, first),
        out_shape=(
            jax.ShapeDtypeStruct((rows, wide), bf),
            jax.ShapeDtypeStruct((n, 3 * wide), bf),
            jax.ShapeDtypeStruct((8, wide), f32),
        ),
        in_specs=[ANY] + [VMEM] * (9 if first else 11),
        out_specs=(VMEM,) * 3,
        scratch_shapes=[
            pltpu.VMEM((rows, wide), bf),
            pltpu.VMEM((F, rows, B), bf),
            pltpu.VMEM((rows, wide), f32),
            pltpu.SMEM((F,), jnp.int32),
            pltpu.SemaphoreType.DMA,
        ],
        input_output_aliases={} if first else {10: 1, 11: 2},
        compiler_params=pltpu.CompilerParams(vmem_limit_bytes=LIMIT),
        cost_estimate=pl.CostEstimate(flops=4 * rows * wide * B, bytes_accessed=6 << 20, transcendentals=0),
        name="stage",
    )(*args)


def product(scale, blocks, p, table_ref, perm_ref, column_ref, left_ref, right_ref):
    which = table_ref[perm_ref[p] ^ (lax.axis_index("dp") * blocks)]
    at = col(column_ref[which])
    return dot_tn(left_ref[:, at], right_ref[:, at]) * scale


def gain_row(part_ref, scale, j):
    return jnp.sum(part_ref[:, j * B : (j + 1) * B], axis=0, keepdims=True) * scale


def sent_kernel(scale, blocks, table_ref, perm_ref, column_ref, left_ref, right_ref, part_ref, send_ref, gain_ref):
    for j in range(F):
        gain_ref[j : j + 1, :] = gain_row(part_ref, scale, j)
    send_ref[F * B :, :] = gain_ref[...].astype(jnp.bfloat16)

    @pl.loop(0, F, unroll=8)
    def _(p):
        value = product(scale, blocks, p, table_ref, perm_ref, column_ref, left_ref, right_ref)
        send_ref[pl.ds(pl.multiple_of(p * B, B), B), :] = value.astype(jnp.bfloat16)


def kept_kernel(scale, blocks, table_ref, perm_ref, column_ref, left_ref, right_ref, keep_ref, grad_ref, sem):
    out = pltpu.make_async_copy(right_ref.at[:, pl.ds(2 * F * B, F * B)], grad_ref, sem)
    out.start()

    @pl.loop(0, F, unroll=8)
    def _(p):
        value = product(scale, blocks, F + p, table_ref, perm_ref, column_ref, left_ref, right_ref)
        keep_ref[pl.ds(pl.multiple_of(p * B, B), B), :] = value

    out.wait()


def grads(scale, blocks, table, perm, column, left, right, part):
    n = left.shape[0]
    params = pltpu.CompilerParams(vmem_limit_bytes=LIMIT)
    f32 = jnp.float32
    cost = pl.CostEstimate(flops=2 * n * B * B * F, bytes_accessed=8 << 20, transcendentals=0)
    send, gain = pl.pallas_call(
        functools.partial(sent_kernel, scale, blocks),
        out_shape=(jax.ShapeDtypeStruct((F * B + F, B), jnp.bfloat16), jax.ShapeDtypeStruct((F, B), f32)),
        in_specs=[SMEM] * 3 + [VMEM] * 3,
        out_specs=(VMEM, VMEM),
        compiler_params=params,
        cost_estimate=cost,
        name="sent",
    )(table, perm, column, left, right, part)
    got = swap(send, 0)
    keep, input_gradient = pl.pallas_call(
        functools.partial(kept_kernel, scale, blocks),
        out_shape=(jax.ShapeDtypeStruct((F * B, B), f32), jax.ShapeDtypeStruct((n, F * B), jnp.bfloat16)),
        in_specs=[SMEM] * 3 + [VMEM] * 2,
        out_specs=(VMEM, ANY),
        scratch_shapes=[pltpu.SemaphoreType.DMA],
        compiler_params=params,
        cost_estimate=cost,
        name="kept",
    )(table, perm, column, left, right)
    return got, gain, keep, input_gradient


def split_kernel(sizes, offsets, *refs):
    count = len(sizes)
    keeps, gots, gain_ref = refs[:count], refs[count : 2 * count], refs[2 * count]
    sends, rest, total_ref = refs[2 * count + 1 : 3 * count + 1], refs[3 * count + 1 : 4 * count + 1], refs[4 * count + 1]
    f32 = jnp.float32
    for side in range(count):
        half = sizes[side] // 2
        for begin, target in ((0, sends[side]), (half, rest[side])):

            def body(k, side=side, begin=begin, target=target):
                piece = math.gcd(half, 256)
                at = pl.ds(pl.multiple_of(begin + k * piece + offsets[side], piece), piece)
                to = pl.ds(pl.multiple_of(k * piece, piece), piece)
                target[to, :] = (keeps[side][at, :] + gots[side][at, :].astype(f32)).astype(target.dtype)

            pl.loop(0, half // math.gcd(half, 256))(body)
    tail = gots[0].shape[0] - F
    total = gain_ref[...] + gots[0][tail:, :].astype(f32)
    total_ref[...] = total
    sends[0][sizes[0] // 2 :, :] = total.astype(jnp.bfloat16)


def split(sizes, offsets, keeps, gots, gain):
    f32 = jnp.float32
    halves = [size // 2 for size in sizes]
    outs = [jax.ShapeDtypeStruct((half + (F if side == 0 else 0), B), jnp.bfloat16) for side, half in enumerate(halves)]
    outs += [jax.ShapeDtypeStruct((half, B), f32) for half in halves] + [jax.ShapeDtypeStruct((F, B), f32)]
    got = pl.pallas_call(
        functools.partial(split_kernel, sizes, offsets),
        out_shape=tuple(outs),
        in_specs=[VMEM] * (2 * len(sizes) + 1),
        out_specs=(VMEM,) * len(outs),
        compiler_params=pltpu.CompilerParams(vmem_limit_bytes=LIMIT),
        name="split",
    )(*keeps, *gots, gain)
    count = len(sizes)
    return got[:count], got[count : 2 * count], got[-1]


def last_kernel(sizes, offsets, dp, *refs):
    count = len(sizes)
    keeps, gots, gain_ref = refs[:count], refs[count : 2 * count], refs[2 * count]
    out_ref, own_ref, gain_buf = refs[2 * count + 1 :]
    f32 = jnp.float32
    start = 0
    for side in range(count):
        piece = math.gcd(sizes[side], 256)

        @pl.loop(0, sizes[side] // piece)
        def _(k):
            at = pl.ds(pl.multiple_of(k * piece + offsets[side], piece), piece)
            to = pl.ds(pl.multiple_of(k * piece + start, piece), piece)
            out_ref[to, :] = keeps[side][at, :] + gots[side][at, :].astype(f32)

        start += sizes[side]
    tail = gots[0].shape[0] - F
    gain_buf[...] = gain_ref[...] + gots[0][tail:, :].astype(f32)
    each = F // dp
    me = lax.axis_index("dp")
    for r in range(each):
        own_ref[:, r * B : (r + 1) * B] = gain_buf[pl.ds(me * each + r, 1), :]


def last(sizes, offsets, dp, keeps, gots, gain):
    f32 = jnp.float32
    return pl.pallas_call(
        functools.partial(last_kernel, sizes, offsets, dp),
        out_shape=(jax.ShapeDtypeStruct((sum(sizes), B), f32), jax.ShapeDtypeStruct((1, F * B // dp), f32)),
        in_specs=[VMEM] * (2 * len(sizes) + 1),
        out_specs=(VMEM, VMEM),
        scratch_shapes=[pltpu.VMEM((F, B), f32)],
        compiler_params=pltpu.CompilerParams(vmem_limit_bytes=LIMIT),
        name="last",
    )(*keeps, *gots, gain)


def order_of(bits, low_first):
    def place(q):
        digits = [(q >> k) & 1 for k in range(bits)]
        if not low_first:
            digits = digits[::-1]
        return [1 - d for d in digits]

    return sorted(range(1 << bits), key=place)


def swap(array, bit):
    size = lax.axis_size("dp")
    return lax.ppermute(array, "dp", [(i, i ^ (1 << bit)) for i in range(size)])


def reduce_owners(got, gain, keep, dp, blocks):
    bits = dp.bit_length() - 2
    cut = (dp // 2) * max(blocks // 2, 1) * B
    sizes, offsets = [cut, F * B - cut], [0, cut]
    keeps, gots = [keep, keep], [got, got]
    for index in range(bits):
        sends, keeps, gain = split(sizes, offsets, keeps, gots, gain)
        gots = [swap(sends[0], index + 1), swap(sends[1], bits - index)]
        sizes, offsets = [size // 2 for size in sizes], [0, 0]
    return last(sizes, offsets, dp, keeps, gots, gain)


def local(acts, weights, gains, cotangent, block_order, owner_table):
    x = acts[0]
    n = x.shape[0]
    segments = lax.axis_size("segment")
    dp = lax.axis_size("dp")
    blocks = 2 * F // dp
    scale = 1.0 / math.sqrt(n * dp)
    rows = n // CHUNKS
    steps = CHUNKS + LAG * (segments - 1)
    pairs = [(i, i - 1) for i in range(1, segments)]
    raw, w1, w0 = prepare(block_order, weights[0])
    cot = shuffle(block_order, cotangent)
    forward_plan, mix_plan = plans(segments)
    sent, carried, ahead = [], None, None
    for step in range(steps):
        if any(plan[step] for plan in forward_plan):
            ahead = forward(step, forward_plan, x, gains, raw, ahead)
        inv, left, z, slope, xh = ahead
        inc = sent[step - LAG] if step >= LAG else cot[:rows]
        out = stage(step, segments, block_order, cot, inc, xh, inv, slope, gains, w1, w0, left, carried)
        carried = out[1:]
        if step < steps - LAG:
            sent.append(lax.ppermute(out[0], "segment", pairs))
        if any(plan[step] for plan in mix_plan):
            ahead = (inv, mix(step, mix_plan, z, left), z, slope, xh)
    left = ahead[1]
    right, part = carried

    bits = dp.bit_length() - 2
    first = max(blocks // 2, 1)
    places = [(2 * q) * blocks + i for q in order_of(bits, True) for i in range(first)]
    places += [(2 * q) * blocks + i for q in order_of(bits, False) for i in range(first, blocks)]
    perm = jnp.array([p + blocks for p in places] + places, jnp.int32)
    column = jnp.concatenate([jnp.arange(F, dtype=jnp.int32), F + block_order])
    got, gain, keep, input_gradient = grads(scale, blocks, owner_table, perm, column, left, right, part)
    owned, own_gain = reduce_owners(got, gain, keep, dp, blocks)
    return input_gradient[None], owned.reshape(1, blocks, B, B), own_gain


def solution(mesh):
    return jax.shard_map(
        local,
        mesh=mesh,
        in_specs=(
            P("segment", "dp", None),
            P("segment", None, None, None, None),
            P("segment", None),
            P("dp", None),
            P(),
            P(),
        ),
        out_specs=(P("segment", "dp", None), P("segment", "dp", None, None), P("segment", "dp")),
        check_vma=False,
    )
```

time: 142 us -> 126 us (0.89)
  Pallas kernels: 67.8 us -> 56.8 us
  local copies, waits for them, and re-layouts: 5.29 us -> 0.85 us
  other arithmetic: 1.97 us -> 0.08 us
    pallas_call x14, Pallas kernels: 35 us -> 23.2 us  [stage(): pl.pallas_call(functools.partial(stage_kernel, step, segments, first), ou...]
    pallas_call x2 -> x7, Pallas kernels: 7.36 us -> 13.6 us  [the longest x1 4.49 us: prepare(): pl.pallas_call(prepare_kernel, out_shape=(factor, factor, factor), in_spe...]
    pallas_call x10 -> x3, Pallas kernels: 15 us -> 9.64 us  [mix(): pl.pallas_call(functools.partial(mix_kernel, step, plan), out_shape=jax.S...]
    unnamed x18 -> x14, local copies, waits for them, and re-layouts: 4.55 us -> 0.83 us
    ppermute x12, starting transfers between devices: 31.3 us -> 33.8 us  [local(): sent.append(lax.ppermute(out[0], 'segment', pairs))]
    ppermute x12, waiting for transfers between devices: 6.67 us -> 8.28 us  [local(): sent.append(lax.ppermute(out[0], 'segment', pairs))]
    ppermute x7 -> x5, waiting for transfers between devices: 21.1 us -> 19.6 us  [swap(): return lax.ppermute(array, 'dp', [(i, i ^ 1 << bit) for i in range(size)])]
    ppermute x7 -> x5, starting transfers between devices: 6.54 us -> 5.38 us  [swap(): return lax.ppermute(array, 'dp', [(i, i ^ 1 << bit) for i in range(size)])]
  transfers between devices with their start and end apart: 19 -> 17, of which waited for: 11 -> 12; matrix products, arithmetic and copies ran while one was open for 1% -> 0% of each run, Pallas kernels for 38% -> 33%
where the time goes in v2:
time: 126 us
  Pallas kernels  56.8 us (45%)
  starting transfers between devices  39.2 us (31%)
  waiting for transfers between devices  27.9 us (22%)
    ppermute x12, starting transfers between devices, local(): sent.append(lax.ppermute(out[0], 'segment', pairs))  33.8 us
    pallas_call x14, Pallas kernels, stage(): pl.pallas_call(functools.partial(stage_kernel, step, segments, first), ou...  23.2 us
    ppermute x5, waiting for transfers between devices, swap(): return lax.ppermute(array, 'dp', [(i, i ^ 1 << bit) for i in range(size)])  19.6 us
    pallas_call x8, Pallas kernels, forward(): pl.pallas_call(functools.partial(forward_kernel, step, plan, first), out_...  10.4 us
    pallas_call x3, Pallas kernels, mix(): pl.pallas_call(functools.partial(mix_kernel, step, plan), out_shape=jax.S...  9.64 us
    ppermute x12, waiting for transfers between devices, local(): sent.append(lax.ppermute(out[0], 'segment', pairs))  8.28 us
    ppermute x5, starting transfers between devices, swap(): return lax.ppermute(array, 'dp', [(i, i ^ 1 << bit) for i in range(size)])  5.38 us
    pallas_call x1, Pallas kernels, prepare(): pl.pallas_call(prepare_kernel, out_shape=(factor, factor, factor), in_spe...  4.49 us
  transfers between devices with their start and end apart: 17, of which 12 were waited for; matrix products, arithmetic and copies ran while one was open for 0% of the time, Pallas kernels for 33%

profile of v2, /device:TPU:16, one launch (start us, length us, event | category | flops | bytes accessed | tf_op | source)
XLA Modules:
  0.0 126.0 jit_solution(191760375946352188)
XLA Ops:
  1.5 4.5 %prepare.1 = (bf16[64,128,128]{2,1,0:T(8,128)(2,1)S(1)}, bf16[64,128,128]{2,1,0:T(8,128)(2,1)S(1)}, bf16[64,128,128]{2,1,0:T(8,128)(2,1)S(1)}) custom-call(s32[64]{0:T(128)S(1)} %copy-done.3, bf16[2,64,128,128]{3,2,1,0:T(8,128)(2,1)} %bitcast.12), custom_call_target="tpu_custom_call" | custom-call | tf_op jit(solution)/shard_map/prepare/pallas_call | solution.py:91
  7.3 3.8 %forward.8 = (f32[128,128]{1,0:T(8,128)S(1)}, bf16[128,16384]{1,0:T(8,128)(2,1)S(1)}, bf16[128,8192]{1,0:T(8,128)(2,1)S(1)}, f32[128,8192]{1,0:T(8,128)S(1)}, f32[128,8192]{1,0:T(8,128)S(1)}) custom-call(bf16[128,8192]{1,0:T(8,128)(2,1)S(1)} %bitcast.4, f32[1,8192]{1,0:T(1,128)S(1)} %copy-done.1, bf16[64,128,128]{2,1,0:T(8,128)(2,1)S(1)} %get-tuple-element.102.refs_2_), custom_call_target="tpu_custom_call" | custom-call | flops 1048576 | bytes 4194304 | tf_op jit(solution)/shard_map/forward/pallas_call | solution.py:191
  11.2 2.4 %collective-permute-start.1 = (bf16[16,8192]{1,0:T(8,128)(2,1)S(1)}, bf16[16,8192]{1,0:T(8,128)(2,1)S(1)}, u32[]{:S(2)}, u32[]{:S(2)}) collective-permute-start(bf16[16,8192]{1,0:T(8,128)(2,1)S(1)} %get-tuple-element.145), channel_id=1, source_target_pairs={{8,0},{16,8},{24,16},{9,1},{17,9},{25,17},{10,2},{18,10},{26,18},{... | collective-permute-start | bytes 786440 | tf_op jit(solution)/shard_map/ppermute | solution.py:531
  13.6 3.9 %forward.9 = (f32[128,128]{1,0:T(8,128)S(1)}, bf16[128,16384]{1,0:T(8,128)(2,1)S(1)}, bf16[128,8192]{1,0:T(8,128)(2,1)S(1)}, f32[128,8192]{1,0:T(8,128)S(1)}, f32[128,8192]{1,0:T(8,128)S(1)}) custom-call(bf16[128,8192]{1,0:T(8,128)(2,1)S(1)} %bitcast.5, ...), custom_call_target="tpu_custom_call", output_to_operand_aliasing={{0}: (3, {}), {1}: (4, {}), {2}: (5, {}), {3}: (6, {}), {4}... | custom-call | flops 1048576 | bytes 4194304 | tf_op jit(solution)/shard_map/forward/pallas_call | solution.py:191
  21.9 2.7 %stage.16 = (bf16[16,8192]{1,0:T(8,128)(2,1)S(1)}, bf16[128,24576]{1,0:T(8,128)(2,1)S(1)}, f32[8,8192]{1,0:T(8,128)S(1)}) custom-call(s32[64]{0:T(128)S(1)} %copy-done.4, bf16[128,8192]{1,0:T(8,128)(2,1)S(1)} %shuffle.1.refs_1_, bf16[16,8192]{1,0:T(8,128)(2,1)S(1)} %collective-permute-done.1.refs_2_, ...), custom_call_target="tpu_custom_call", output_to_operand_aliasing={{1}: (10, {}), {2}: (11, {})} | custom-call | flops 67108864 | bytes 6291456 | tf_op jit(solution)/shard_map/stage/pallas_call | solution.py:322
  27.9 2.7 %stage.17 = (bf16[16,8192]{1,0:T(8,128)(2,1)S(1)}, bf16[128,24576]{1,0:T(8,128)(2,1)S(1)}, f32[8,8192]{1,0:T(8,128)S(1)}) custom-call(s32[64]{0:T(128)S(1)} %copy-done.4, bf16[128,8192]{1,0:T(8,128)(2,1)S(1)} %shuffle.1.refs_1_, bf16[16,8192]{1,0:T(8,128)(2,1)S(1)} %collective-permute-done.refs_2_, ...), custom_call_target="tpu_custom_call", output_to_operand_aliasing={{1}: (10, {}), {2}: (11, {})} | custom-call | flops 67108864 | bytes 6291456 | tf_op jit(solution)/shard_map/stage/pallas_call | solution.py:322
  34.2 2.7 %stage.18 = (bf16[16,8192]{1,0:T(8,128)(2,1)S(1)}, bf16[128,24576]{1,0:T(8,128)(2,1)S(1)}, f32[8,8192]{1,0:T(8,128)S(1)}) custom-call(s32[64]{0:T(128)S(1)} %copy-done.4, bf16[128,8192]{1,0:T(8,128)(2,1)S(1)} %shuffle.1.refs_1_, bf16[16,8192]{1,0:T(8,128)(2,1)S(1)} %collective-permute-done.3.refs_2_, ...), custom_call_target="tpu_custom_call", output_to_operand_aliasing={{1}: (10, {}), {2}: (11, {})} | custom-call | flops 67108864 | bytes 6291456 | tf_op jit(solution)/shard_map/stage/pallas_call | solution.py:322
  37.0 2.2 %collective-permute-start.5 = (bf16[16,8192]{1,0:T(8,128)(2,1)S(1)}, bf16[16,8192]{1,0:T(8,128)(2,1)S(1)}, u32[]{:S(2)}, u32[]{:S(2)}) collective-permute-start(bf16[16,8192]{1,0:T(8,128)(2,1)S(1)} %get-tuple-element.160), channel_id=1, source_target_pairs={{8,0},{16,8},{24,16},{9,1},{17,9},{25,17},{10,2},{18,10},{26,18},{... | collective-permute-start | bytes 786440 | tf_op jit(solution)/shard_map/ppermute | solution.py:531
  40.2 2.7 %stage.19 = (bf16[16,8192]{1,0:T(8,128)(2,1)S(1)}, bf16[128,24576]{1,0:T(8,128)(2,1)S(1)}, f32[8,8192]{1,0:T(8,128)S(1)}) custom-call(s32[64]{0:T(128)S(1)} %copy-done.4, bf16[128,8192]{1,0:T(8,128)(2,1)S(1)} %shuffle.1.refs_1_, bf16[16,8192]{1,0:T(8,128)(2,1)S(1)} %collective-permute-done.2.refs_2_, ...), custom_call_target="tpu_custom_call", output_to_operand_aliasing={{1}: (10, {}), {2}: (11, {})} | custom-call | flops 67108864 | bytes 6291456 | tf_op jit(solution)/shard_map/stage/pallas_call | solution.py:322
  45.8 2.7 %stage.20 = (bf16[16,8192]{1,0:T(8,128)(2,1)S(1)}, bf16[128,24576]{1,0:T(8,128)(2,1)S(1)}, f32[8,8192]{1,0:T(8,128)S(1)}) custom-call(s32[64]{0:T(128)S(1)} %copy-done.4, bf16[128,8192]{1,0:T(8,128)(2,1)S(1)} %shuffle.1.refs_1_, bf16[16,8192]{1,0:T(8,128)(2,1)S(1)} %collective-permute-done.5.refs_2_, ...), custom_call_target="tpu_custom_call", output_to_operand_aliasing={{1}: (10, {}), {2}: (11, {})} | custom-call | flops 67108864 | bytes 6291456 | tf_op jit(solution)/shard_map/stage/pallas_call | solution.py:322
  48.5 2.3 %collective-permute-start.7 = (bf16[16,8192]{1,0:T(8,128)(2,1)S(1)}, bf16[16,8192]{1,0:T(8,128)(2,1)S(1)}, u32[]{:S(2)}, u32[]{:S(2)}) collective-permute-start(bf16[16,8192]{1,0:T(8,128)(2,1)S(1)} %get-tuple-element.166), channel_id=1, source_target_pairs={{8,0},{16,8},{24,16},{9,1},{17,9},{25,17},{10,2},{18,10},{26,18},{... | collective-permute-start | bytes 786440 | tf_op jit(solution)/shard_map/ppermute | solution.py:531
  51.8 2.7 %stage.21 = (bf16[16,8192]{1,0:T(8,128)(2,1)S(1)}, bf16[128,24576]{1,0:T(8,128)(2,1)S(1)}, f32[8,8192]{1,0:T(8,128)S(1)}) custom-call(s32[64]{0:T(128)S(1)} %copy-done.4, bf16[128,8192]{1,0:T(8,128)(2,1)S(1)} %shuffle.1.refs_1_, bf16[16,8192]{1,0:T(8,128)(2,1)S(1)} %collective-permute-done.4.refs_2_, ...), custom_call_target="tpu_custom_call", output_to_operand_aliasing={{1}: (10, {}), {2}: (11, {})} | custom-call | flops 67108864 | bytes 6291456 | tf_op jit(solution)/shard_map/stage/pallas_call | solution.py:322
  54.5 3.1 %collective-permute-start.6 = (bf16[16,8192]{1,0:T(8,128)(2,1)S(1)}, bf16[16,8192]{1,0:T(8,128)(2,1)S(1)}, u32[]{:S(2)}, u32[]{:S(2)}) collective-permute-start(bf16[16,8192]{1,0:T(8,128)(2,1)S(1)} %get-tuple-element.165), channel_id=1, source_target_pairs={{8,0},{16,8},{24,16},{9,1},{17,9},{25,17},{10,2},{18,10},{26,18},{... | collective-permute-start | bytes 786440 | tf_op jit(solution)/shard_map/ppermute | solution.py:531
  57.9 2.7 %stage.22 = (bf16[16,8192]{1,0:T(8,128)(2,1)S(1)}, bf16[128,24576]{1,0:T(8,128)(2,1)S(1)}, f32[8,8192]{1,0:T(8,128)S(1)}) custom-call(s32[64]{0:T(128)S(1)} %copy-done.4, bf16[128,8192]{1,0:T(8,128)(2,1)S(1)} %shuffle.1.refs_1_, bf16[16,8192]{1,0:T(8,128)(2,1)S(1)} %collective-permute-done.7.refs_2_, ...), custom_call_target="tpu_custom_call", output_to_operand_aliasing={{1}: (10, {}), {2}: (11, {})} | custom-call | flops 67108864 | bytes 6291456 | tf_op jit(solution)/shard_map/stage/pallas_call | solution.py:322
  60.6 2.4 %collective-permute-start.9 = (bf16[16,8192]{1,0:T(8,128)(2,1)S(1)}, bf16[16,8192]{1,0:T(8,128)(2,1)S(1)}, u32[]{:S(2)}, u32[]{:S(2)}) collective-permute-start(bf16[16,8192]{1,0:T(8,128)(2,1)S(1)} %get-tuple-element.172), channel_id=1, source_target_pairs={{8,0},{16,8},{24,16},{9,1},{17,9},{25,17},{10,2},{18,10},{26,18},{... | collective-permute-start | bytes 786440 | tf_op jit(solution)/shard_map/ppermute | solution.py:531
  63.5 2.7 %stage.23 = (bf16[16,8192]{1,0:T(8,128)(2,1)S(1)}, bf16[128,24576]{1,0:T(8,128)(2,1)S(1)}, f32[8,8192]{1,0:T(8,128)S(1)}) custom-call(s32[64]{0:T(128)S(1)} %copy-done.4, bf16[128,8192]{1,0:T(8,128)(2,1)S(1)} %shuffle.1.refs_1_, bf16[16,8192]{1,0:T(8,128)(2,1)S(1)} %collective-permute-done.6.refs_2_, ...), custom_call_target="tpu_custom_call", output_to_operand_aliasing={{1}: (10, {}), {2}: (11, {})} | custom-call | flops 67108864 | bytes 6291456 | tf_op jit(solution)/shard_map/stage/pallas_call | solution.py:322
  66.3 3.3 %collective-permute-start.8 = (bf16[16,8192]{1,0:T(8,128)(2,1)S(1)}, bf16[16,8192]{1,0:T(8,128)(2,1)S(1)}, u32[]{:S(2)}, u32[]{:S(2)}) collective-permute-start(bf16[16,8192]{1,0:T(8,128)(2,1)S(1)} %get-tuple-element.171), channel_id=1, source_target_pairs={{8,0},{16,8},{24,16},{9,1},{17,9},{25,17},{10,2},{18,10},{26,18},{... | collective-permute-start | bytes 786440 | tf_op jit(solution)/shard_map/ppermute | solution.py:531
  70.3 5.6 %collective-permute-start.11 = (bf16[16,8192]{1,0:T(8,128)(2,1)S(1)}, bf16[16,8192]{1,0:T(8,128)(2,1)S(1)}, u32[]{:S(2)}, u32[]{:S(2)}) collective-permute-start(bf16[16,8192]{1,0:T(8,128)(2,1)S(1)} %get-tuple-element.178), channel_id=1, source_target_pairs={{8,0},{16,8},{24,16},{9,1},{17,9},{25,17},{10,2},{18,10},{26,18},{... | collective-permute-start | bytes 786440 | tf_op jit(solution)/shard_map/ppermute | solution.py:531
  77.4 4.6 %collective-permute-start.10 = (bf16[16,8192]{1,0:T(8,128)(2,1)S(1)}, bf16[16,8192]{1,0:T(8,128)(2,1)S(1)}, u32[]{:S(2)}, u32[]{:S(2)}) collective-permute-start(bf16[16,8192]{1,0:T(8,128)(2,1)S(1)} %get-tuple-element.177), channel_id=1, source_target_pairs={{8,0},{16,8},{24,16},{9,1},{17,9},{25,17},{10,2},{18,10},{26,18},{... | collective-permute-start | bytes 786440 | tf_op jit(solution)/shard_map/ppermute | solution.py:531
  82.1 9.4 %mix.5.refs_9_.left_ref = bf16[128,16384]{1,0:T(8,128)(2,1)S(1)} custom-call(bf16[128,8192]{1,0:T(8,128)(2,1)S(1)} %get-tuple-element.138.z_ref, bf16[128,16384]{1,0:T(8,128)(2,1)S(1)} %get-tuple-element.139.old_ref.refs_9_), custom_call_target="tpu_custom_call", output_to_operand_aliasing={{}: (1, {})} | custom-call | flops 1048576 | bytes 4194304 | tf_op jit(solution)/shard_map/mix/pallas_call | solution.py:238
  93.1 3.1 %sent.1 = (bf16[8256,128]{1,0:T(8,128)(2,1)S(1)}, f32[64,128]{1,0:T(8,128)S(1)}) custom-call(s32[128]{0:T(128)S(1)} %copy-done.5, s32[128]{0:T(128)S(1)} %copy-done.6, s32[128]{0:T(128)S(1)} %pad_add_fusion.column_ref, bf16[128,16384]{1,0:T(8,128)(2,1)S(1)} %mix.5.refs_9_.left_ref, bf16[128,24576]{1,0:T(8,128)(2,1)S(1)} %get-tuple-element.183.right_ref, ...), custom_call_target="tpu_custom_call" | custom-call | flops 268435456 | bytes 8388608 | tf_op jit(solution)/shard_map/sent/pallas_call | solution.py:383
  96.3 3.0 %kept.1 = (f32[8192,128]{1,0:T(8,128)S(1)}, bf16[128,8192]{1,0:T(8,128)(2,1)}) custom-call(s32[128]{0:T(128)S(1)} %copy-done.5, s32[128]{0:T(128)S(1)} %copy-done.6, s32[128]{0:T(128)S(1)} %pad_add_fusion.column_ref, bf16[128,16384]{1,0:T(8,128)(2,1)S(1)} %mix.5.refs_9_.left_ref, bf16[128,24576]{1,0:T(8,128)(2,1)S(1)} %get-tuple-element.183.right_ref), custom_call_target="tpu_custom_call" | custom-call | flops 268435456 | bytes 8388608 | tf_op jit(solution)/shard_map/kept/pallas_call | solution.py:393
  104.0 12.1 %collective-permute-done.14.refs_3_ = bf16[2048,128]{1,0:T(8,128)(2,1)S(1)} collective-permute-done((bf16[2048,128]{1,0:T(8,128)(2,1)S(1)}, bf16[2048,128]{1,0:T(8,128)(2,1)S(1)}, u32[]{:S(2)}, u32[]{:S(2)}) %collective-permute-start.14) | collective-permute-done | bytes 524320 | tf_op jit(solution)/shard_map/ppermute | solution.py:494
  118.6 6.3 %collective-permute-done.16.refs_3_ = bf16[1024,128]{1,0:T(8,128)(2,1)S(1)} collective-permute-done((bf16[1024,128]{1,0:T(8,128)(2,1)S(1)}, bf16[1024,128]{1,0:T(8,128)(2,1)S(1)}, u32[]{:S(2)}, u32[]{:S(2)}) %collective-permute-start.16) | collective-permute-done | bytes 262176 | tf_op jit(solution)/shard_map/ppermute | solution.py:494
  (60 shorter events, 31.4 us)
Async XLA Ops:
  0.6 5.3 %copy-start.2 = (bf16[128,8192]{1,0:T(8,128)(2,1)S(1)}, bf16[128,8192]{1,0:T(8,128)(2,1)}, u32[]{:S(2)}) copy-start(bf16[128,8192]{1,0:T(8,128)(2,1)} %cot_ref.1) | copy-start | bytes 6291460
  0.6 0.8 copy-start.3
  1.4 5.8 %copy-start = (bf16[1,128,8192]{2,1,0:T(8,128)(2,1)S(1)}, bf16[1,128,8192]{2,1,0:T(8,128)(2,1)}, u32[]{:S(2)}) copy-start(bf16[1,128,8192]{2,1,0:T(8,128)(2,1)} %param.7) | copy-start | bytes 6291460
  1.4 5.8 %copy-start.1 = (f32[1,8192]{1,0:T(1,128)S(1)}, f32[1,8192]{1,0:T(1,128)}, u32[]{:S(2)}) copy-start(f32[1,8192]{1,0:T(1,128)} %refs_6_.27) | copy-start | bytes 98308
  6.0 5.2 %copy-start.4 = (s32[64]{0:T(128)S(1)}, s32[64]{0:T(128)}, u32[]{:S(2)}) copy-start(s32[64]{0:T(128)} %refs_0_.27) | copy-start | bytes 772
  11.2 10.8 %collective-permute-start.1 = (bf16[16,8192]{1,0:T(8,128)(2,1)S(1)}, bf16[16,8192]{1,0:T(8,128)(2,1)S(1)}, u32[]{:S(2)}, u32[]{:S(2)}) collective-permute-start(bf16[16,8192]{1,0:T(8,128)(2,1)S(1)} %get-tuple-element.145), channel_id=1, source_target_pairs={{8,0},{16,8},{24,16},{9,1},{17,9},{25,17},{10,2},{18,10},{26,18},{... | collective-permute-start | bytes 786440 | tf_op jit(solution)/shard_map/ppermute | solution.py:531
  17.5 10.4 %collective-permute-start = (bf16[16,8192]{1,0:T(8,128)(2,1)S(1)}, bf16[16,8192]{1,0:T(8,128)(2,1)S(1)}, u32[]{:S(2)}, u32[]{:S(2)}) collective-permute-start(bf16[16,8192]{1,0:T(8,128)(2,1)S(1)} %get-tuple-element.144), channel_id=1, source_target_pairs={{8,0},{16,8},{24,16},{9,1},{17,9},{25,17},{10,2},{18,10},{26,18},{... | collective-permute-start | bytes 786440 | tf_op jit(solution)/shard_map/ppermute | solution.py:531
  24.7 9.6 %collective-permute-start.3 = (bf16[16,8192]{1,0:T(8,128)(2,1)S(1)}, bf16[16,8192]{1,0:T(8,128)(2,1)S(1)}, u32[]{:S(2)}, u32[]{:S(2)}) collective-permute-start(bf16[16,8192]{1,0:T(8,128)(2,1)S(1)} %get-tuple-element.151), channel_id=1, source_target_pairs={{8,0},{16,8},{24,16},{9,1},{17,9},{25,17},{10,2},{18,10},{26,18},{... | collective-permute-start | bytes 786440 | tf_op jit(solution)/shard_map/ppermute | solution.py:531
  30.6 9.6 %collective-permute-start.2 = (bf16[16,8192]{1,0:T(8,128)(2,1)S(1)}, bf16[16,8192]{1,0:T(8,128)(2,1)S(1)}, u32[]{:S(2)}, u32[]{:S(2)}) collective-permute-start(bf16[16,8192]{1,0:T(8,128)(2,1)S(1)} %get-tuple-element.150), channel_id=1, source_target_pairs={{8,0},{16,8},{24,16},{9,1},{17,9},{25,17},{10,2},{18,10},{26,18},{... | collective-permute-start | bytes 786440 | tf_op jit(solution)/shard_map/ppermute | solution.py:531
  37.0 8.9 %collective-permute-start.5 = (bf16[16,8192]{1,0:T(8,128)(2,1)S(1)}, bf16[16,8192]{1,0:T(8,128)(2,1)S(1)}, u32[]{:S(2)}, u32[]{:S(2)}) collective-permute-start(bf16[16,8192]{1,0:T(8,128)(2,1)S(1)} %get-tuple-element.160), channel_id=1, source_target_pairs={{8,0},{16,8},{24,16},{9,1},{17,9},{25,17},{10,2},{18,10},{26,18},{... | collective-permute-start | bytes 786440 | tf_op jit(solution)/shard_map/ppermute | solution.py:531
  42.9 8.9 %collective-permute-start.4 = (bf16[16,8192]{1,0:T(8,128)(2,1)S(1)}, bf16[16,8192]{1,0:T(8,128)(2,1)S(1)}, u32[]{:S(2)}, u32[]{:S(2)}) collective-permute-start(bf16[16,8192]{1,0:T(8,128)(2,1)S(1)} %get-tuple-element.156), channel_id=1, source_target_pairs={{8,0},{16,8},{24,16},{9,1},{17,9},{25,17},{10,2},{18,10},{26,18},{... | collective-permute-start | bytes 786440 | tf_op jit(solution)/shard_map/ppermute | solution.py:531
  48.5 9.4 %collective-permute-start.7 = (bf16[16,8192]{1,0:T(8,128)(2,1)S(1)}, bf16[16,8192]{1,0:T(8,128)(2,1)S(1)}, u32[]{:S(2)}, u32[]{:S(2)}) collective-permute-start(bf16[16,8192]{1,0:T(8,128)(2,1)S(1)} %get-tuple-element.166), channel_id=1, source_target_pairs={{8,0},{16,8},{24,16},{9,1},{17,9},{25,17},{10,2},{18,10},{26,18},{... | collective-permute-start | bytes 786440 | tf_op jit(solution)/shard_map/ppermute | solution.py:531
  54.5 9.1 %collective-permute-start.6 = (bf16[16,8192]{1,0:T(8,128)(2,1)S(1)}, bf16[16,8192]{1,0:T(8,128)(2,1)S(1)}, u32[]{:S(2)}, u32[]{:S(2)}) collective-permute-start(bf16[16,8192]{1,0:T(8,128)(2,1)S(1)} %get-tuple-element.165), channel_id=1, source_target_pairs={{8,0},{16,8},{24,16},{9,1},{17,9},{25,17},{10,2},{18,10},{26,18},{... | collective-permute-start | bytes 786440 | tf_op jit(solution)/shard_map/ppermute | solution.py:531
  60.6 9.6 %collective-permute-start.9 = (bf16[16,8192]{1,0:T(8,128)(2,1)S(1)}, bf16[16,8192]{1,0:T(8,128)(2,1)S(1)}, u32[]{:S(2)}, u32[]{:S(2)}) collective-permute-start(bf16[16,8192]{1,0:T(8,128)(2,1)S(1)} %get-tuple-element.172), channel_id=1, source_target_pairs={{8,0},{16,8},{24,16},{9,1},{17,9},{25,17},{10,2},{18,10},{26,18},{... | collective-permute-start | bytes 786440 | tf_op jit(solution)/shard_map/ppermute | solution.py:531
  66.3 11.1 %collective-permute-start.8 = (bf16[16,8192]{1,0:T(8,128)(2,1)S(1)}, bf16[16,8192]{1,0:T(8,128)(2,1)S(1)}, u32[]{:S(2)}, u32[]{:S(2)}) collective-permute-start(bf16[16,8192]{1,0:T(8,128)(2,1)S(1)} %get-tuple-element.171), channel_id=1, source_target_pairs={{8,0},{16,8},{24,16},{9,1},{17,9},{25,17},{10,2},{18,10},{26,18},{... | collective-permute-start | bytes 786440 | tf_op jit(solution)/shard_map/ppermute | solution.py:531
  70.3 21.3 %collective-permute-start.11 = (bf16[16,8192]{1,0:T(8,128)(2,1)S(1)}, bf16[16,8192]{1,0:T(8,128)(2,1)S(1)}, u32[]{:S(2)}, u32[]{:S(2)}) collective-permute-start(bf16[16,8192]{1,0:T(8,128)(2,1)S(1)} %get-tuple-element.178), channel_id=1, source_target_pairs={{8,0},{16,8},{24,16},{9,1},{17,9},{25,17},{10,2},{18,10},{26,18},{... | collective-permute-start | bytes 786440 | tf_op jit(solution)/shard_map/ppermute | solution.py:531
  77.4 14.9 %collective-permute-start.10 = (bf16[16,8192]{1,0:T(8,128)(2,1)S(1)}, bf16[16,8192]{1,0:T(8,128)(2,1)S(1)}, u32[]{:S(2)}, u32[]{:S(2)}) collective-permute-start(bf16[16,8192]{1,0:T(8,128)(2,1)S(1)} %get-tuple-element.177), channel_id=1, source_target_pairs={{8,0},{16,8},{24,16},{9,1},{17,9},{25,17},{10,2},{18,10},{26,18},{... | collective-permute-start | bytes 786440 | tf_op jit(solution)/shard_map/ppermute | solution.py:531
  92.3 0.8 copy-start.5
  92.3 0.8 copy-start.6
  96.2 4.2 %collective-permute-start.12 = (bf16[8256,128]{1,0:T(8,128)(2,1)S(1)}, bf16[8256,128]{1,0:T(8,128)(2,1)S(1)}, u32[]{:S(2)}, u32[]{:S(2)}) collective-permute-start(bf16[8256,128]{1,0:T(8,128)(2,1)S(1)} %get-tuple-element.187), channel_id=1, source_target_pairs={{0,1},{1,0},{2,3},{3,2},{4,5},{5,4},{6,7},{7,6},{8,9},{9,8},{10,11... | collective-permute-start | bytes 6340616 | tf_op jit(solution)/shard_map/ppermute | solution.py:494
  100.9 15.2 %collective-permute-start.13 = (bf16[2112,128]{1,0:T(8,128)(2,1)S(1)}, bf16[2112,128]{1,0:T(8,128)(2,1)S(1)}, u32[]{:S(2)}, u32[]{:S(2)}) collective-permute-start(bf16[2112,128]{1,0:T(8,128)(2,1)S(1)} %get-tuple-element.191), channel_id=1, source_target_pairs={{0,2},{1,3},{2,0},{3,1},{4,6},{5,7},{6,4},{7,5},{8,10},{9,11},{10,... | collective-permute-start | bytes 1622024 | tf_op jit(solution)/shard_map/ppermute | solution.py:494
  102.5 13.7 %collective-permute-start.14 = (bf16[2048,128]{1,0:T(8,128)(2,1)S(1)}, bf16[2048,128]{1,0:T(8,128)(2,1)S(1)}, u32[]{:S(2)}, u32[]{:S(2)}) collective-permute-start(bf16[2048,128]{1,0:T(8,128)(2,1)S(1)} %get-tuple-element.192), channel_id=1, source_target_pairs={{0,4},{1,5},{2,6},{3,7},{4,0},{5,1},{6,2},{7,3},{8,12},{9,13},{10,... | collective-permute-start | bytes 1572872 | tf_op jit(solution)/shard_map/ppermute | solution.py:494
  116.4 8.5 %collective-permute-start.15 = (bf16[1088,128]{1,0:T(8,128)(2,1)S(1)}, bf16[1088,128]{1,0:T(8,128)(2,1)S(1)}, u32[]{:S(2)}, u32[]{:S(2)}) collective-permute-start(bf16[1088,128]{1,0:T(8,128)(2,1)S(1)} %get-tuple-element.196), channel_id=1, source_target_pairs={{0,4},{1,5},{2,6},{3,7},{4,0},{5,1},{6,2},{7,3},{8,12},{9,13},{10,... | collective-permute-start | bytes 835592 | tf_op jit(solution)/shard_map/ppermute | solution.py:494
  118.0 6.9 %collective-permute-start.16 = (bf16[1024,128]{1,0:T(8,128)(2,1)S(1)}, bf16[1024,128]{1,0:T(8,128)(2,1)S(1)}, u32[]{:S(2)}, u32[]{:S(2)}) collective-permute-start(bf16[1024,128]{1,0:T(8,128)(2,1)S(1)} %get-tuple-element.197), channel_id=1, source_target_pairs={{0,2},{1,3},{2,0},{3,1},{4,6},{5,7},{6,4},{7,5},{8,10},{9,11},{10,... | collective-permute-start | bytes 786440 | tf_op jit(solution)/shard_map/ppermute | solution.py:494

commit v3 on v2

--- a/solution.py
+++ b/solution.py
@@ -164,7 +164,7 @@
             v = x_ref[at_rows, col(j)].astype(jnp.float32)
             return total + v * v
 
-        total = lax.fori_loop(0, F, square, jnp.zeros((rows, B), jnp.float32), unroll=16)
+        total = lax.fori_loop(0, F, square, jnp.zeros((rows, B), jnp.float32), unroll=8)
         mean = jnp.sum(total, axis=1, keepdims=True) * (1.0 / (F * B))
         inv = jnp.broadcast_to(lax.rsqrt(mean + EPS), (rows, B))
         inv_ref[at_rows, :] = inv
@@ -352,131 +352,173 @@
     return jnp.sum(part_ref[:, j * B : (j + 1) * B], axis=0, keepdims=True) * scale
 
 
-def sent_kernel(scale, blocks, table_ref, perm_ref, column_ref, left_ref, right_ref, part_ref, send_ref, gain_ref):
+def products(scale, blocks, jobs, unroll, *lookup):
+    for start, count, target in jobs:
+
+        @pl.loop(0, count, unroll=unroll)
+        def _(p):
+            value = product(scale, blocks, start + p, *lookup)
+            target[pl.ds(pl.multiple_of(p * B, B), B), :] = value.astype(target.dtype)
+
+
+def first_kernel(scale, blocks, table_ref, perm_ref, column_ref, left_ref, right_ref, part_ref, send_ref, gain_ref):
+    count = F // 2
     for j in range(F):
         gain_ref[j : j + 1, :] = gain_row(part_ref, scale, j)
-    send_ref[F * B :, :] = gain_ref[...].astype(jnp.bfloat16)
-
-    @pl.loop(0, F, unroll=8)
-    def _(p):
-        value = product(scale, blocks, p, table_ref, perm_ref, column_ref, left_ref, right_ref)
-        send_ref[pl.ds(pl.multiple_of(p * B, B), B), :] = value.astype(jnp.bfloat16)
-
-
-def kept_kernel(scale, blocks, table_ref, perm_ref, column_ref, left_ref, right_ref, keep_ref, grad_ref, sem):
+    send_ref[count * B :, :] = gain_ref[...].astype(jnp.bfloat16)
+    products(scale, blocks, [(0, count, send_ref)], 8, table_ref, perm_ref, column_ref, left_ref, right_ref)
+
+
+def second_kernel(scale, blocks, table_ref, perm_ref, column_ref, left_ref, right_ref, keep_ref, send_ref):
+    count = F // 2
+    jobs = [(F, count, keep_ref), (count, count, send_ref)]
+    products(scale, blocks, jobs, 4, table_ref, perm_ref, column_ref, left_ref, right_ref)
+
+
+def third_kernel(scale, blocks, table_ref, perm_ref, column_ref, left_ref, right_ref, after_ref, keep_ref, grad_ref, sem):
+    count = F // 2
     out = pltpu.make_async_copy(right_ref.at[:, pl.ds(2 * F * B, F * B)], grad_ref, sem)
     out.start()
-
-    @pl.loop(0, F, unroll=8)
-    def _(p):
-        value = product(scale, blocks, F + p, table_ref, perm_ref, column_ref, left_ref, right_ref)
-        keep_ref[pl.ds(pl.multiple_of(p * B, B), B), :] = value
-
+    products(scale, blocks, [(F + count, count, keep_ref)], 1, table_ref, perm_ref, column_ref, left_ref, right_ref)
     out.wait()
 
 
-def grads(scale, blocks, table, perm, column, left, right, part):
-    n = left.shape[0]
-    params = pltpu.CompilerParams(vmem_limit_bytes=LIMIT)
+def call(kernel, name, args, specs, outs, out_specs, scratch=()):
+    return pl.pallas_call(
+        kernel,
+        out_shape=outs,
+        in_specs=specs,
+        out_specs=out_specs,
+        scratch_shapes=scratch,
+        compiler_params=pltpu.CompilerParams(vmem_limit_bytes=LIMIT),
+        cost_estimate=pl.CostEstimate(flops=1 << 26, bytes_accessed=4 << 20, transcendentals=0),
+        name=name,
+    )(*args)
+
+
+def sum_rows(terms, start, size, target):
+    piece = math.gcd(size, 256)
+
+    @pl.loop(0, size // piece)
+    def _(k):
+        total = 0.0
+        for ref, offset in terms:
+            at = pl.ds(pl.multiple_of(offset + start + k * piece, piece), piece)
+            total = total + ref[at, :].astype(jnp.float32)
+        target(k, piece, total)
+
+
+def into(ref, start=0):
+    def write(k, piece, value):
+        ref[pl.ds(pl.multiple_of(start + k * piece, piece), piece), :] = value.astype(ref.dtype)
+
+    return write
+
+
+def split_kernel(sizes, offsets, send_only, where, *refs):
+    count = len(sizes)
+    inputs, outs = refs[: len(where[0])], refs[len(where[0]) + 1 :]
+    gain_ref = refs[len(where[0])]
+    for side in range(count):
+        terms = [(inputs[i], offsets[side][n]) for n, i in enumerate(where[1 + side])]
+        half = sizes[side] if send_only else sizes[side] // 2
+        sum_rows(terms, 0, half, into(outs[side]))
+        if not send_only:
+            sum_rows(terms, half, half, into(outs[count + side]))
+    carrier = inputs[where[1][-1]]
+    total = gain_ref[...] + carrier[carrier.shape[0] - F :, :].astype(jnp.float32)
+    outs[-1][...] = total
+    outs[0][outs[0].shape[0] - F :, :] = total.astype(jnp.bfloat16)
+
+
+def gather(terms):
+    arrays, where, offsets = [], [], []
+    for side in terms:
+        places = []
+        for array, _ in side:
+            found = [i for i, a in enumerate(arrays) if a is array]
+            places.append(found[0] if found else len(arrays))
+            if not found:
+                arrays.append(array)
+        where.append(places)
+        offsets.append([offset for _, offset in side])
+    return arrays, [list(range(len(arrays)))] + where, offsets
+
+
+def split(terms, sizes, gain, send_only):
+    arrays, where, offsets = gather(terms)
     f32 = jnp.float32
-    cost = pl.CostEstimate(flops=2 * n * B * B * F, bytes_accessed=8 << 20, transcendentals=0)
-    send, gain = pl.pallas_call(
-        functools.partial(sent_kernel, scale, blocks),
-        out_shape=(jax.ShapeDtypeStruct((F * B + F, B), jnp.bfloat16), jax.ShapeDtypeStruct((F, B), f32)),
-        in_specs=[SMEM] * 3 + [VMEM] * 3,
-        out_specs=(VMEM, VMEM),
-        compiler_params=params,
-        cost_estimate=cost,
-        name="sent",
-    )(table, perm, column, left, right, part)
-    got = swap(send, 0)
-    keep, input_gradient = pl.pallas_call(
-        functools.partial(kept_kernel, scale, blocks),
-        out_shape=(jax.ShapeDtypeStruct((F * B, B), f32), jax.ShapeDtypeStruct((n, F * B), jnp.bfloat16)),
-        in_specs=[SMEM] * 3 + [VMEM] * 2,
-        out_specs=(VMEM, ANY),
-        scratch_shapes=[pltpu.SemaphoreType.DMA],
-        compiler_params=params,
-        cost_estimate=cost,
-        name="kept",
-    )(table, perm, column, left, right)
-    return got, gain, keep, input_gradient
-
-
-def split_kernel(sizes, offsets, *refs):
+    halves = [size if send_only else size // 2 for size in sizes]
+    outs = [jax.ShapeDtypeStruct((half + (F if side == 0 else 0), B), jnp.bfloat16) for side, half in enumerate(halves)]
+    outs += [] if send_only else [jax.ShapeDtypeStruct((half, B), f32) for half in halves]
+    outs += [jax.ShapeDtypeStruct((F, B), f32)]
+    got = call(
+        functools.partial(split_kernel, sizes, offsets, send_only, where),
+        "split", (*arrays, gain), [VMEM] * (len(arrays) + 1), tuple(outs), (VMEM,) * len(outs),
+    )
     count = len(sizes)
-    keeps, gots, gain_ref = refs[:count], refs[count : 2 * count], refs[2 * count]
-    sends, rest, total_ref = refs[2 * count + 1 : 3 * count + 1], refs[3 * count + 1 : 4 * count + 1], refs[4 * count + 1]
-    f32 = jnp.float32
-    for side in range(count):
-        half = sizes[side] // 2
-        for begin, target in ((0, sends[side]), (half, rest[side])):
-
-            def body(k, side=side, begin=begin, target=target):
-                piece = math.gcd(half, 256)
-                at = pl.ds(pl.multiple_of(begin + k * piece + offsets[side], piece), piece)
-                to = pl.ds(pl.multiple_of(k * piece, piece), piece)
-                target[to, :] = (keeps[side][at, :] + gots[side][at, :].astype(f32)).astype(target.dtype)
-
-            pl.loop(0, half // math.gcd(half, 256))(body)
-    tail = gots[0].shape[0] - F
-    total = gain_ref[...] + gots[0][tail:, :].astype(f32)
-    total_ref[...] = total
-    sends[0][sizes[0] // 2 :, :] = total.astype(jnp.bfloat16)
-
-
-def split(sizes, offsets, keeps, gots, gain):
-    f32 = jnp.float32
-    halves = [size // 2 for size in sizes]
-    outs = [jax.ShapeDtypeStruct((half + (F if side == 0 else 0), B), jnp.bfloat16) for side, half in enumerate(halves)]
-    outs += [jax.ShapeDtypeStruct((half, B), f32) for half in halves] + [jax.ShapeDtypeStruct((F, B), f32)]
-    got = pl.pallas_call(
-        functools.partial(split_kernel, sizes, offsets),
-        out_shape=tuple(outs),
-        in_specs=[VMEM] * (2 * len(sizes) + 1),
-        out_specs=(VMEM,) * len(outs),
-        compiler_params=pltpu.CompilerParams(vmem_limit_bytes=LIMIT),
-        name="split",
-    )(*keeps, *gots, gain)
-    count = len(sizes)
-    return got[:count], got[count : 2 * count], got[-1]
-
-
-def last_kernel(sizes, offsets, dp, *refs):
-    count = len(sizes)
-    keeps, gots, gain_ref = refs[:count], refs[count : 2 * count], refs[2 * count]
-    out_ref, own_ref, gain_buf = refs[2 * count + 1 :]
-    f32 = jnp.float32
+    return got[:count], got[count:-1], got[-1]
+
+
+def last_kernel(sizes, offsets, where, dp, *refs):
+    inputs, gain_ref = refs[: len(where[0])], refs[len(where[0])]
+    out_ref, own_ref, gain_buf = refs[len(where[0]) + 1 :]
     start = 0
-    for side in range(count):
-        piece = math.gcd(sizes[side], 256)
-
-        @pl.loop(0, sizes[side] // piece)
-        def _(k):
-            at = pl.ds(pl.multiple_of(k * piece + offsets[side], piece), piece)
-            to = pl.ds(pl.multiple_of(k * piece + start, piece), piece)
-            out_ref[to, :] = keeps[side][at, :] + gots[side][at, :].astype(f32)
-
-        start += sizes[side]
-    tail = gots[0].shape[0] - F
-    gain_buf[...] = gain_ref[...] + gots[0][tail:, :].astype(f32)
+    for side, size in enumerate(sizes):
+        terms = [(inputs[i], offsets[side][n]) for n, i in enumerate(where[1 + side])]
+        sum_rows(terms, 0, size, into(out_ref, start))
+        start += size
+    carrier = inputs[where[1][-1]]
+    gain_buf[...] = gain_ref[...] + carrier[carrier.shape[0] - F :, :].astype(jnp.float32)
     each = F // dp
     me = lax.axis_index("dp")
     for r in range(each):
         own_ref[:, r * B : (r + 1) * B] = gain_buf[pl.ds(me * each + r, 1), :]
 
 
-def last(sizes, offsets, dp, keeps, gots, gain):
+def last(terms, sizes, dp, gain):
+    arrays, where, offsets = gather(terms)
     f32 = jnp.float32
-    return pl.pallas_call(
-        functools.partial(last_kernel, sizes, offsets, dp),
-        out_shape=(jax.ShapeDtypeStruct((sum(sizes), B), f32), jax.ShapeDtypeStruct((1, F * B // dp), f32)),
-        in_specs=[VMEM] * (2 * len(sizes) + 1),
-        out_specs=(VMEM, VMEM),
-        scratch_shapes=[pltpu.VMEM((F, B), f32)],
-        compiler_params=pltpu.CompilerParams(vmem_limit_bytes=LIMIT),
-        name="last",
-    )(*keeps, *gots, gain)
+    return call(
+        functools.partial(last_kernel, sizes, offsets, where, dp),
+        "last", (*arrays, gain), [VMEM] * (len(arrays) + 1),
+        (jax.ShapeDtypeStruct((sum(sizes), B), f32), jax.ShapeDtypeStruct((1, F * B // dp), f32)),
+        (VMEM, VMEM), [pltpu.VMEM((F, B), f32)],
+    )
+
+
+def weight_gradients(scale, blocks, dp, tables, left, right, part):
+    bf, f32 = jnp.bfloat16, jnp.float32
+    n = left.shape[0]
+    rows = F * B // 2
+    bits = dp.bit_length() - 2
+    cut = (dp // 4) * max(blocks // 2, 1) * B
+    sizes = [cut, rows - cut]
+    lookup = [SMEM] * 3 + [VMEM] * 2
+    send, gain = call(
+        functools.partial(first_kernel, scale, blocks), "first", (*tables, left, right, part), lookup + [VMEM],
+        (jax.ShapeDtypeStruct((rows + F, B), bf), jax.ShapeDtypeStruct((F, B), f32)), (VMEM, VMEM),
+    )
+    got = swap(send, 0)
+    keep, send = call(
+        functools.partial(second_kernel, scale, blocks), "second", (*tables, left, right), lookup,
+        (jax.ShapeDtypeStruct((rows, B), f32), jax.ShapeDtypeStruct((rows, B), bf)), (VMEM, VMEM),
+    )
+    got_rest = swap(send, 0)
+    sends, _, gain = split([[(keep, 0), (got, 0)], [(keep, cut), (got, cut)]], sizes, gain, True)
+    gots = [swap(sends[0], 1), swap(sends[1], bits)]
+    keep, input_gradient = call(
+        functools.partial(third_kernel, scale, blocks), "third", (*tables, left, right, gain), lookup + [VMEM],
+        (jax.ShapeDtypeStruct((rows, B), f32), jax.ShapeDtypeStruct((n, F * B), bf)), (VMEM, ANY), [pltpu.SemaphoreType.DMA],
+    )
+    terms = [[(keep, at), (got_rest, at), (array, 0)] for at, array in zip((0, cut), gots)]
+    for index in range(1, bits):
+        sends, keeps, gain = split(terms, sizes, gain, False)
+        sizes = [size // 2 for size in sizes]
+        gots = [swap(sends[0], index + 1), swap(sends[1], bits - index)]
+        terms = [[(kept, 0), (array, 0)] for kept, array in zip(keeps, gots)]
+    owned, own_gain = last(terms, sizes, dp, gain)
+    return owned, own_gain, input_gradient
 
 
 def order_of(bits, low_first):
@@ -492,18 +534,6 @@
 def swap(array, bit):
     size = lax.axis_size("dp")
     return lax.ppermute(array, "dp", [(i, i ^ (1 << bit)) for i in range(size)])
-
-
-def reduce_owners(got, gain, keep, dp, blocks):
-    bits = dp.bit_length() - 2
-    cut = (dp // 2) * max(blocks // 2, 1) * B
-    sizes, offsets = [cut, F * B - cut], [0, cut]
-    keeps, gots = [keep, keep], [got, got]
-    for index in range(bits):
-        sends, keeps, gain = split(sizes, offsets, keeps, gots, gain)
-        gots = [swap(sends[0], index + 1), swap(sends[1], bits - index)]
-        sizes, offsets = [size // 2 for size in sizes], [0, 0]
-    return last(sizes, offsets, dp, keeps, gots, gain)
 
 
 def local(acts, weights, gains, cotangent, block_order, owner_table):
@@ -536,12 +566,14 @@
 
     bits = dp.bit_length() - 2
     first = max(blocks // 2, 1)
-    places = [(2 * q) * blocks + i for q in order_of(bits, True) for i in range(first)]
-    places += [(2 * q) * blocks + i for q in order_of(bits, False) for i in range(first, blocks)]
+    one = [(2 * q) * blocks + i for q in order_of(bits, True) for i in range(first)]
+    two = [(2 * q) * blocks + i for q in order_of(bits, False) for i in range(first, blocks)]
+    places = one[: len(one) // 2] + two[: len(two) // 2] + one[len(one) // 2 :] + two[len(two) // 2 :]
     perm = jnp.array([p + blocks for p in places] + places, jnp.int32)
     column = jnp.concatenate([jnp.arange(F, dtype=jnp.int32), F + block_order])
-    got, gain, keep, input_gradient = grads(scale, blocks, owner_table, perm, column, left, right, part)
-    owned, own_gain = reduce_owners(got, gain, keep, dp, blocks)
+    owned, own_gain, input_gradient = weight_gradients(
+        scale, blocks, dp, (owner_table, perm, column), left, right, part
+    )
     return input_gradient[None], owned.reshape(1, blocks, B, B), own_gain
 
 

time: 126 us -> 126 us (level)
  waiting for transfers between devices: 27.9 us -> 19.4 us
  Pallas kernels: 56.8 us -> 64.1 us
    ppermute x5 -> x6, waiting for transfers between devices: 19.6 us -> 11.3 us  [swap(): return lax.ppermute(array, 'dp', [(i, i ^ 1 << bit) for i in range(size)])]
    pallas_call x5 -> x6, Pallas kernels: 7.86 us -> 14.9 us  [call(): pl.pallas_call(kernel, out_shape=outs, in_specs=specs, out_specs=out_spec...]
    ppermute x5 -> x6, starting transfers between devices: 5.38 us -> 5.92 us  [swap(): return lax.ppermute(array, 'dp', [(i, i ^ 1 << bit) for i in range(size)])]
  transfers between devices with their start and end apart: 17 -> 18, of which waited for: 12 -> 11; matrix products, arithmetic and copies ran while one was open for 0% -> 0% of each run, Pallas kernels for 33% -> 40%
where the time goes in v3:
time: 126 us; the launch traced here: 125 us
  Pallas kernels  64.1 us (51%)
  starting transfers between devices  39.6 us (31%)
  waiting for transfers between devices  19.4 us (15%)
    ppermute x12, starting transfers between devices, local(): sent.append(lax.ppermute(out[0], 'segment', pairs))  33.7 us
    pallas_call x14, Pallas kernels, stage(): pl.pallas_call(functools.partial(stage_kernel, step, segments, first), ou...  23.2 us
    pallas_call x6, Pallas kernels, call(): pl.pallas_call(kernel, out_shape=outs, in_specs=specs, out_specs=out_spec...  14.9 us
    ppermute x6, waiting for transfers between devices, swap(): return lax.ppermute(array, 'dp', [(i, i ^ 1 << bit) for i in range(size)])  11.3 us
    pallas_call x8, Pallas kernels, forward(): pl.pallas_call(functools.partial(forward_kernel, step, plan, first), out_...  10.6 us
    pallas_call x3, Pallas kernels, mix(): pl.pallas_call(functools.partial(mix_kernel, step, plan), out_shape=jax.S...  9.64 us
    ppermute x12, waiting for transfers between devices, local(): sent.append(lax.ppermute(out[0], 'segment', pairs))  8.09 us
    ppermute x6, starting transfers between devices, swap(): return lax.ppermute(array, 'dp', [(i, i ^ 1 << bit) for i in range(size)])  5.92 us
  transfers between devices with their start and end apart: 18, of which 11 were waited for; matrix products, arithmetic and copies ran while one was open for 0% of the time, Pallas kernels for 40%

profile of v3, /device:TPU:16, one launch (start us, length us, event | category | flops | bytes accessed | tf_op | source)
XLA Modules:
  0.0 125.1 jit_solution(11412764820094691902)
XLA Ops:
  1.5 4.5 %prepare.1 = (bf16[64,128,128]{2,1,0:T(8,128)(2,1)S(1)}, bf16[64,128,128]{2,1,0:T(8,128)(2,1)S(1)}, bf16[64,128,128]{2,1,0:T(8,128)(2,1)S(1)}) custom-call(s32[64]{0:T(128)S(1)} %copy-done.3, bf16[2,64,128,128]{3,2,1,0:T(8,128)(2,1)} %bitcast.12), custom_call_target="tpu_custom_call" | custom-call | tf_op jit(solution)/shard_map/prepare/pallas_call | solution.py:91
  7.3 3.9 %forward.8 = (f32[128,128]{1,0:T(8,128)S(1)}, bf16[128,16384]{1,0:T(8,128)(2,1)S(1)}, bf16[128,8192]{1,0:T(8,128)(2,1)S(1)}, f32[128,8192]{1,0:T(8,128)S(1)}, f32[128,8192]{1,0:T(8,128)S(1)}) custom-call(bf16[128,8192]{1,0:T(8,128)(2,1)S(1)} %bitcast.4, f32[1,8192]{1,0:T(1,128)S(1)} %copy-done.1, bf16[64,128,128]{2,1,0:T(8,128)(2,1)S(1)} %get-tuple-element.102.refs_2_), custom_call_target="tpu_custom_call" | custom-call | flops 1048576 | bytes 4194304 | tf_op jit(solution)/shard_map/forward/pallas_call | solution.py:191
  11.3 2.4 %collective-permute-start.1 = (bf16[16,8192]{1,0:T(8,128)(2,1)S(1)}, bf16[16,8192]{1,0:T(8,128)(2,1)S(1)}, u32[]{:S(2)}, u32[]{:S(2)}) collective-permute-start(bf16[16,8192]{1,0:T(8,128)(2,1)S(1)} %get-tuple-element.145), channel_id=1, source_target_pairs={{8,0},{16,8},{24,16},{9,1},{17,9},{25,17},{10,2},{18,10},{26,18},{... | collective-permute-start | bytes 786440 | tf_op jit(solution)/shard_map/ppermute | solution.py:561
  13.6 3.9 %forward.9 = (f32[128,128]{1,0:T(8,128)S(1)}, bf16[128,16384]{1,0:T(8,128)(2,1)S(1)}, bf16[128,8192]{1,0:T(8,128)(2,1)S(1)}, f32[128,8192]{1,0:T(8,128)S(1)}, f32[128,8192]{1,0:T(8,128)S(1)}) custom-call(bf16[128,8192]{1,0:T(8,128)(2,1)S(1)} %bitcast.5, ...), custom_call_target="tpu_custom_call", output_to_operand_aliasing={{0}: (3, {}), {1}: (4, {}), {2}: (5, {}), {3}: (6, {}), {4}... | custom-call | flops 1048576 | bytes 4194304 | tf_op jit(solution)/shard_map/forward/pallas_call | solution.py:191
  21.9 2.7 %stage.16 = (bf16[16,8192]{1,0:T(8,128)(2,1)S(1)}, bf16[128,24576]{1,0:T(8,128)(2,1)S(1)}, f32[8,8192]{1,0:T(8,128)S(1)}) custom-call(s32[64]{0:T(128)S(1)} %copy-done.4, bf16[128,8192]{1,0:T(8,128)(2,1)S(1)} %shuffle.1.refs_1_, bf16[16,8192]{1,0:T(8,128)(2,1)S(1)} %collective-permute-done.1.refs_2_, ...), custom_call_target="tpu_custom_call", output_to_operand_aliasing={{1}: (10, {}), {2}: (11, {})} | custom-call | flops 67108864 | bytes 6291456 | tf_op jit(solution)/shard_map/stage/pallas_call | solution.py:322
  27.9 2.7 %stage.17 = (bf16[16,8192]{1,0:T(8,128)(2,1)S(1)}, bf16[128,24576]{1,0:T(8,128)(2,1)S(1)}, f32[8,8192]{1,0:T(8,128)S(1)}) custom-call(s32[64]{0:T(128)S(1)} %copy-done.4, bf16[128,8192]{1,0:T(8,128)(2,1)S(1)} %shuffle.1.refs_1_, bf16[16,8192]{1,0:T(8,128)(2,1)S(1)} %collective-permute-done.refs_2_, ...), custom_call_target="tpu_custom_call", output_to_operand_aliasing={{1}: (10, {}), {2}: (11, {})} | custom-call | flops 67108864 | bytes 6291456 | tf_op jit(solution)/shard_map/stage/pallas_call | solution.py:322
  34.3 2.7 %stage.18 = (bf16[16,8192]{1,0:T(8,128)(2,1)S(1)}, bf16[128,24576]{1,0:T(8,128)(2,1)S(1)}, f32[8,8192]{1,0:T(8,128)S(1)}) custom-call(s32[64]{0:T(128)S(1)} %copy-done.4, bf16[128,8192]{1,0:T(8,128)(2,1)S(1)} %shuffle.1.refs_1_, bf16[16,8192]{1,0:T(8,128)(2,1)S(1)} %collective-permute-done.3.refs_2_, ...), custom_call_target="tpu_custom_call", output_to_operand_aliasing={{1}: (10, {}), {2}: (11, {})} | custom-call | flops 67108864 | bytes 6291456 | tf_op jit(solution)/shard_map/stage/pallas_call | solution.py:322
  37.0 2.2 %collective-permute-start.5 = (bf16[16,8192]{1,0:T(8,128)(2,1)S(1)}, bf16[16,8192]{1,0:T(8,128)(2,1)S(1)}, u32[]{:S(2)}, u32[]{:S(2)}) collective-permute-start(bf16[16,8192]{1,0:T(8,128)(2,1)S(1)} %get-tuple-element.160), channel_id=1, source_target_pairs={{8,0},{16,8},{24,16},{9,1},{17,9},{25,17},{10,2},{18,10},{26,18},{... | collective-permute-start | bytes 786440 | tf_op jit(solution)/shard_map/ppermute | solution.py:561
  40.3 2.7 %stage.19 = (bf16[16,8192]{1,0:T(8,128)(2,1)S(1)}, bf16[128,24576]{1,0:T(8,128)(2,1)S(1)}, f32[8,8192]{1,0:T(8,128)S(1)}) custom-call(s32[64]{0:T(128)S(1)} %copy-done.4, bf16[128,8192]{1,0:T(8,128)(2,1)S(1)} %shuffle.1.refs_1_, bf16[16,8192]{1,0:T(8,128)(2,1)S(1)} %collective-permute-done.2.refs_2_, ...), custom_call_target="tpu_custom_call", output_to_operand_aliasing={{1}: (10, {}), {2}: (11, {})} | custom-call | flops 67108864 | bytes 6291456 | tf_op jit(solution)/shard_map/stage/pallas_call | solution.py:322
  45.9 2.7 %stage.20 = (bf16[16,8192]{1,0:T(8,128)(2,1)S(1)}, bf16[128,24576]{1,0:T(8,128)(2,1)S(1)}, f32[8,8192]{1,0:T(8,128)S(1)}) custom-call(s32[64]{0:T(128)S(1)} %copy-done.4, bf16[128,8192]{1,0:T(8,128)(2,1)S(1)} %shuffle.1.refs_1_, bf16[16,8192]{1,0:T(8,128)(2,1)S(1)} %collective-permute-done.5.refs_2_, ...), custom_call_target="tpu_custom_call", output_to_operand_aliasing={{1}: (10, {}), {2}: (11, {})} | custom-call | flops 67108864 | bytes 6291456 | tf_op jit(solution)/shard_map/stage/pallas_call | solution.py:322
  48.6 2.4 %collective-permute-start.7 = (bf16[16,8192]{1,0:T(8,128)(2,1)S(1)}, bf16[16,8192]{1,0:T(8,128)(2,1)S(1)}, u32[]{:S(2)}, u32[]{:S(2)}) collective-permute-start(bf16[16,8192]{1,0:T(8,128)(2,1)S(1)} %get-tuple-element.166), channel_id=1, source_target_pairs={{8,0},{16,8},{24,16},{9,1},{17,9},{25,17},{10,2},{18,10},{26,18},{... | collective-permute-start | bytes 786440 | tf_op jit(solution)/shard_map/ppermute | solution.py:561
  51.9 2.7 %stage.21 = (bf16[16,8192]{1,0:T(8,128)(2,1)S(1)}, bf16[128,24576]{1,0:T(8,128)(2,1)S(1)}, f32[8,8192]{1,0:T(8,128)S(1)}) custom-call(s32[64]{0:T(128)S(1)} %copy-done.4, bf16[128,8192]{1,0:T(8,128)(2,1)S(1)} %shuffle.1.refs_1_, bf16[16,8192]{1,0:T(8,128)(2,1)S(1)} %collective-permute-done.4.refs_2_, ...), custom_call_target="tpu_custom_call", output_to_operand_aliasing={{1}: (10, {}), {2}: (11, {})} | custom-call | flops 67108864 | bytes 6291456 | tf_op jit(solution)/shard_map/stage/pallas_call | solution.py:322
  54.6 3.1 %collective-permute-start.6 = (bf16[16,8192]{1,0:T(8,128)(2,1)S(1)}, bf16[16,8192]{1,0:T(8,128)(2,1)S(1)}, u32[]{:S(2)}, u32[]{:S(2)}) collective-permute-start(bf16[16,8192]{1,0:T(8,128)(2,1)S(1)} %get-tuple-element.165), channel_id=1, source_target_pairs={{8,0},{16,8},{24,16},{9,1},{17,9},{25,17},{10,2},{18,10},{26,18},{... | collective-permute-start | bytes 786440 | tf_op jit(solution)/shard_map/ppermute | solution.py:561
  58.0 2.7 %stage.22 = (bf16[16,8192]{1,0:T(8,128)(2,1)S(1)}, bf16[128,24576]{1,0:T(8,128)(2,1)S(1)}, f32[8,8192]{1,0:T(8,128)S(1)}) custom-call(s32[64]{0:T(128)S(1)} %copy-done.4, bf16[128,8192]{1,0:T(8,128)(2,1)S(1)} %shuffle.1.refs_1_, bf16[16,8192]{1,0:T(8,128)(2,1)S(1)} %collective-permute-done.7.refs_2_, ...), custom_call_target="tpu_custom_call", output_to_operand_aliasing={{1}: (10, {}), {2}: (11, {})} | custom-call | flops 67108864 | bytes 6291456 | tf_op jit(solution)/shard_map/stage/pallas_call | solution.py:322
  60.7 2.4 %collective-permute-start.9 = (bf16[16,8192]{1,0:T(8,128)(2,1)S(1)}, bf16[16,8192]{1,0:T(8,128)(2,1)S(1)}, u32[]{:S(2)}, u32[]{:S(2)}) collective-permute-start(bf16[16,8192]{1,0:T(8,128)(2,1)S(1)} %get-tuple-element.172), channel_id=1, source_target_pairs={{8,0},{16,8},{24,16},{9,1},{17,9},{25,17},{10,2},{18,10},{26,18},{... | collective-permute-start | bytes 786440 | tf_op jit(solution)/shard_map/ppermute | solution.py:561
  63.6 2.7 %stage.23 = (bf16[16,8192]{1,0:T(8,128)(2,1)S(1)}, bf16[128,24576]{1,0:T(8,128)(2,1)S(1)}, f32[8,8192]{1,0:T(8,128)S(1)}) custom-call(s32[64]{0:T(128)S(1)} %copy-done.4, bf16[128,8192]{1,0:T(8,128)(2,1)S(1)} %shuffle.1.refs_1_, bf16[16,8192]{1,0:T(8,128)(2,1)S(1)} %collective-permute-done.6.refs_2_, ...), custom_call_target="tpu_custom_call", output_to_operand_aliasing={{1}: (10, {}), {2}: (11, {})} | custom-call | flops 67108864 | bytes 6291456 | tf_op jit(solution)/shard_map/stage/pallas_call | solution.py:322
  66.3 3.2 %collective-permute-start.8 = (bf16[16,8192]{1,0:T(8,128)(2,1)S(1)}, bf16[16,8192]{1,0:T(8,128)(2,1)S(1)}, u32[]{:S(2)}, u32[]{:S(2)}) collective-permute-start(bf16[16,8192]{1,0:T(8,128)(2,1)S(1)} %get-tuple-element.171), channel_id=1, source_target_pairs={{8,0},{16,8},{24,16},{9,1},{17,9},{25,17},{10,2},{18,10},{26,18},{... | collective-permute-start | bytes 786440 | tf_op jit(solution)/shard_map/ppermute | solution.py:561
  70.2 5.7 %collective-permute-start.11 = (bf16[16,8192]{1,0:T(8,128)(2,1)S(1)}, bf16[16,8192]{1,0:T(8,128)(2,1)S(1)}, u32[]{:S(2)}, u32[]{:S(2)}) collective-permute-start(bf16[16,8192]{1,0:T(8,128)(2,1)S(1)} %get-tuple-element.178), channel_id=1, source_target_pairs={{8,0},{16,8},{24,16},{9,1},{17,9},{25,17},{10,2},{18,10},{26,18},{... | collective-permute-start | bytes 786440 | tf_op jit(solution)/shard_map/ppermute | solution.py:561
  77.5 4.4 %collective-permute-start.10 = (bf16[16,8192]{1,0:T(8,128)(2,1)S(1)}, bf16[16,8192]{1,0:T(8,128)(2,1)S(1)}, u32[]{:S(2)}, u32[]{:S(2)}) collective-permute-start(bf16[16,8192]{1,0:T(8,128)(2,1)S(1)} %get-tuple-element.177), channel_id=1, source_target_pairs={{8,0},{16,8},{24,16},{9,1},{17,9},{25,17},{10,2},{18,10},{26,18},{... | collective-permute-start | bytes 786440 | tf_op jit(solution)/shard_map/ppermute | solution.py:561
  82.0 9.4 %mix.5.refs_9_.left_ref = bf16[128,16384]{1,0:T(8,128)(2,1)S(1)} custom-call(bf16[128,8192]{1,0:T(8,128)(2,1)S(1)} %get-tuple-element.138.z_ref, bf16[128,16384]{1,0:T(8,128)(2,1)S(1)} %get-tuple-element.139.old_ref.refs_9_), custom_call_target="tpu_custom_call", output_to_operand_aliasing={{}: (1, {})} | custom-call | flops 1048576 | bytes 4194304 | tf_op jit(solution)/shard_map/mix/pallas_call | solution.py:238
  94.9 4.4 %second.1 = (f32[4096,128]{1,0:T(8,128)S(1)}, bf16[4096,128]{1,0:T(8,128)(2,1)S(1)}) custom-call(s32[128]{0:T(128)S(1)} %copy-done.5, s32[128]{0:T(128)S(1)} %copy-done.6, s32[128]{0:T(128)S(1)} %pad_add_fusion.column_ref, bf16[128,16384]{1,0:T(8,128)(2,1)S(1)} %mix.5.refs_9_.left_ref, bf16[128,24576]{1,0:T(8,128)(2,1)S(1)} %get-tuple-element.183.right_ref), custom_call_target="tpu_custom_call" | custom-call | flops 67108864 | bytes 4194304 | tf_op jit(solution)/shard_map/second/pallas_call | solution.py:387
  103.2 6.9 %third.1 = (f32[4096,128]{1,0:T(8,128)S(1)}, bf16[128,8192]{1,0:T(8,128)(2,1)}) custom-call(s32[128]{0:T(128)S(1)} %copy-done.5, s32[128]{0:T(128)S(1)} %copy-done.6, s32[128]{0:T(128)S(1)} %pad_add_fusion.column_ref, bf16[128,16384]{1,0:T(8,128)(2,1)S(1)} %mix.5.refs_9_.left_ref, bf16[128,24576]{1,0:T(8,128)(2,1)S(1)} %get-tuple-element.183.right_ref, ...), custom_call_target="tpu_custom_call" | custom-call | flops 67108864 | bytes 4194304 | tf_op jit(solution)/shard_map/third/pallas_call | solution.py:387
  110.1 5.1 %collective-permute-done.15.refs_3_ = bf16[2048,128]{1,0:T(8,128)(2,1)S(1)} collective-permute-done((bf16[2048,128]{1,0:T(8,128)(2,1)S(1)}, bf16[2048,128]{1,0:T(8,128)(2,1)S(1)}, u32[]{:S(2)}, u32[]{:S(2)}) %collective-permute-start.15) | collective-permute-done | bytes 524320 | tf_op jit(solution)/shard_map/ppermute | solution.py:536
  117.9 6.2 %collective-permute-done.17.refs_3_ = bf16[1024,128]{1,0:T(8,128)(2,1)S(1)} collective-permute-done((bf16[1024,128]{1,0:T(8,128)(2,1)S(1)}, bf16[1024,128]{1,0:T(8,128)(2,1)S(1)}, u32[]{:S(2)}, u32[]{:S(2)}) %collective-permute-start.17) | collective-permute-done | bytes 262176 | tf_op jit(solution)/shard_map/ppermute | solution.py:536
  (63 shorter events, 32.4 us)
Async XLA Ops:
  0.6 5.3 %copy-start.2 = (bf16[128,8192]{1,0:T(8,128)(2,1)S(1)}, bf16[128,8192]{1,0:T(8,128)(2,1)}, u32[]{:S(2)}) copy-start(bf16[128,8192]{1,0:T(8,128)(2,1)} %cot_ref.1) | copy-start | bytes 6291460
  0.6 0.8 copy-start.3
  1.4 5.8 %copy-start = (bf16[1,128,8192]{2,1,0:T(8,128)(2,1)S(1)}, bf16[1,128,8192]{2,1,0:T(8,128)(2,1)}, u32[]{:S(2)}) copy-start(bf16[1,128,8192]{2,1,0:T(8,128)(2,1)} %param.7) | copy-start | bytes 6291460
  1.4 5.8 %copy-start.1 = (f32[1,8192]{1,0:T(1,128)S(1)}, f32[1,8192]{1,0:T(1,128)}, u32[]{:S(2)}) copy-start(f32[1,8192]{1,0:T(1,128)} %refs_6_.27) | copy-start | bytes 98308
  6.0 5.3 %copy-start.4 = (s32[64]{0:T(128)S(1)}, s32[64]{0:T(128)}, u32[]{:S(2)}) copy-start(s32[64]{0:T(128)} %refs_0_.27) | copy-start | bytes 772
  11.3 10.6 %collective-permute-start.1 = (bf16[16,8192]{1,0:T(8,128)(2,1)S(1)}, bf16[16,8192]{1,0:T(8,128)(2,1)S(1)}, u32[]{:S(2)}, u32[]{:S(2)}) collective-permute-start(bf16[16,8192]{1,0:T(8,128)(2,1)S(1)} %get-tuple-element.145), channel_id=1, source_target_pairs={{8,0},{16,8},{24,16},{9,1},{17,9},{25,17},{10,2},{18,10},{26,18},{... | collective-permute-start | bytes 786440 | tf_op jit(solution)/shard_map/ppermute | solution.py:561
  17.6 10.3 %collective-permute-start = (bf16[16,8192]{1,0:T(8,128)(2,1)S(1)}, bf16[16,8192]{1,0:T(8,128)(2,1)S(1)}, u32[]{:S(2)}, u32[]{:S(2)}) collective-permute-start(bf16[16,8192]{1,0:T(8,128)(2,1)S(1)} %get-tuple-element.144), channel_id=1, source_target_pairs={{8,0},{16,8},{24,16},{9,1},{17,9},{25,17},{10,2},{18,10},{26,18},{... | collective-permute-start | bytes 786440 | tf_op jit(solution)/shard_map/ppermute | solution.py:561
  24.6 9.7 %collective-permute-start.3 = (bf16[16,8192]{1,0:T(8,128)(2,1)S(1)}, bf16[16,8192]{1,0:T(8,128)(2,1)S(1)}, u32[]{:S(2)}, u32[]{:S(2)}) collective-permute-start(bf16[16,8192]{1,0:T(8,128)(2,1)S(1)} %get-tuple-element.151), channel_id=1, source_target_pairs={{8,0},{16,8},{24,16},{9,1},{17,9},{25,17},{10,2},{18,10},{26,18},{... | collective-permute-start | bytes 786440 | tf_op jit(solution)/shard_map/ppermute | solution.py:561
  30.6 9.7 %collective-permute-start.2 = (bf16[16,8192]{1,0:T(8,128)(2,1)S(1)}, bf16[16,8192]{1,0:T(8,128)(2,1)S(1)}, u32[]{:S(2)}, u32[]{:S(2)}) collective-permute-start(bf16[16,8192]{1,0:T(8,128)(2,1)S(1)} %get-tuple-element.150), channel_id=1, source_target_pairs={{8,0},{16,8},{24,16},{9,1},{17,9},{25,17},{10,2},{18,10},{26,18},{... | collective-permute-start | bytes 786440 | tf_op jit(solution)/shard_map/ppermute | solution.py:561
  37.0 8.9 %collective-permute-start.5 = (bf16[16,8192]{1,0:T(8,128)(2,1)S(1)}, bf16[16,8192]{1,0:T(8,128)(2,1)S(1)}, u32[]{:S(2)}, u32[]{:S(2)}) collective-permute-start(bf16[16,8192]{1,0:T(8,128)(2,1)S(1)} %get-tuple-element.160), channel_id=1, source_target_pairs={{8,0},{16,8},{24,16},{9,1},{17,9},{25,17},{10,2},{18,10},{26,18},{... | collective-permute-start | bytes 786440 | tf_op jit(solution)/shard_map/ppermute | solution.py:561
  43.0 8.9 %collective-permute-start.4 = (bf16[16,8192]{1,0:T(8,128)(2,1)S(1)}, bf16[16,8192]{1,0:T(8,128)(2,1)S(1)}, u32[]{:S(2)}, u32[]{:S(2)}) collective-permute-start(bf16[16,8192]{1,0:T(8,128)(2,1)S(1)} %get-tuple-element.156), channel_id=1, source_target_pairs={{8,0},{16,8},{24,16},{9,1},{17,9},{25,17},{10,2},{18,10},{26,18},{... | collective-permute-start | bytes 786440 | tf_op jit(solution)/shard_map/ppermute | solution.py:561
  48.6 9.4 %collective-permute-start.7 = (bf16[16,8192]{1,0:T(8,128)(2,1)S(1)}, bf16[16,8192]{1,0:T(8,128)(2,1)S(1)}, u32[]{:S(2)}, u32[]{:S(2)}) collective-permute-start(bf16[16,8192]{1,0:T(8,128)(2,1)S(1)} %get-tuple-element.166), channel_id=1, source_target_pairs={{8,0},{16,8},{24,16},{9,1},{17,9},{25,17},{10,2},{18,10},{26,18},{... | collective-permute-start | bytes 786440 | tf_op jit(solution)/shard_map/ppermute | solution.py:561
  54.6 9.0 %collective-permute-start.6 = (bf16[16,8192]{1,0:T(8,128)(2,1)S(1)}, bf16[16,8192]{1,0:T(8,128)(2,1)S(1)}, u32[]{:S(2)}, u32[]{:S(2)}) collective-permute-start(bf16[16,8192]{1,0:T(8,128)(2,1)S(1)} %get-tuple-element.165), channel_id=1, source_target_pairs={{8,0},{16,8},{24,16},{9,1},{17,9},{25,17},{10,2},{18,10},{26,18},{... | collective-permute-start | bytes 786440 | tf_op jit(solution)/shard_map/ppermute | solution.py:561
  60.7 9.5 %collective-permute-start.9 = (bf16[16,8192]{1,0:T(8,128)(2,1)S(1)}, bf16[16,8192]{1,0:T(8,128)(2,1)S(1)}, u32[]{:S(2)}, u32[]{:S(2)}) collective-permute-start(bf16[16,8192]{1,0:T(8,128)(2,1)S(1)} %get-tuple-element.172), channel_id=1, source_target_pairs={{8,0},{16,8},{24,16},{9,1},{17,9},{25,17},{10,2},{18,10},{26,18},{... | collective-permute-start | bytes 786440 | tf_op jit(solution)/shard_map/ppermute | solution.py:561
  66.3 11.1 %collective-permute-start.8 = (bf16[16,8192]{1,0:T(8,128)(2,1)S(1)}, bf16[16,8192]{1,0:T(8,128)(2,1)S(1)}, u32[]{:S(2)}, u32[]{:S(2)}) collective-permute-start(bf16[16,8192]{1,0:T(8,128)(2,1)S(1)} %get-tuple-element.171), channel_id=1, source_target_pairs={{8,0},{16,8},{24,16},{9,1},{17,9},{25,17},{10,2},{18,10},{26,18},{... | collective-permute-start | bytes 786440 | tf_op jit(solution)/shard_map/ppermute | solution.py:561
  70.2 21.2 %collective-permute-start.11 = (bf16[16,8192]{1,0:T(8,128)(2,1)S(1)}, bf16[16,8192]{1,0:T(8,128)(2,1)S(1)}, u32[]{:S(2)}, u32[]{:S(2)}) collective-permute-start(bf16[16,8192]{1,0:T(8,128)(2,1)S(1)} %get-tuple-element.178), channel_id=1, source_target_pairs={{8,0},{16,8},{24,16},{9,1},{17,9},{25,17},{10,2},{18,10},{26,18},{... | collective-permute-start | bytes 786440 | tf_op jit(solution)/shard_map/ppermute | solution.py:561
  77.5 14.7 %collective-permute-start.10 = (bf16[16,8192]{1,0:T(8,128)(2,1)S(1)}, bf16[16,8192]{1,0:T(8,128)(2,1)S(1)}, u32[]{:S(2)}, u32[]{:S(2)}) collective-permute-start(bf16[16,8192]{1,0:T(8,128)(2,1)S(1)} %get-tuple-element.177), channel_id=1, source_target_pairs={{8,0},{16,8},{24,16},{9,1},{17,9},{25,17},{10,2},{18,10},{26,18},{... | collective-permute-start | bytes 786440 | tf_op jit(solution)/shard_map/ppermute | solution.py:561
  92.2 0.8 copy-start.5
  94.8 5.0 %collective-permute-start.12 = (bf16[4160,128]{1,0:T(8,128)(2,1)S(1)}, bf16[4160,128]{1,0:T(8,128)(2,1)S(1)}, u32[]{:S(2)}, u32[]{:S(2)}) collective-permute-start(bf16[4160,128]{1,0:T(8,128)(2,1)S(1)} %get-tuple-element.186), channel_id=1, source_target_pairs={{0,1},{1,0},{2,3},{3,2},{4,5},{5,4},{6,7},{7,6},{8,9},{9,8},{10,11... | collective-permute-start | bytes 3194888 | tf_op jit(solution)/shard_map/ppermute | solution.py:536
  99.3 10.9 %collective-permute-start.13 = (bf16[4096,128]{1,0:T(8,128)(2,1)S(1)}, bf16[4096,128]{1,0:T(8,128)(2,1)S(1)}, u32[]{:S(2)}, u32[]{:S(2)}) collective-permute-start(bf16[4096,128]{1,0:T(8,128)(2,1)S(1)} %get-tuple-element.191), channel_id=1, source_target_pairs={{0,1},{1,0},{2,3},{3,2},{4,5},{5,4},{6,7},{7,6},{8,9},{9,8},{10,11... | collective-permute-start | bytes 3145736 | tf_op jit(solution)/shard_map/ppermute | solution.py:536
  100.1 15.1 %collective-permute-start.14 = (bf16[2112,128]{1,0:T(8,128)(2,1)S(1)}, bf16[2112,128]{1,0:T(8,128)(2,1)S(1)}, u32[]{:S(2)}, u32[]{:S(2)}) collective-permute-start(bf16[2112,128]{1,0:T(8,128)(2,1)S(1)} %get-tuple-element.192), channel_id=1, source_target_pairs={{0,2},{1,3},{2,0},{3,1},{4,6},{5,7},{6,4},{7,5},{8,10},{9,11},{10,... | collective-permute-start | bytes 1622024 | tf_op jit(solution)/shard_map/ppermute | solution.py:536
  101.7 13.6 %collective-permute-start.15 = (bf16[2048,128]{1,0:T(8,128)(2,1)S(1)}, bf16[2048,128]{1,0:T(8,128)(2,1)S(1)}, u32[]{:S(2)}, u32[]{:S(2)}) collective-permute-start(bf16[2048,128]{1,0:T(8,128)(2,1)S(1)} %get-tuple-element.193), channel_id=1, source_target_pairs={{0,4},{1,5},{2,6},{3,7},{4,0},{5,1},{6,2},{7,3},{8,12},{9,13},{10,... | collective-permute-start | bytes 1572872 | tf_op jit(solution)/shard_map/ppermute | solution.py:536
  115.7 8.4 %collective-permute-start.16 = (bf16[1088,128]{1,0:T(8,128)(2,1)S(1)}, bf16[1088,128]{1,0:T(8,128)(2,1)S(1)}, u32[]{:S(2)}, u32[]{:S(2)}) collective-permute-start(bf16[1088,128]{1,0:T(8,128)(2,1)S(1)} %get-tuple-element.195), channel_id=1, source_target_pairs={{0,4},{1,5},{2,6},{3,7},{4,0},{5,1},{6,2},{7,3},{8,12},{9,13},{10,... | collective-permute-start | bytes 835592 | tf_op jit(solution)/shard_map/ppermute | solution.py:536
  117.2 6.8 %collective-permute-start.17 = (bf16[1024,128]{1,0:T(8,128)(2,1)S(1)}, bf16[1024,128]{1,0:T(8,128)(2,1)S(1)}, u32[]{:S(2)}, u32[]{:S(2)}) collective-permute-start(bf16[1024,128]{1,0:T(8,128)(2,1)S(1)} %get-tuple-element.197), channel_id=1, source_target_pairs={{0,2},{1,3},{2,0},{3,1},{4,6},{5,7},{6,4},{7,5},{8,10},{9,11},{10,... | collective-permute-start | bytes 786440 | tf_op jit(solution)/shard_map/ppermute | solution.py:536
  (1 other events, 0.8 us)

commit v4 on v3

--- a/solution.py
+++ b/solution.py
@@ -372,14 +372,14 @@
 def second_kernel(scale, blocks, table_ref, perm_ref, column_ref, left_ref, right_ref, keep_ref, send_ref):
     count = F // 2
     jobs = [(F, count, keep_ref), (count, count, send_ref)]
-    products(scale, blocks, jobs, 4, table_ref, perm_ref, column_ref, left_ref, right_ref)
+    products(scale, blocks, jobs, 8, table_ref, perm_ref, column_ref, left_ref, right_ref)
 
 
 def third_kernel(scale, blocks, table_ref, perm_ref, column_ref, left_ref, right_ref, after_ref, keep_ref, grad_ref, sem):
     count = F // 2
     out = pltpu.make_async_copy(right_ref.at[:, pl.ds(2 * F * B, F * B)], grad_ref, sem)
     out.start()
-    products(scale, blocks, [(F + count, count, keep_ref)], 1, table_ref, perm_ref, column_ref, left_ref, right_ref)
+    products(scale, blocks, [(F + count, count, keep_ref)], 2, table_ref, perm_ref, column_ref, left_ref, right_ref)
     out.wait()
 
 

time: 126 us -> 124 us (0.984)
  Pallas kernels: 64.1 us -> 59.7 us
  waiting for transfers between devices: 19.4 us -> 22.4 us
    pallas_call x6, Pallas kernels: 14.9 us -> 10.5 us  [call(): pl.pallas_call(kernel, out_shape=outs, in_specs=specs, out_specs=out_spec...]
    ppermute x6, waiting for transfers between devices: 11.3 us -> 14.3 us  [swap(): return lax.ppermute(array, 'dp', [(i, i ^ 1 << bit) for i in range(size)])]
  transfers between devices with their start and end apart: 18 -> 18, of which waited for: 11 -> 11; matrix products, arithmetic and copies ran while one was open for 0% -> 0% of each run, Pallas kernels for 40% -> 37%
where the time goes in v4:
time: 124 us
  Pallas kernels  59.7 us (48%)
  starting transfers between devices  39.6 us (32%)
  waiting for transfers between devices  22.4 us (18%)
    ppermute x12, starting transfers between devices, local(): sent.append(lax.ppermute(out[0], 'segment', pairs))  33.7 us
    pallas_call x14, Pallas kernels, stage(): pl.pallas_call(functools.partial(stage_kernel, step, segments, first), ou...  23.2 us
    ppermute x6, waiting for transfers between devices, swap(): return lax.ppermute(array, 'dp', [(i, i ^ 1 << bit) for i in range(size)])  14.3 us
    pallas_call x8, Pallas kernels, forward(): pl.pallas_call(functools.partial(forward_kernel, step, plan, first), out_...  10.6 us
    pallas_call x6, Pallas kernels, call(): pl.pallas_call(kernel, out_shape=outs, in_specs=specs, out_specs=out_spec...  10.5 us
    pallas_call x3, Pallas kernels, mix(): pl.pallas_call(functools.partial(mix_kernel, step, plan), out_shape=jax.S...  9.64 us
    ppermute x12, waiting for transfers between devices, local(): sent.append(lax.ppermute(out[0], 'segment', pairs))  8.09 us
    ppermute x6, starting transfers between devices, swap(): return lax.ppermute(array, 'dp', [(i, i ^ 1 << bit) for i in range(size)])  5.92 us
  transfers between devices with their start and end apart: 18, of which 11 were waited for; matrix products, arithmetic and copies ran while one was open for 0% of the time, Pallas kernels for 37%

profile of v4, /device:TPU:16, one launch (start us, length us, event | category | flops | bytes accessed | tf_op | source)
XLA Modules:
  0.0 123.7 jit_solution(14113628984095570658)
XLA Ops:
  1.5 4.5 %prepare.1 = (bf16[64,128,128]{2,1,0:T(8,128)(2,1)S(1)}, bf16[64,128,128]{2,1,0:T(8,128)(2,1)S(1)}, bf16[64,128,128]{2,1,0:T(8,128)(2,1)S(1)}) custom-call(s32[64]{0:T(128)S(1)} %copy-done.3, bf16[2,64,128,128]{3,2,1,0:T(8,128)(2,1)} %bitcast.12), custom_call_target="tpu_custom_call" | custom-call | tf_op jit(solution)/shard_map/prepare/pallas_call | solution.py:91
  7.3 3.9 %forward.8 = (f32[128,128]{1,0:T(8,128)S(1)}, bf16[128,16384]{1,0:T(8,128)(2,1)S(1)}, bf16[128,8192]{1,0:T(8,128)(2,1)S(1)}, f32[128,8192]{1,0:T(8,128)S(1)}, f32[128,8192]{1,0:T(8,128)S(1)}) custom-call(bf16[128,8192]{1,0:T(8,128)(2,1)S(1)} %bitcast.4, f32[1,8192]{1,0:T(1,128)S(1)} %copy-done.1, bf16[64,128,128]{2,1,0:T(8,128)(2,1)S(1)} %get-tuple-element.102.refs_2_), custom_call_target="tpu_custom_call" | custom-call | flops 1048576 | bytes 4194304 | tf_op jit(solution)/shard_map/forward/pallas_call | solution.py:191
  11.3 2.4 %collective-permute-start.1 = (bf16[16,8192]{1,0:T(8,128)(2,1)S(1)}, bf16[16,8192]{1,0:T(8,128)(2,1)S(1)}, u32[]{:S(2)}, u32[]{:S(2)}) collective-permute-start(bf16[16,8192]{1,0:T(8,128)(2,1)S(1)} %get-tuple-element.145), channel_id=1, source_target_pairs={{8,0},{16,8},{24,16},{9,1},{17,9},{25,17},{10,2},{18,10},{26,18},{... | collective-permute-start | bytes 786440 | tf_op jit(solution)/shard_map/ppermute | solution.py:561
  13.6 3.9 %forward.9 = (f32[128,128]{1,0:T(8,128)S(1)}, bf16[128,16384]{1,0:T(8,128)(2,1)S(1)}, bf16[128,8192]{1,0:T(8,128)(2,1)S(1)}, f32[128,8192]{1,0:T(8,128)S(1)}, f32[128,8192]{1,0:T(8,128)S(1)}) custom-call(bf16[128,8192]{1,0:T(8,128)(2,1)S(1)} %bitcast.5, ...), custom_call_target="tpu_custom_call", output_to_operand_aliasing={{0}: (3, {}), {1}: (4, {}), {2}: (5, {}), {3}: (6, {}), {4}... | custom-call | flops 1048576 | bytes 4194304 | tf_op jit(solution)/shard_map/forward/pallas_call | solution.py:191
  21.9 2.7 %stage.16 = (bf16[16,8192]{1,0:T(8,128)(2,1)S(1)}, bf16[128,24576]{1,0:T(8,128)(2,1)S(1)}, f32[8,8192]{1,0:T(8,128)S(1)}) custom-call(s32[64]{0:T(128)S(1)} %copy-done.4, bf16[128,8192]{1,0:T(8,128)(2,1)S(1)} %shuffle.1.refs_1_, bf16[16,8192]{1,0:T(8,128)(2,1)S(1)} %collective-permute-done.1.refs_2_, ...), custom_call_target="tpu_custom_call", output_to_operand_aliasing={{1}: (10, {}), {2}: (11, {})} | custom-call | flops 67108864 | bytes 6291456 | tf_op jit(solution)/shard_map/stage/pallas_call | solution.py:322
  27.9 2.7 %stage.17 = (bf16[16,8192]{1,0:T(8,128)(2,1)S(1)}, bf16[128,24576]{1,0:T(8,128)(2,1)S(1)}, f32[8,8192]{1,0:T(8,128)S(1)}) custom-call(s32[64]{0:T(128)S(1)} %copy-done.4, bf16[128,8192]{1,0:T(8,128)(2,1)S(1)} %shuffle.1.refs_1_, bf16[16,8192]{1,0:T(8,128)(2,1)S(1)} %collective-permute-done.refs_2_, ...), custom_call_target="tpu_custom_call", output_to_operand_aliasing={{1}: (10, {}), {2}: (11, {})} | custom-call | flops 67108864 | bytes 6291456 | tf_op jit(solution)/shard_map/stage/pallas_call | solution.py:322
  34.3 2.7 %stage.18 = (bf16[16,8192]{1,0:T(8,128)(2,1)S(1)}, bf16[128,24576]{1,0:T(8,128)(2,1)S(1)}, f32[8,8192]{1,0:T(8,128)S(1)}) custom-call(s32[64]{0:T(128)S(1)} %copy-done.4, bf16[128,8192]{1,0:T(8,128)(2,1)S(1)} %shuffle.1.refs_1_, bf16[16,8192]{1,0:T(8,128)(2,1)S(1)} %collective-permute-done.3.refs_2_, ...), custom_call_target="tpu_custom_call", output_to_operand_aliasing={{1}: (10, {}), {2}: (11, {})} | custom-call | flops 67108864 | bytes 6291456 | tf_op jit(solution)/shard_map/stage/pallas_call | solution.py:322
  40.3 2.7 %stage.19 = (bf16[16,8192]{1,0:T(8,128)(2,1)S(1)}, bf16[128,24576]{1,0:T(8,128)(2,1)S(1)}, f32[8,8192]{1,0:T(8,128)S(1)}) custom-call(s32[64]{0:T(128)S(1)} %copy-done.4, bf16[128,8192]{1,0:T(8,128)(2,1)S(1)} %shuffle.1.refs_1_, bf16[16,8192]{1,0:T(8,128)(2,1)S(1)} %collective-permute-done.2.refs_2_, ...), custom_call_target="tpu_custom_call", output_to_operand_aliasing={{1}: (10, {}), {2}: (11, {})} | custom-call | flops 67108864 | bytes 6291456 | tf_op jit(solution)/shard_map/stage/pallas_call | solution.py:322
  43.0 2.2 %collective-permute-start.4 = (bf16[16,8192]{1,0:T(8,128)(2,1)S(1)}, bf16[16,8192]{1,0:T(8,128)(2,1)S(1)}, u32[]{:S(2)}, u32[]{:S(2)}) collective-permute-start(bf16[16,8192]{1,0:T(8,128)(2,1)S(1)} %get-tuple-element.156), channel_id=1, source_target_pairs={{8,0},{16,8},{24,16},{9,1},{17,9},{25,17},{10,2},{18,10},{26,18},{... | collective-permute-start | bytes 786440 | tf_op jit(solution)/shard_map/ppermute | solution.py:561
  45.9 2.7 %stage.20 = (bf16[16,8192]{1,0:T(8,128)(2,1)S(1)}, bf16[128,24576]{1,0:T(8,128)(2,1)S(1)}, f32[8,8192]{1,0:T(8,128)S(1)}) custom-call(s32[64]{0:T(128)S(1)} %copy-done.4, bf16[128,8192]{1,0:T(8,128)(2,1)S(1)} %shuffle.1.refs_1_, bf16[16,8192]{1,0:T(8,128)(2,1)S(1)} %collective-permute-done.5.refs_2_, ...), custom_call_target="tpu_custom_call", output_to_operand_aliasing={{1}: (10, {}), {2}: (11, {})} | custom-call | flops 67108864 | bytes 6291456 | tf_op jit(solution)/shard_map/stage/pallas_call | solution.py:322
  48.6 2.4 %collective-permute-start.7 = (bf16[16,8192]{1,0:T(8,128)(2,1)S(1)}, bf16[16,8192]{1,0:T(8,128)(2,1)S(1)}, u32[]{:S(2)}, u32[]{:S(2)}) collective-permute-start(bf16[16,8192]{1,0:T(8,128)(2,1)S(1)} %get-tuple-element.166), channel_id=1, source_target_pairs={{8,0},{16,8},{24,16},{9,1},{17,9},{25,17},{10,2},{18,10},{26,18},{... | collective-permute-start | bytes 786440 | tf_op jit(solution)/shard_map/ppermute | solution.py:561
  51.9 2.7 %stage.21 = (bf16[16,8192]{1,0:T(8,128)(2,1)S(1)}, bf16[128,24576]{1,0:T(8,128)(2,1)S(1)}, f32[8,8192]{1,0:T(8,128)S(1)}) custom-call(s32[64]{0:T(128)S(1)} %copy-done.4, bf16[128,8192]{1,0:T(8,128)(2,1)S(1)} %shuffle.1.refs_1_, bf16[16,8192]{1,0:T(8,128)(2,1)S(1)} %collective-permute-done.4.refs_2_, ...), custom_call_target="tpu_custom_call", output_to_operand_aliasing={{1}: (10, {}), {2}: (11, {})} | custom-call | flops 67108864 | bytes 6291456 | tf_op jit(solution)/shard_map/stage/pallas_call | solution.py:322
  54.6 3.1 %collective-permute-start.6 = (bf16[16,8192]{1,0:T(8,128)(2,1)S(1)}, bf16[16,8192]{1,0:T(8,128)(2,1)S(1)}, u32[]{:S(2)}, u32[]{:S(2)}) collective-permute-start(bf16[16,8192]{1,0:T(8,128)(2,1)S(1)} %get-tuple-element.165), channel_id=1, source_target_pairs={{8,0},{16,8},{24,16},{9,1},{17,9},{25,17},{10,2},{18,10},{26,18},{... | collective-permute-start | bytes 786440 | tf_op jit(solution)/shard_map/ppermute | solution.py:561
  58.0 2.7 %stage.22 = (bf16[16,8192]{1,0:T(8,128)(2,1)S(1)}, bf16[128,24576]{1,0:T(8,128)(2,1)S(1)}, f32[8,8192]{1,0:T(8,128)S(1)}) custom-call(s32[64]{0:T(128)S(1)} %copy-done.4, bf16[128,8192]{1,0:T(8,128)(2,1)S(1)} %shuffle.1.refs_1_, bf16[16,8192]{1,0:T(8,128)(2,1)S(1)} %collective-permute-done.7.refs_2_, ...), custom_call_target="tpu_custom_call", output_to_operand_aliasing={{1}: (10, {}), {2}: (11, {})} | custom-call | flops 67108864 | bytes 6291456 | tf_op jit(solution)/shard_map/stage/pallas_call | solution.py:322
  60.7 2.4 %collective-permute-start.9 = (bf16[16,8192]{1,0:T(8,128)(2,1)S(1)}, bf16[16,8192]{1,0:T(8,128)(2,1)S(1)}, u32[]{:S(2)}, u32[]{:S(2)}) collective-permute-start(bf16[16,8192]{1,0:T(8,128)(2,1)S(1)} %get-tuple-element.172), channel_id=1, source_target_pairs={{8,0},{16,8},{24,16},{9,1},{17,9},{25,17},{10,2},{18,10},{26,18},{... | collective-permute-start | bytes 786440 | tf_op jit(solution)/shard_map/ppermute | solution.py:561
  63.6 2.7 %stage.23 = (bf16[16,8192]{1,0:T(8,128)(2,1)S(1)}, bf16[128,24576]{1,0:T(8,128)(2,1)S(1)}, f32[8,8192]{1,0:T(8,128)S(1)}) custom-call(s32[64]{0:T(128)S(1)} %copy-done.4, bf16[128,8192]{1,0:T(8,128)(2,1)S(1)} %shuffle.1.refs_1_, bf16[16,8192]{1,0:T(8,128)(2,1)S(1)} %collective-permute-done.6.refs_2_, ...), custom_call_target="tpu_custom_call", output_to_operand_aliasing={{1}: (10, {}), {2}: (11, {})} | custom-call | flops 67108864 | bytes 6291456 | tf_op jit(solution)/shard_map/stage/pallas_call | solution.py:322
  66.3 3.2 %collective-permute-start.8 = (bf16[16,8192]{1,0:T(8,128)(2,1)S(1)}, bf16[16,8192]{1,0:T(8,128)(2,1)S(1)}, u32[]{:S(2)}, u32[]{:S(2)}) collective-permute-start(bf16[16,8192]{1,0:T(8,128)(2,1)S(1)} %get-tuple-element.171), channel_id=1, source_target_pairs={{8,0},{16,8},{24,16},{9,1},{17,9},{25,17},{10,2},{18,10},{26,18},{... | collective-permute-start | bytes 786440 | tf_op jit(solution)/shard_map/ppermute | solution.py:561
  70.2 5.7 %collective-permute-start.11 = (bf16[16,8192]{1,0:T(8,128)(2,1)S(1)}, bf16[16,8192]{1,0:T(8,128)(2,1)S(1)}, u32[]{:S(2)}, u32[]{:S(2)}) collective-permute-start(bf16[16,8192]{1,0:T(8,128)(2,1)S(1)} %get-tuple-element.178), channel_id=1, source_target_pairs={{8,0},{16,8},{24,16},{9,1},{17,9},{25,17},{10,2},{18,10},{26,18},{... | collective-permute-start | bytes 786440 | tf_op jit(solution)/shard_map/ppermute | solution.py:561
  77.5 4.4 %collective-permute-start.10 = (bf16[16,8192]{1,0:T(8,128)(2,1)S(1)}, bf16[16,8192]{1,0:T(8,128)(2,1)S(1)}, u32[]{:S(2)}, u32[]{:S(2)}) collective-permute-start(bf16[16,8192]{1,0:T(8,128)(2,1)S(1)} %get-tuple-element.177), channel_id=1, source_target_pairs={{8,0},{16,8},{24,16},{9,1},{17,9},{25,17},{10,2},{18,10},{26,18},{... | collective-permute-start | bytes 786440 | tf_op jit(solution)/shard_map/ppermute | solution.py:561
  82.0 9.4 %mix.5.refs_9_.left_ref = bf16[128,16384]{1,0:T(8,128)(2,1)S(1)} custom-call(bf16[128,8192]{1,0:T(8,128)(2,1)S(1)} %get-tuple-element.138.z_ref, bf16[128,16384]{1,0:T(8,128)(2,1)S(1)} %get-tuple-element.139.old_ref.refs_9_), custom_call_target="tpu_custom_call", output_to_operand_aliasing={{}: (1, {})} | custom-call | flops 1048576 | bytes 4194304 | tf_op jit(solution)/shard_map/mix/pallas_call | solution.py:238
  94.9 3.0 %second.1 = (f32[4096,128]{1,0:T(8,128)S(1)}, bf16[4096,128]{1,0:T(8,128)(2,1)S(1)}) custom-call(s32[128]{0:T(128)S(1)} %copy-done.5, s32[128]{0:T(128)S(1)} %copy-done.6, s32[128]{0:T(128)S(1)} %pad_add_fusion.column_ref, bf16[128,16384]{1,0:T(8,128)(2,1)S(1)} %mix.5.refs_9_.left_ref, bf16[128,24576]{1,0:T(8,128)(2,1)S(1)} %get-tuple-element.183.right_ref), custom_call_target="tpu_custom_call" | custom-call | flops 67108864 | bytes 4194304 | tf_op jit(solution)/shard_map/second/pallas_call | solution.py:387
  101.8 3.9 %third.1 = (f32[4096,128]{1,0:T(8,128)S(1)}, bf16[128,8192]{1,0:T(8,128)(2,1)}) custom-call(s32[128]{0:T(128)S(1)} %copy-done.5, s32[128]{0:T(128)S(1)} %copy-done.6, s32[128]{0:T(128)S(1)} %pad_add_fusion.column_ref, bf16[128,16384]{1,0:T(8,128)(2,1)S(1)} %mix.5.refs_9_.left_ref, bf16[128,24576]{1,0:T(8,128)(2,1)S(1)} %get-tuple-element.183.right_ref, ...), custom_call_target="tpu_custom_call" | custom-call | flops 67108864 | bytes 4194304 | tf_op jit(solution)/shard_map/third/pallas_call | solution.py:387
  105.8 8.1 %collective-permute-done.15.refs_3_ = bf16[2048,128]{1,0:T(8,128)(2,1)S(1)} collective-permute-done((bf16[2048,128]{1,0:T(8,128)(2,1)S(1)}, bf16[2048,128]{1,0:T(8,128)(2,1)S(1)}, u32[]{:S(2)}, u32[]{:S(2)}) %collective-permute-start.15) | collective-permute-done | bytes 524320 | tf_op jit(solution)/shard_map/ppermute | solution.py:536
  116.5 6.2 %collective-permute-done.17.refs_3_ = bf16[1024,128]{1,0:T(8,128)(2,1)S(1)} collective-permute-done((bf16[1024,128]{1,0:T(8,128)(2,1)S(1)}, bf16[1024,128]{1,0:T(8,128)(2,1)S(1)}, u32[]{:S(2)}, u32[]{:S(2)}) %collective-permute-start.17) | collective-permute-done | bytes 262176 | tf_op jit(solution)/shard_map/ppermute | solution.py:536
  (63 shorter events, 32.4 us)
Async XLA Ops:
  0.6 5.3 %copy-start.2 = (bf16[128,8192]{1,0:T(8,128)(2,1)S(1)}, bf16[128,8192]{1,0:T(8,128)(2,1)}, u32[]{:S(2)}) copy-start(bf16[128,8192]{1,0:T(8,128)(2,1)} %cot_ref.1) | copy-start | bytes 6291460
  0.6 0.8 copy-start.3
  1.4 5.8 %copy-start = (bf16[1,128,8192]{2,1,0:T(8,128)(2,1)S(1)}, bf16[1,128,8192]{2,1,0:T(8,128)(2,1)}, u32[]{:S(2)}) copy-start(bf16[1,128,8192]{2,1,0:T(8,128)(2,1)} %param.7) | copy-start | bytes 6291460
  1.4 5.8 %copy-start.1 = (f32[1,8192]{1,0:T(1,128)S(1)}, f32[1,8192]{1,0:T(1,128)}, u32[]{:S(2)}) copy-start(f32[1,8192]{1,0:T(1,128)} %refs_6_.27) | copy-start | bytes 98308
  6.0 5.3 %copy-start.4 = (s32[64]{0:T(128)S(1)}, s32[64]{0:T(128)}, u32[]{:S(2)}) copy-start(s32[64]{0:T(128)} %refs_0_.27) | copy-start | bytes 772
  11.3 10.6 %collective-permute-start.1 = (bf16[16,8192]{1,0:T(8,128)(2,1)S(1)}, bf16[16,8192]{1,0:T(8,128)(2,1)S(1)}, u32[]{:S(2)}, u32[]{:S(2)}) collective-permute-start(bf16[16,8192]{1,0:T(8,128)(2,1)S(1)} %get-tuple-element.145), channel_id=1, source_target_pairs={{8,0},{16,8},{24,16},{9,1},{17,9},{25,17},{10,2},{18,10},{26,18},{... | collective-permute-start | bytes 786440 | tf_op jit(solution)/shard_map/ppermute | solution.py:561
  17.6 10.3 %collective-permute-start = (bf16[16,8192]{1,0:T(8,128)(2,1)S(1)}, bf16[16,8192]{1,0:T(8,128)(2,1)S(1)}, u32[]{:S(2)}, u32[]{:S(2)}) collective-permute-start(bf16[16,8192]{1,0:T(8,128)(2,1)S(1)} %get-tuple-element.144), channel_id=1, source_target_pairs={{8,0},{16,8},{24,16},{9,1},{17,9},{25,17},{10,2},{18,10},{26,18},{... | collective-permute-start | bytes 786440 | tf_op jit(solution)/shard_map/ppermute | solution.py:561
  24.6 9.7 %collective-permute-start.3 = (bf16[16,8192]{1,0:T(8,128)(2,1)S(1)}, bf16[16,8192]{1,0:T(8,128)(2,1)S(1)}, u32[]{:S(2)}, u32[]{:S(2)}) collective-permute-start(bf16[16,8192]{1,0:T(8,128)(2,1)S(1)} %get-tuple-element.151), channel_id=1, source_target_pairs={{8,0},{16,8},{24,16},{9,1},{17,9},{25,17},{10,2},{18,10},{26,18},{... | collective-permute-start | bytes 786440 | tf_op jit(solution)/shard_map/ppermute | solution.py:561
  30.6 9.7 %collective-permute-start.2 = (bf16[16,8192]{1,0:T(8,128)(2,1)S(1)}, bf16[16,8192]{1,0:T(8,128)(2,1)S(1)}, u32[]{:S(2)}, u32[]{:S(2)}) collective-permute-start(bf16[16,8192]{1,0:T(8,128)(2,1)S(1)} %get-tuple-element.150), channel_id=1, source_target_pairs={{8,0},{16,8},{24,16},{9,1},{17,9},{25,17},{10,2},{18,10},{26,18},{... | collective-permute-start | bytes 786440 | tf_op jit(solution)/shard_map/ppermute | solution.py:561
  37.0 8.9 %collective-permute-start.5 = (bf16[16,8192]{1,0:T(8,128)(2,1)S(1)}, bf16[16,8192]{1,0:T(8,128)(2,1)S(1)}, u32[]{:S(2)}, u32[]{:S(2)}) collective-permute-start(bf16[16,8192]{1,0:T(8,128)(2,1)S(1)} %get-tuple-element.160), channel_id=1, source_target_pairs={{8,0},{16,8},{24,16},{9,1},{17,9},{25,17},{10,2},{18,10},{26,18},{... | collective-permute-start | bytes 786440 | tf_op jit(solution)/shard_map/ppermute | solution.py:561
  43.0 8.9 %collective-permute-start.4 = (bf16[16,8192]{1,0:T(8,128)(2,1)S(1)}, bf16[16,8192]{1,0:T(8,128)(2,1)S(1)}, u32[]{:S(2)}, u32[]{:S(2)}) collective-permute-start(bf16[16,8192]{1,0:T(8,128)(2,1)S(1)} %get-tuple-element.156), channel_id=1, source_target_pairs={{8,0},{16,8},{24,16},{9,1},{17,9},{25,17},{10,2},{18,10},{26,18},{... | collective-permute-start | bytes 786440 | tf_op jit(solution)/shard_map/ppermute | solution.py:561
  48.6 9.4 %collective-permute-start.7 = (bf16[16,8192]{1,0:T(8,128)(2,1)S(1)}, bf16[16,8192]{1,0:T(8,128)(2,1)S(1)}, u32[]{:S(2)}, u32[]{:S(2)}) collective-permute-start(bf16[16,8192]{1,0:T(8,128)(2,1)S(1)} %get-tuple-element.166), channel_id=1, source_target_pairs={{8,0},{16,8},{24,16},{9,1},{17,9},{25,17},{10,2},{18,10},{26,18},{... | collective-permute-start | bytes 786440 | tf_op jit(solution)/shard_map/ppermute | solution.py:561
  54.6 9.0 %collective-permute-start.6 = (bf16[16,8192]{1,0:T(8,128)(2,1)S(1)}, bf16[16,8192]{1,0:T(8,128)(2,1)S(1)}, u32[]{:S(2)}, u32[]{:S(2)}) collective-permute-start(bf16[16,8192]{1,0:T(8,128)(2,1)S(1)} %get-tuple-element.165), channel_id=1, source_target_pairs={{8,0},{16,8},{24,16},{9,1},{17,9},{25,17},{10,2},{18,10},{26,18},{... | collective-permute-start | bytes 786440 | tf_op jit(solution)/shard_map/ppermute | solution.py:561
  60.7 9.5 %collective-permute-start.9 = (bf16[16,8192]{1,0:T(8,128)(2,1)S(1)}, bf16[16,8192]{1,0:T(8,128)(2,1)S(1)}, u32[]{:S(2)}, u32[]{:S(2)}) collective-permute-start(bf16[16,8192]{1,0:T(8,128)(2,1)S(1)} %get-tuple-element.172), channel_id=1, source_target_pairs={{8,0},{16,8},{24,16},{9,1},{17,9},{25,17},{10,2},{18,10},{26,18},{... | collective-permute-start | bytes 786440 | tf_op jit(solution)/shard_map/ppermute | solution.py:561
  66.3 11.1 %collective-permute-start.8 = (bf16[16,8192]{1,0:T(8,128)(2,1)S(1)}, bf16[16,8192]{1,0:T(8,128)(2,1)S(1)}, u32[]{:S(2)}, u32[]{:S(2)}) collective-permute-start(bf16[16,8192]{1,0:T(8,128)(2,1)S(1)} %get-tuple-element.171), channel_id=1, source_target_pairs={{8,0},{16,8},{24,16},{9,1},{17,9},{25,17},{10,2},{18,10},{26,18},{... | collective-permute-start | bytes 786440 | tf_op jit(solution)/shard_map/ppermute | solution.py:561
  70.2 21.2 %collective-permute-start.11 = (bf16[16,8192]{1,0:T(8,128)(2,1)S(1)}, bf16[16,8192]{1,0:T(8,128)(2,1)S(1)}, u32[]{:S(2)}, u32[]{:S(2)}) collective-permute-start(bf16[16,8192]{1,0:T(8,128)(2,1)S(1)} %get-tuple-element.178), channel_id=1, source_target_pairs={{8,0},{16,8},{24,16},{9,1},{17,9},{25,17},{10,2},{18,10},{26,18},{... | collective-permute-start | bytes 786440 | tf_op jit(solution)/shard_map/ppermute | solution.py:561
  77.5 14.7 %collective-permute-start.10 = (bf16[16,8192]{1,0:T(8,128)(2,1)S(1)}, bf16[16,8192]{1,0:T(8,128)(2,1)S(1)}, u32[]{:S(2)}, u32[]{:S(2)}) collective-permute-start(bf16[16,8192]{1,0:T(8,128)(2,1)S(1)} %get-tuple-element.177), channel_id=1, source_target_pairs={{8,0},{16,8},{24,16},{9,1},{17,9},{25,17},{10,2},{18,10},{26,18},{... | collective-permute-start | bytes 786440 | tf_op jit(solution)/shard_map/ppermute | solution.py:561
  92.2 0.8 copy-start.5
  94.8 3.6 %collective-permute-start.12 = (bf16[4160,128]{1,0:T(8,128)(2,1)S(1)}, bf16[4160,128]{1,0:T(8,128)(2,1)S(1)}, u32[]{:S(2)}, u32[]{:S(2)}) collective-permute-start(bf16[4160,128]{1,0:T(8,128)(2,1)S(1)} %get-tuple-element.186), channel_id=1, source_target_pairs={{0,1},{1,0},{2,3},{3,2},{4,5},{5,4},{6,7},{7,6},{8,9},{9,8},{10,11... | collective-permute-start | bytes 3194888 | tf_op jit(solution)/shard_map/ppermute | solution.py:536
  97.9 7.9 %collective-permute-start.13 = (bf16[4096,128]{1,0:T(8,128)(2,1)S(1)}, bf16[4096,128]{1,0:T(8,128)(2,1)S(1)}, u32[]{:S(2)}, u32[]{:S(2)}) collective-permute-start(bf16[4096,128]{1,0:T(8,128)(2,1)S(1)} %get-tuple-element.191), channel_id=1, source_target_pairs={{0,1},{1,0},{2,3},{3,2},{4,5},{5,4},{6,7},{7,6},{8,9},{9,8},{10,11... | collective-permute-start | bytes 3145736 | tf_op jit(solution)/shard_map/ppermute | solution.py:536
  98.8 15.1 %collective-permute-start.14 = (bf16[2112,128]{1,0:T(8,128)(2,1)S(1)}, bf16[2112,128]{1,0:T(8,128)(2,1)S(1)}, u32[]{:S(2)}, u32[]{:S(2)}) collective-permute-start(bf16[2112,128]{1,0:T(8,128)(2,1)S(1)} %get-tuple-element.192), channel_id=1, source_target_pairs={{0,2},{1,3},{2,0},{3,1},{4,6},{5,7},{6,4},{7,5},{8,10},{9,11},{10,... | collective-permute-start | bytes 1622024 | tf_op jit(solution)/shard_map/ppermute | solution.py:536
  100.3 13.6 %collective-permute-start.15 = (bf16[2048,128]{1,0:T(8,128)(2,1)S(1)}, bf16[2048,128]{1,0:T(8,128)(2,1)S(1)}, u32[]{:S(2)}, u32[]{:S(2)}) collective-permute-start(bf16[2048,128]{1,0:T(8,128)(2,1)S(1)} %get-tuple-element.193), channel_id=1, source_target_pairs={{0,4},{1,5},{2,6},{3,7},{4,0},{5,1},{6,2},{7,3},{8,12},{9,13},{10,... | collective-permute-start | bytes 1572872 | tf_op jit(solution)/shard_map/ppermute | solution.py:536
  114.3 8.4 %collective-permute-start.16 = (bf16[1088,128]{1,0:T(8,128)(2,1)S(1)}, bf16[1088,128]{1,0:T(8,128)(2,1)S(1)}, u32[]{:S(2)}, u32[]{:S(2)}) collective-permute-start(bf16[1088,128]{1,0:T(8,128)(2,1)S(1)} %get-tuple-element.195), channel_id=1, source_target_pairs={{0,4},{1,5},{2,6},{3,7},{4,0},{5,1},{6,2},{7,3},{8,12},{9,13},{10,... | collective-permute-start | bytes 835592 | tf_op jit(solution)/shard_map/ppermute | solution.py:536
  115.9 6.8 %collective-permute-start.17 = (bf16[1024,128]{1,0:T(8,128)(2,1)S(1)}, bf16[1024,128]{1,0:T(8,128)(2,1)S(1)}, u32[]{:S(2)}, u32[]{:S(2)}) collective-permute-start(bf16[1024,128]{1,0:T(8,128)(2,1)S(1)} %get-tuple-element.197), channel_id=1, source_target_pairs={{0,2},{1,3},{2,0},{3,1},{4,6},{5,7},{6,4},{7,5},{8,10},{9,11},{10,... | collective-permute-start | bytes 786440 | tf_op jit(solution)/shard_map/ppermute | solution.py:536
  (1 other events, 0.8 us)
